TPU v7x, 32 devices: a whole 2x2x4 slice. The times are simulated.
32 devices in a mesh: group: 2 (over y), tile: 4 (over z), col: 2 (over x), layer: 2 (over core).
Axes of the slice: x: 2, y: 2, z: 4, core: 2. Of those that a mesh axis runs over, the one named last changes fastest.
Arguments:
- source: float32 [4, 40, 96, 512], P('group', 'layer', 'tile', 'col'), parts along dimension 0, may hold values from -12 to 12
- profile: float32 [40], P('layer'), may hold values from 0.5 to 1
- column: float32 [192, 512], P(('group', 'tile'), 'col'), parts along dimension 0, may hold values from 0.6 to 1.2
- terrain_height_error: int32 [4, 96, 512], P('group', 'tile', 'col'), parts along dimension 0, may hold values from -150 to 149
Outputs:
- solution: float32 [4, 40, 96, 512], P('group', 'layer', 'tile', 'col'), parts along dimension 0
There are 2 independent parts, one for each index of `group`. A program takes and returns all parts, laid end to end along the dimension named above; an argument that names none is the same for every part. Nothing has to cross between parts.
All inputs are finite; a program needn't handle non-finite values.
Results may differ from a plain program's by a relative error of at most 0.0001.
Values sent between devices are 32-bit elements; how exact they have to be, the bound alone decides.
No kernel may reach another device: no remote copies, remote signals or barrier semaphores. Data moves between devices by JAX's collectives and lax.ppermute only.
A program may use at most 64 MiB of HBM per device.

v0:
```python
import jax
import jax.numpy as jnp
from jax import lax
from jax.sharding import PartitionSpec as P

ITERS = 2


weight_horiz = 1.0
weight_vert = 2.0
weight_cross = 0.3
gain_bound = 1.6
total_weight = 10.4
diag_shift = 0.5
source_scale = 8.0


def padded_2(shard, sides, width):
    for axis, dim in sides:
        count, length = (lax.axis_size(axis), shard.shape[dim])
        up = [(i, (i + 1) % count) for i in range(count - 1)]
        down = [(j, i) for i, j in up]
        last = lax.slice_in_dim(shard, length - width, length, axis=dim)
        initial = lax.slice_in_dim(shard, 0, width, axis=dim)
        before = lax.ppermute(last, axis, up)
        after = lax.ppermute(initial, axis, down)
        shard = jnp.concatenate([before, shard, after], axis=dim)
    return shard


def stencil_sum(padded):
    horiz = (
        padded[:, 1:-1, 2:, 1:-1]
        + padded[:, 1:-1, :-2, 1:-1]
        + padded[:, 1:-1, 1:-1, 2:]
        + padded[:, 1:-1, 1:-1, :-2]
    )
    vert = padded[:, 2:, 1:-1, 1:-1] + padded[:, :-2, 1:-1, 1:-1]
    cross = (
        padded[:, 2:, 2:, 1:-1]
        + padded[:, 2:, :-2, 1:-1]
        + padded[:, :-2, 2:, 1:-1]
        + padded[:, :-2, :-2, 1:-1]
    )
    cross = (
        cross
        + padded[:, 2:, 1:-1, 2:]
        + padded[:, 2:, 1:-1, :-2]
        + padded[:, :-2, 1:-1, 2:]
        + padded[:, :-2, 1:-1, :-2]
    )
    return weight_horiz * horiz + weight_vert * vert + weight_cross * cross


def apply_operator(field, metric, diag_full):
    weighted = metric * field
    vertical = padded_2(weighted, (("layer", 1),), 1)
    padded = padded_2(vertical, (("tile", 2), ("col", 3)), 1)
    return diag_full * field - metric * stencil_sum(padded)


def error_spread(values):
    return values[:, None, None, None]


def local(source, profile, column, terrain_height_error):
    multiplier_factor = 1.0 + 0.002 * terrain_height_error.astype(jnp.float32)
    metric = (
        profile[None, :, None, None] * column[None, None, :, :] * multiplier_factor[:, None, :, :]
    )
    diag_full = gain_bound * total_weight * metric + diag_shift
    forcing_term = source_scale * metric * source
    residual = forcing_term
    scaled = forcing_term / diag_full
    applied = apply_operator(scaled, metric, diag_full)
    solution = jnp.zeros_like(forcing_term)
    direction = jnp.zeros_like(forcing_term)
    search_img = jnp.zeros_like(forcing_term)
    preconditioned_direction = jnp.zeros_like(forcing_term)
    img_dir = jnp.zeros_like(forcing_term)
    gamma_old = None
    alpha_old = None
    for step in range(ITERS):
        gamma_now, delta_now = lax.psum(
            (jnp.sum(residual * scaled, axis=(1, 2, 3)), jnp.sum(applied * scaled, axis=(1, 2, 3))),
            ("tile", "col", "layer"),
        )
        if step == 0:
            beta_now = jnp.zeros_like(gamma_now)
            alpha_now = gamma_now / delta_now
        else:
            beta_now = gamma_now / gamma_old
            alpha_now = gamma_now / (delta_now - beta_now * gamma_now / alpha_old)
        direction = scaled + error_spread(beta_now) * direction
        solution = solution + error_spread(alpha_now) * direction
        if step + 1 < ITERS:
            pre_app = applied / diag_full
            preconditioned_image = apply_operator(pre_app, metric, diag_full)
            img_dir = preconditioned_image + error_spread(beta_now) * img_dir
            preconditioned_direction = pre_app + error_spread(beta_now) * preconditioned_direction
            search_img = applied + error_spread(beta_now) * search_img
            residual = residual - error_spread(alpha_now) * search_img
            scaled = scaled - error_spread(alpha_now) * preconditioned_direction
            applied = applied - error_spread(alpha_now) * img_dir
        gamma_old = gamma_now
        alpha_old = alpha_now
    return solution


def solution(mesh):
    placed = (
        P("group", "layer", "tile", "col"),
        P("layer"),
        P(("group", "tile"), "col"),
        P("group", "tile", "col"),
    )
    return jax.shard_map(
        local,
        mesh=mesh,
        in_specs=placed,
        out_specs=P("group", "layer", "tile", "col"),
        check_vma=False,
    )
```

profile of v0, /device:TPU:0, one launch (start us, length us, event | category | flops | bytes accessed | tf_op | source)
XLA Modules:
  0.0 139.2 jit_solution(2850471159662051467)
XLA Ops:
  0.0 0.8 multiply_add_fusion.1
  0.8 0.8 broadcast_multiply_fusion
  1.6 1.5 %multiply_multiply_fusion.3 = f32[2,20,24,256]{3,2,1,0:T(8,128)S(1)} fusion(f32[2,24,256]{2,1,0:T(8,128)S(1)} %multiply_add_fusion.1, f32[20,24,256]{2,1,0:T(8,128)S(1)} %broadcast_multiply_fusion, f32[2,20,24,256]{3,2,1,0:T(8,128)} %param.4), kind=kLoop, calls=%fused_computation.3 | loop fusion | flops 1720320 | bytes 2506752 | tf_op jit(solution)/shard_map/mul | solution.py:56
  3.1 2.4 %collective-permute-start = (f32[2,1,24,256]{3,2,1,0:T(8,128)S(1)}, f32[2,1,24,256]{3,2,1,0:T(8,128)S(1)}, u32[]{:S(2)}, u32[]{:S(2)}) collective-permute-start(f32[2,1,24,256]{3,2,1,0:T(8,128)S(1)} %get-tuple-element.33), channel_id=1, source_target_pairs={{0,1},{2,3},{4,5},{6,7},{8,9},{10,11},{12,13},{14,15},{16,17},{18,... | collective-permute-start | bytes 147464 | tf_op jit(solution)/shard_map/ppermute | solution.py:25
  5.5 1.3 collective-permute-start.1
  6.8 0.0 collective-permute-done
  6.9 1.8 %collective-permute-done.1 = f32[2,1,24,256]{3,2,1,0:T(8,128)S(1)} collective-permute-done((f32[2,1,24,256]{3,2,1,0:T(8,128)S(1)}, f32[2,1,24,256]{3,2,1,0:T(8,128)S(1)}, u32[]{:S(2)}, u32[]{:S(2)}) %collective-permute-start.1) | collective-permute-done | bytes 49184 | tf_op jit(solution)/shard_map/ppermute | solution.py:26
  8.7 0.1 pad_maximum_fusion.13
  8.8 1.3 collective-permute-start.2
  10.1 4.9 %collective-permute-start.3 = (f32[2,22,1,256]{3,1,2,0:T(8,128)S(1)}, f32[2,22,1,256]{3,1,2,0:T(8,128)S(1)}, u32[]{:S(2)}, u32[]{:S(2)}) collective-permute-start(f32[2,22,1,256]{3,1,2,0:T(8,128)S(1)} %copy.72), channel_id=1, source_target_pairs={{0,4},{4,8},{8,12},{1,5},{5,9},{9,13},{2,6},{6,10},{10,14},{3,7},{... | collective-permute-start | bytes 135176 | tf_op jit(solution)/shard_map/ppermute | solution.py:25
  15.0 0.1 collective-permute-done.2
  15.2 1.6 %collective-permute-done.3 = f32[2,22,1,256]{3,1,2,0:T(8,128)S(1)} collective-permute-done((f32[2,22,1,256]{3,1,2,0:T(8,128)S(1)}, f32[2,22,1,256]{3,1,2,0:T(8,128)S(1)}, u32[]{:S(2)}, u32[]{:S(2)}) %collective-permute-start.3) | collective-permute-done | bytes 45088 | tf_op jit(solution)/shard_map/ppermute | solution.py:25
  16.8 0.2 pad_maximum_fusion.3
  17.0 0.3 fusion.24
  17.3 0.4 copy.57
  17.7 0.4 copy.59
  18.1 3.8 %collective-permute-start.5 = (f32[2,22,26,1]{2,1,3,0:T(8,128)S(1)}, f32[2,22,26,1]{2,1,3,0:T(8,128)S(1)}, u32[]{:S(2)}, u32[]{:S(2)}) collective-permute-start(f32[2,22,26,1]{2,1,3,0:T(8,128)S(1)} %copy.59), channel_id=1, source_target_pairs={{0,2},{1,3},{4,6},{5,7},{8,10},{9,11},{12,14},{13,15},{16,18},{17,... | collective-permute-start | bytes 13736 | tf_op jit(solution)/shard_map/ppermute | solution.py:25
  21.9 1.3 collective-permute-start.4
  23.2 1.9 %pad_maximum_fusion.2 = (f32[2,22,25,256]{3,2,1,0:T(8,128)}, f32[2,22,25,256]{3,2,1,0:T(8,128)}) fusion(f32[2,22,1,256]{3,2,1,0:T(1,128)S(1)} %copy.52, f32[2,1,24,256]{3,2,1,0:T(8,128)S(1)} %collective-permute-done.1, f32[2,20,24,256]{3,2,1,0:T(8,128)S(1)} %multiply_multiply_fusion.3, f32[2,1,24,256]{3,2,1,0:T(8,128)S(1)} %collective-permute-done, ...), kind=kLoop, calls=%fused_computation.10 | loop fusion | flops 1689600 | bytes 3424256 | tf_op jit(solution)/shard_map/concatenate | solution.py:27
  25.1 2.5 %collective-permute-done.4 = f32[2,22,26,1]{2,1,3,0:T(8,128)S(1)} collective-permute-done((f32[2,22,26,1]{2,1,3,0:T(8,128)S(1)}, f32[2,22,26,1]{2,1,3,0:T(8,128)S(1)}, u32[]{:S(2)}, u32[]{:S(2)}) %collective-permute-start.4) | collective-permute-done | bytes 4608 | tf_op jit(solution)/shard_map/ppermute | solution.py:26
  27.6 0.4 copy.58
  28.0 0.0 collective-permute-done.5
  28.0 1.3 copy.60
  29.3 0.0 copy-done.7
  29.3 2.8 %pad_maximum_fusion = (f32[2,22,26,257]{3,2,1,0:T(8,128)S(1)}, f32[2,22,26,257]{3,2,1,0:T(8,128)S(1)}) fusion(f32[2,22,26,1]{3,2,1,0:T(8,128)S(1)} %copy.58, f32[2,22,1,256]{3,2,1,0:T(1,128)S(1)} %copy.52, f32[2,1,24,256]{3,2,1,0:T(8,128)S(1)} %collective-permute-done.1, f32[2,20,24,256]{3,2,1,0:T(8,128)S(1)} %multiply_multiply_fusion.3, ...), kind=kLoop, calls=%fused_computation.6 | loop fusion | flops 2940080 | bytes 3532672 | tf_op jit(solution)/shard_map/concatenate | solution.py:27
  32.1 0.0 copy-done
  32.1 0.0 copy-done.3
  32.2 0.0 copy-done.4
  32.2 3.1 %multiply_multiply_fusion.1 = (f32[2,20,24,256]{3,2,1,0:T(8,128)S(1)}, f32[2,20,24,256]{3,2,1,0:T(8,128)S(1)}) fusion(f32[2,24,256]{2,1,0:T(8,128)S(1)} %multiply_add_fusion.1, f32[20,24,256]{2,1,0:T(8,128)S(1)} %broadcast_multiply_fusion, f32[2,22,26,257]{3,2,1,0:T(8,128)S(1)} %get-tuple-element.22, f32[2,22,26,257]{3,2,1,0:T(8,128)S(1)} %get-tuple-element.21, ...), kind=kLoop, calls=%fused_computation.1 | loop fusion | flops 6881280 | bytes 16367616 | tf_op jit(solution)/shard_map/mul | solution.py:56
  35.3 0.0 copy-start.1
  35.3 0.7 fusion.25
  36.0 1.3 collective-permute-start.6
  37.3 1.3 collective-permute-start.7
  38.6 0.0 copy-done.1
  38.6 0.6 multiply_reduce_fusion.1
  39.2 34.9 %all-reduce.1 = (f32[2]{0:T(128)S(1)}, f32[2]{0:T(128)S(1)}) all-reduce(f32[2]{0:T(128)S(1)} %get-tuple-element.6, f32[2]{0:T(128)S(1)} %get-tuple-element.5), channel_id=1, replica_groups=mesh['group'=2,'tile'=4,'col'=2,'layer'=2] {'tile','col','layer'}, use_global_device_ids=true, to_apply=%region_1.0 | all-reduce | flops 4 | bytes 32 | tf_op jit(solution)/shard_map/psum | solution.py:84
  74.1 0.0 collective-permute-done.6
  74.1 0.0 collective-permute-done.7
  74.1 0.8 pad_maximum_fusion.10
  75.0 1.3 collective-permute-start.8
  76.3 0.0 copy-done.10
  76.3 4.5 %collective-permute-start.9 = (f32[2,22,1,256]{3,1,2,0:T(8,128)S(1)}, f32[2,22,1,256]{3,1,2,0:T(8,128)S(1)}, u32[]{:S(2)}, u32[]{:S(2)}) collective-permute-start(f32[2,22,1,256]{3,1,2,0:T(8,128)S(1)} %copy.74), channel_id=1, source_target_pairs={{0,4},{4,8},{8,12},{1,5},{5,9},{9,13},{2,6},{6,10},{10,14},{3,7},{... | collective-permute-start | bytes 135176 | tf_op jit(solution)/shard_map/ppermute | solution.py:25
  80.8 0.0 copy-done.2
  80.8 0.6 multiply_reduce_fusion
  81.4 0.0 collective-permute-done.8
  81.4 0.0 copy-start.8
  81.5 1.1 collective-permute-done.9
  82.6 0.0 copy-start.9
  82.6 1.0 pad_maximum_fusion.5
  83.7 1.4 fusion.23
  85.0 2.1 %copy.67 = f32[2,22,26,1]{2,1,3,0:T(8,128)} copy(f32[2,22,26,1]{3,2,1,0:T(8,128)} %get-tuple-element.15) | data formatting | bytes 9152 | tf_op jit(solution)/shard_map/slice | solution.py:24
  87.1 2.1 %copy.69 = f32[2,22,26,1]{2,1,3,0:T(8,128)} copy(f32[2,22,26,1]{3,2,1,0:T(8,128)} %get-tuple-element.16) | data formatting | bytes 9152 | tf_op jit(solution)/shard_map/slice | solution.py:23
  89.2 1.9 %collective-permute-start.11 = (f32[2,22,26,1]{2,1,3,0:T(8,128)}, f32[2,22,26,1]{2,1,3,0:T(8,128)}, u32[]{:S(2)}, u32[]{:S(2)}) collective-permute-start(f32[2,22,26,1]{2,1,3,0:T(8,128)} %copy.69), channel_id=1, source_target_pairs={{0,2},{1,3},{4,6},{5,7},{8,10},{9,11},{12,14},{13,15},{16,18},{17,... | collective-permute-start | bytes 13736 | tf_op jit(solution)/shard_map/ppermute | solution.py:25
  91.1 1.3 collective-permute-start.10
  92.4 2.8 %pad_maximum_fusion.4 = (f32[2,22,25,256]{3,2,1,0:T(8,128)}, f32[2,22,25,256]{3,2,1,0:T(8,128)}) fusion(f32[2,22,1,256]{3,2,1,0:T(1,128)} %copy-done.8, f32[2,1,24,256]{3,2,1,0:T(8,128)} %collective-permute-done.7, f32[2,20,24,256]{3,2,1,0:T(8,128)S(1)} %get-tuple-element.13, f32[2,1,24,256]{3,2,1,0:T(8,128)S(1)} %collective-permute-done.6, ...), kind=kLoop, calls=%fused_computation.13 | loop fusion | flops 1689600 | bytes 3424256 | tf_op jit(solution)/shard_map/concatenate | solution.py:27
  95.2 1.9 %collective-permute-done.10 = f32[2,22,26,1]{2,1,3,0:T(8,128)} collective-permute-done((f32[2,22,26,1]{2,1,3,0:T(8,128)}, f32[2,22,26,1]{2,1,3,0:T(8,128)}, u32[]{:S(2)}, u32[]{:S(2)}) %collective-permute-start.10) | collective-permute-done | bytes 4608 | tf_op jit(solution)/shard_map/ppermute | solution.py:26
  97.1 2.0 %copy.68 = f32[2,22,26,1]{3,2,1,0:T(8,128)} copy(f32[2,22,26,1]{2,1,3,0:T(8,128)} %collective-permute-done.10) | data formatting | bytes 9152 | tf_op jit(solution)/shard_map/ppermute | solution.py:26
  99.1 0.0 collective-permute-done.11
  99.1 2.0 %copy.70 = f32[2,22,26,1]{3,2,1,0:T(8,128)} copy(f32[2,22,26,1]{2,1,3,0:T(8,128)} %collective-permute-done.11) | data formatting | bytes 9152 | tf_op jit(solution)/shard_map/ppermute | solution.py:25
  101.1 3.1 %pad_maximum_fusion.1 = (f32[2,22,26,257]{3,2,1,0:T(8,128)S(1)}, f32[2,22,26,257]{3,2,1,0:T(8,128)S(1)}) fusion(f32[2,22,26,1]{3,2,1,0:T(8,128)} %copy.68, f32[2,22,1,256]{3,2,1,0:T(1,128)} %copy-done.8, f32[2,1,24,256]{3,2,1,0:T(8,128)} %collective-permute-done.7, f32[2,20,24,256]{3,2,1,0:T(8,128)S(1)} %get-tuple-element.13, ...), kind=kLoop, calls=%fused_computation.8 | loop fusion | flops 2940080 | bytes 3532672 | tf_op jit(solution)/shard_map/concatenate | solution.py:27
  104.2 3.5 %fusion.11 = f32[2]{0:T(128)S(1)} fusion(f32[2,20,24,256]{3,2,1,0:T(8,128)S(1)} %copy-done.2, f32[2,22,26,257]{3,2,1,0:T(8,128)S(1)} %get-tuple-element.20, f32[2,22,26,257]{3,2,1,0:T(8,128)S(1)} %get-tuple-element.19, f32[2,22,25,256]{3,2,1,0:T(8,128)S(1)} %copy-done.6, f32[2,22,25,256]{3,2,1,0:T(8,128)S(1)} %copy-done.5, ...), kind=kLoop, calls=%fused_computation.27 | loop fusion | flops 8110078 | bytes 15384592 | tf_op jit(solution)/shard_map/reduce_sum | solution.py:85
  107.7 29.5 %all-reduce = (f32[2]{0:T(128)S(1)}, f32[2]{0:T(128)S(1)}) all-reduce(f32[2]{0:T(128)S(1)} %multiply_reduce_fusion, f32[2]{0:T(128)S(1)} %fusion.11), channel_id=1, replica_groups=mesh['group'=2,'tile'=4,'col'=2,'layer'=2] {'tile','col','layer'}, use_global_device_ids=true, to_apply=%region_5.0 | all-reduce | flops 4 | bytes 32 | tf_op jit(solution)/shard_map/psum | solution.py:84
  137.1 0.7 subtract_divide_fusion
  137.8 1.4 %multiply_add_fusion = f32[2,20,24,256]{3,2,1,0:T(8,128)} fusion(f32[2]{0:T(128)S(1)} %get-tuple-element.12, f32[2]{0:T(128)S(1)} %get-tuple-element.11, f32[2]{0:T(128)S(1)} %div.19, f32[2,20,24,256]{3,2,1,0:T(8,128)S(1)} %copy-done.2, f32[2,24,256]{2,1,0:T(8,128)S(1)} %multiply_add_fusion.1, f32[20,24,256]{2,1,0:T(8,128)S(1)} %broadcast_multiply_fusion, ...), kind=kLoop, calls=%fused_computation.62 | loop fusion | flops 3440640 | bytes 3489816 | tf_op jit(solution)/shard_map/add | solution.py:95
  (22 shorter events, 0.2 us)
Async XLA Ops:
  3.1 3.7 %collective-permute-start = (f32[2,1,24,256]{3,2,1,0:T(8,128)S(1)}, f32[2,1,24,256]{3,2,1,0:T(8,128)S(1)}, u32[]{:S(2)}, u32[]{:S(2)}) collective-permute-start(f32[2,1,24,256]{3,2,1,0:T(8,128)S(1)} %get-tuple-element.33), channel_id=1, source_target_pairs={{0,1},{2,3},{4,5},{6,7},{8,9},{10,11},{12,13},{14,15},{16,17},{18,... | collective-permute-start | bytes 147464 | tf_op jit(solution)/shard_map/ppermute | solution.py:25
  5.5 3.1 %collective-permute-start.1 = (f32[2,1,24,256]{3,2,1,0:T(8,128)S(1)}, f32[2,1,24,256]{3,2,1,0:T(8,128)S(1)}, u32[]{:S(2)}, u32[]{:S(2)}) collective-permute-start(f32[2,1,24,256]{3,2,1,0:T(8,128)S(1)} %get-tuple-element.34), channel_id=1, source_target_pairs={{1,0},{3,2},{5,4},{7,6},{9,8},{11,10},{13,12},{15,14},{17,16},{19,... | collective-permute-start | bytes 147464 | tf_op jit(solution)/shard_map/ppermute | solution.py:26
  8.7 20.6 %copy-start.7 = (f32[2,1,24,256]{3,2,1,0:T(8,128)}, f32[2,1,24,256]{3,2,1,0:T(8,128)S(1)}, u32[]{:S(2)}) copy-start(f32[2,1,24,256]{3,2,1,0:T(8,128)S(1)} %collective-permute-done.1) | copy-start | bytes 147460
  8.8 6.4 %collective-permute-start.2 = (f32[2,22,1,256]{3,1,2,0:T(8,128)S(1)}, f32[2,22,1,256]{3,1,2,0:T(8,128)S(1)}, u32[]{:S(2)}, u32[]{:S(2)}) collective-permute-start(f32[2,22,1,256]{3,1,2,0:T(8,128)S(1)} %copy.71), channel_id=1, source_target_pairs={{4,0},{8,4},{12,8},{5,1},{9,5},{13,9},{6,2},{10,6},{14,10},{7,3},{... | collective-permute-start | bytes 135176 | tf_op jit(solution)/shard_map/ppermute | solution.py:26
  10.1 6.7 %collective-permute-start.3 = (f32[2,22,1,256]{3,1,2,0:T(8,128)S(1)}, f32[2,22,1,256]{3,1,2,0:T(8,128)S(1)}, u32[]{:S(2)}, u32[]{:S(2)}) collective-permute-start(f32[2,22,1,256]{3,1,2,0:T(8,128)S(1)} %copy.72), channel_id=1, source_target_pairs={{0,4},{4,8},{8,12},{1,5},{5,9},{9,13},{2,6},{6,10},{10,14},{3,7},{... | collective-permute-start | bytes 135176 | tf_op jit(solution)/shard_map/ppermute | solution.py:25
  18.1 10.0 %collective-permute-start.5 = (f32[2,22,26,1]{2,1,3,0:T(8,128)S(1)}, f32[2,22,26,1]{2,1,3,0:T(8,128)S(1)}, u32[]{:S(2)}, u32[]{:S(2)}) collective-permute-start(f32[2,22,26,1]{2,1,3,0:T(8,128)S(1)} %copy.59), channel_id=1, source_target_pairs={{0,2},{1,3},{4,6},{5,7},{8,10},{9,11},{12,14},{13,15},{16,18},{17,... | collective-permute-start | bytes 13736 | tf_op jit(solution)/shard_map/ppermute | solution.py:25
  21.9 5.7 %collective-permute-start.4 = (f32[2,22,26,1]{2,1,3,0:T(8,128)S(1)}, f32[2,22,26,1]{2,1,3,0:T(8,128)S(1)}, u32[]{:S(2)}, u32[]{:S(2)}) collective-permute-start(f32[2,22,26,1]{2,1,3,0:T(8,128)S(1)} %copy.57), channel_id=1, source_target_pairs={{2,0},{3,1},{6,4},{7,5},{10,8},{11,9},{14,12},{15,13},{18,16},{19,... | collective-permute-start | bytes 13736 | tf_op jit(solution)/shard_map/ppermute | solution.py:26
  29.3 2.8 %copy-start = (f32[2,20,24,256]{3,2,1,0:T(8,128)S(1)}, f32[2,20,24,256]{3,2,1,0:T(8,128)}, u32[]{:S(2)}) copy-start(f32[2,20,24,256]{3,2,1,0:T(8,128)} %param.4) | copy-start | bytes 2949124
  29.3 2.9 %copy-start.3 = (f32[2,22,25,256]{3,2,1,0:T(8,128)S(1)}, f32[2,22,25,256]{3,2,1,0:T(8,128)}, u32[]{:S(2)}) copy-start(f32[2,22,25,256]{3,2,1,0:T(8,128)} %get-tuple-element.27) | copy-start | bytes 3379204
  29.3 2.9 %copy-start.4 = (f32[2,22,25,256]{3,2,1,0:T(8,128)S(1)}, f32[2,22,25,256]{3,2,1,0:T(8,128)}, u32[]{:S(2)}) copy-start(f32[2,22,25,256]{3,2,1,0:T(8,128)} %get-tuple-element.28) | copy-start | bytes 3379204
  35.3 3.3 %copy-start.1 = (f32[2,20,24,256]{3,2,1,0:T(8,128)}, f32[2,20,24,256]{3,2,1,0:T(8,128)S(1)}, u32[]{:S(2)}) copy-start(f32[2,20,24,256]{3,2,1,0:T(8,128)S(1)} %get-tuple-element.14) | copy-start | bytes 2949124
  36.0 38.1 %collective-permute-start.6 = (f32[2,1,24,256]{3,2,1,0:T(8,128)}, f32[2,1,24,256]{3,2,1,0:T(8,128)S(1)}, u32[]{:S(2)}, u32[]{:S(2)}) collective-permute-start(f32[2,1,24,256]{3,2,1,0:T(8,128)} %get-tuple-element.31), channel_id=1, source_target_pairs={{0,1},{2,3},{4,5},{6,7},{8,9},{10,11},{12,13},{14,15},{16,17},{18,... | collective-permute-start | bytes 147464 | tf_op jit(solution)/shard_map/ppermute | solution.py:25
  37.3 36.8 %collective-permute-start.7 = (f32[2,1,24,256]{3,2,1,0:T(8,128)}, f32[2,1,24,256]{3,2,1,0:T(8,128)}, u32[]{:S(2)}, u32[]{:S(2)}) collective-permute-start(f32[2,1,24,256]{3,2,1,0:T(8,128)} %get-tuple-element.32), channel_id=1, source_target_pairs={{1,0},{3,2},{5,4},{7,6},{9,8},{11,10},{13,12},{15,14},{17,16},{19,... | collective-permute-start | bytes 147464 | tf_op jit(solution)/shard_map/ppermute | solution.py:26
  39.2 41.6 %copy-start.2 = (f32[2,20,24,256]{3,2,1,0:T(8,128)S(1)}, f32[2,20,24,256]{3,2,1,0:T(8,128)}, u32[]{:S(2)}) copy-start(f32[2,20,24,256]{3,2,1,0:T(8,128)} %copy-done.1) | copy-start | bytes 2949124
  74.1 2.2 %copy-start.10 = (f32[2]{0:T(128)}, f32[2]{0:T(128)S(1)}, u32[]{:S(2)}) copy-start(f32[2]{0:T(128)S(1)} %get-tuple-element.10) | copy-start | bytes 28
  75.0 6.4 %collective-permute-start.8 = (f32[2,22,1,256]{3,1,2,0:T(8,128)S(1)}, f32[2,22,1,256]{3,1,2,0:T(8,128)S(1)}, u32[]{:S(2)}, u32[]{:S(2)}) collective-permute-start(f32[2,22,1,256]{3,1,2,0:T(8,128)S(1)} %copy.73), channel_id=1, source_target_pairs={{4,0},{8,4},{12,8},{5,1},{9,5},{13,9},{6,2},{10,6},{14,10},{7,3},{... | collective-permute-start | bytes 135176 | tf_op jit(solution)/shard_map/ppermute | solution.py:26
  76.3 6.3 %collective-permute-start.9 = (f32[2,22,1,256]{3,1,2,0:T(8,128)S(1)}, f32[2,22,1,256]{3,1,2,0:T(8,128)S(1)}, u32[]{:S(2)}, u32[]{:S(2)}) collective-permute-start(f32[2,22,1,256]{3,1,2,0:T(8,128)S(1)} %copy.74), channel_id=1, source_target_pairs={{0,4},{4,8},{8,12},{1,5},{5,9},{9,13},{2,6},{6,10},{10,14},{3,7},{... | collective-permute-start | bytes 135176 | tf_op jit(solution)/shard_map/ppermute | solution.py:25
  81.4 3.6 %copy-start.8 = (f32[2,22,1,256]{3,2,1,0:T(1,128)}, f32[2,22,1,256]{3,2,1,0:T(1,128)S(1)}, u32[]{:S(2)}) copy-start(f32[2,22,1,256]{3,2,1,0:T(1,128)S(1)} %copy.62) | copy-start | bytes 135172
  82.6 2.4 %copy-start.9 = (f32[2,22,1,256]{3,2,1,0:T(1,128)}, f32[2,22,1,256]{3,2,1,0:T(1,128)S(1)}, u32[]{:S(2)}) copy-start(f32[2,22,1,256]{3,2,1,0:T(1,128)S(1)} %copy.64) | copy-start | bytes 135172
  89.2 9.9 %collective-permute-start.11 = (f32[2,22,26,1]{2,1,3,0:T(8,128)}, f32[2,22,26,1]{2,1,3,0:T(8,128)}, u32[]{:S(2)}, u32[]{:S(2)}) collective-permute-start(f32[2,22,26,1]{2,1,3,0:T(8,128)} %copy.69), channel_id=1, source_target_pairs={{0,2},{1,3},{4,6},{5,7},{8,10},{9,11},{12,14},{13,15},{16,18},{17,... | collective-permute-start | bytes 13736 | tf_op jit(solution)/shard_map/ppermute | solution.py:25
  91.1 6.0 %collective-permute-start.10 = (f32[2,22,26,1]{2,1,3,0:T(8,128)}, f32[2,22,26,1]{2,1,3,0:T(8,128)}, u32[]{:S(2)}, u32[]{:S(2)}) collective-permute-start(f32[2,22,26,1]{2,1,3,0:T(8,128)} %copy.67), channel_id=1, source_target_pairs={{2,0},{3,1},{6,4},{7,5},{10,8},{11,9},{14,12},{15,13},{18,16},{19,... | collective-permute-start | bytes 13736 | tf_op jit(solution)/shard_map/ppermute | solution.py:26
  101.1 3.1 %copy-start.5 = (f32[2,22,25,256]{3,2,1,0:T(8,128)S(1)}, f32[2,22,25,256]{3,2,1,0:T(8,128)}, u32[]{:S(2)}) copy-start(f32[2,22,25,256]{3,2,1,0:T(8,128)} %get-tuple-element.23) | copy-start | bytes 3379204
  101.1 3.1 %copy-start.6 = (f32[2,22,25,256]{3,2,1,0:T(8,128)S(1)}, f32[2,22,25,256]{3,2,1,0:T(8,128)}, u32[]{:S(2)}) copy-start(f32[2,22,25,256]{3,2,1,0:T(8,128)} %get-tuple-element.24) | copy-start | bytes 3379204
where the time goes:
time: 140 us; the launch traced here: 139 us
  blocking collectives  64.3 us (46%)
  starting transfers between devices  26.6 us (19%)
  other arithmetic  25.8 us (18%)
  local copies, waits for them, and re-layouts  13.2 us (9%)
  waiting for transfers between devices  9.04 us (6%)
    psum x2, blocking collectives, local(): lax.psum((jnp.sum(residual * scaled, axis=(1, 2, 3)), jnp.sum(applied * s...  64.3 us
    ppermute x6, starting transfers between devices, padded_2(): before = lax.ppermute(last, axis, up)  18.9 us
    concatenate x8, other arithmetic, padded_2(): shard = jnp.concatenate([before, shard, after], axis=dim)  12.8 us
    ppermute x6, starting transfers between devices, padded_2(): after = lax.ppermute(initial, axis, down)  7.74 us
    ppermute x6, waiting for transfers between devices, padded_2(): after = lax.ppermute(initial, axis, down)  6.36 us
    mul x2, other arithmetic, apply_operator(): weighted = metric * field  4.6 us
    reduce_sum x2, other arithmetic, local(): jnp.sum(applied * scaled, axis=(1, 2, 3))  4.11 us
    slice x4, local copies, waits for them, and re-layouts, padded_2(): initial = lax.slice_in_dim(shard, 0, width, axis=dim)  4.09 us
  transfers between devices with their start and end apart: 12, of which 6 were waited for; matrix products, arithmetic and copies ran while one was open for 6% of the time, Pallas kernels for 0%

commit v1 on v0

v1 whole, which is shorter than its diff:
```python
import jax
import jax.numpy as jnp
from jax import lax
from jax.sharding import PartitionSpec as P

weight_vert = 2.0
weight_cross = 0.3
gain_bound = 1.6
total_weight = 10.4
diag_shift = 0.5
source_scale = 8.0


def line_pairs(count, first):
    pairs = []
    for low in range(first, count - 1, 2):
        pairs += [(low, low + 1), (low + 1, low)]
    return pairs


def neighbours(low_edge, high_edge, axis):
    count, index = lax.axis_size(axis), lax.axis_index(axis)
    if count == 1:
        return jnp.zeros_like(low_edge), jnp.zeros_like(high_edge)
    even = index % 2 == 0
    first = lax.ppermute(jnp.where(even, high_edge, low_edge), axis, line_pairs(count, 0))
    if count == 2:
        second = jnp.zeros_like(first)
    else:
        second = lax.ppermute(jnp.where(even, low_edge, high_edge), axis, line_pairs(count, 1))
    return jnp.where(even, second, first), jnp.where(even, first, second)


def padded(shard, axis, dim):
    length = shard.shape[dim]
    before, after = neighbours(
        lax.slice_in_dim(shard, 0, 1, axis=dim), lax.slice_in_dim(shard, length - 1, length, axis=dim), axis
    )
    return jnp.concatenate([before, shard, after], axis=dim)


def stencil(field):
    field = padded(padded(padded(field, "layer", 1), "tile", 2), "col", 3)
    sides = (
        field[:, :, 2:, 1:-1] + field[:, :, :-2, 1:-1] + field[:, :, 1:-1, 2:] + field[:, :, 1:-1, :-2]
    )
    levels = weight_vert * field[:, :, 1:-1, 1:-1] + weight_cross * sides
    return sides[:, 1:-1] + levels[:, 2:] + levels[:, :-2]


def total(values, axes):
    for axis in axes:
        count = lax.axis_size(axis)
        if count & (count - 1):
            values = lax.psum(values, axis)
            continue
        bit = 1
        while bit < count:
            values = values + lax.ppermute(values, axis, [(i, i ^ bit) for i in range(count)])
            bit *= 2
    return values


def local(source, profile, column, terrain_height_error):
    multiplier_factor = 1.0 + 0.002 * terrain_height_error.astype(jnp.float32)
    metric = profile[None, :, None, None] * column[None, None, :, :] * multiplier_factor[:, None, :, :]
    scale = metric / (gain_bound * total_weight * metric + diag_shift)
    gain = metric * scale
    forcing = source_scale * source
    weighted = gain * forcing
    image = stencil(weighted)
    again = gain * image
    image_again = stencil(again)
    lanes = (1, 2)
    sums = jnp.stack(
        [
            jnp.sum(weighted * forcing, axis=lanes),
            jnp.sum(weighted * image, axis=lanes),
            jnp.sum(again * image, axis=lanes),
            jnp.sum(again * image_again, axis=lanes),
        ]
    )
    sums = jnp.sum(total(sums, ("layer", "col", "tile")), axis=-1)
    zz, zb, bb, bbb = (sums[i][:, None, None, None] for i in range(4))
    delta = zz - zb
    alpha = zz / delta
    rest = -zb / delta
    beta = (zz * bb - zb * zb) / (delta * delta)
    gamma = zz * beta
    delta_next = gamma - (rest * rest * zb + 2.0 * alpha * rest * bb + alpha * alpha * bbb)
    alpha_next = gamma / (delta_next - beta * gamma / alpha)
    return scale * ((alpha + alpha_next * (rest + beta)) * forcing + (alpha_next * alpha) * image)


def solution(mesh):
    placed = (
        P("group", "layer", "tile", "col"),
        P("layer"),
        P(("group", "tile"), "col"),
        P("group", "tile", "col"),
    )
    return jax.shard_map(
        local,
        mesh=mesh,
        in_specs=placed,
        out_specs=P("group", "layer", "tile", "col"),
        check_vma=False,
    )
```

time: 140 us -> 239 us (1.71)
  other arithmetic: 25.8 us -> 146 us
  blocking collectives: 64.3 us -> 0 us
  local copies, waits for them, and re-layouts: 13.2 us -> 59.9 us
  starting transfers between devices: 26.6 us -> 15.9 us
  waiting for transfers between devices: 9.04 us -> 17 us
    psum x2 -> x0, blocking collectives: 64.3 us -> none  [local(): lax.psum((jnp.sum(residual * scaled, axis=(1, 2, 3)), jnp.sum(applied * s...]
    add x1 -> x5, other arithmetic: 1.43 us -> 62.9 us  [the longest x2 62.8 us: stencil(): levels = weight_vert * field[:, :, 1:-1, 1:-1] + weight_cross * sides]
    select_n x0 -> x12, other arithmetic: none -> 35.1 us  [the longest x6 20.3 us: neighbours(): return (jnp.where(even, second, first), jnp.where(even, first, second))]
    select_n x0 -> x10, local copies, waits for them, and re-layouts: none -> 21.4 us  [the longest x4 9.26 us: neighbours(): jnp.where(even, high_edge, low_edge)]
    mul x2 -> x6, other arithmetic: 4.6 us -> 23.4 us  [the longest x1 10.2 us: local(): again = gain * image]
    unnamed x26, local copies, waits for them, and re-layouts: 0.07 us -> 11.1 us
    ppermute x8 -> x4, local copies, waits for them, and re-layouts: 5.81 us -> 16.6 us  [the longest x2 8.37 us: neighbours(): lax.ppermute(jnp.where(even, high_edge, low_edge), axis, line_pairs(count...]
    ppermute x12, starting transfers between devices: 26.6 us -> 15.9 us  [the longest x6 11.3 us: neighbours(): lax.ppermute(jnp.where(even, high_edge, low_edge), axis, line_pairs(count...]
  transfers between devices with their start and end apart: 12 -> 12, of which waited for: 6 -> 8; matrix products, arithmetic and copies ran while one was open for 6% -> 7% of each run, Pallas kernels for 0% -> 0%
where the time goes in v1:
time: 239 us
  other arithmetic  146 us (61%)
  local copies, waits for them, and re-layouts  59.9 us (25%)
  waiting for transfers between devices  17 us (7%)
  starting transfers between devices  15.9 us (7%)
    add x2, other arithmetic, stencil(): levels = weight_vert * field[:, :, 1:-1, 1:-1] + weight_cross * sides  62.8 us
    select_n x6, other arithmetic, neighbours(): return (jnp.where(even, second, first), jnp.where(even, first, second))  20.3 us
    reduce_sum x1, other arithmetic, local(): jnp.sum(weighted * forcing, axis=lanes)  14.4 us
    select_n x2, other arithmetic, neighbours(): jnp.where(even, low_edge, high_edge)  12.4 us
    ppermute x6, starting transfers between devices, neighbours(): lax.ppermute(jnp.where(even, high_edge, low_edge), axis, line_pairs(count...  11.3 us
    unnamed x26, local copies, waits for them, and re-layouts  11.1 us
    mul x1, other arithmetic, local(): again = gain * image  10.2 us
    ppermute x4, waiting for transfers between devices, total(): lax.ppermute(values, axis, [(i, i ^ bit) for i in range(count)])  10.2 us
  transfers between devices with their start and end apart: 12, of which 8 were waited for; matrix products, arithmetic and copies ran while one was open for 7% of the time, Pallas kernels for 0%

profile of v1, /device:TPU:0, one launch (start us, length us, event | category | flops | bytes accessed | tf_op | source)
XLA Modules:
  0.0 238.5 jit_solution(9573643089328245182)
XLA Ops:
  0.0 0.8 multiply_add_fusion.2
  0.8 0.8 copy.135
  1.7 0.1 copy.136
  1.8 5.0 %copy.137 = f32[2,20,24,256]{2,1,3,0:T(8,128)} copy(f32[2,20,24,256]{3,2,1,0:T(8,128)} %param.4) | data formatting | bytes 1966080 | tf_op args[0]
  6.8 0.3 broadcast_multiply_fusion
  7.1 4.8 %multiply_multiply_fusion.2 = f32[2,20,24,256]{2,1,3,0:T(8,128)S(1)} fusion(f32[2,20,24,256]{2,1,3,0:T(8,128)} %copy.137, f32[2,24,256]{1,2,0:T(8,128)S(1)} %copy.136, f32[20,24,256]{1,0,2:T(8,128)S(1)} %broadcast_multiply_fusion), kind=kLoop, calls=%fused_computation.60 | loop fusion | flops 1720320 | bytes 2506752 | tf_op jit(solution)/shard_map/mul | solution.py:70
  12.0 2.6 %copy-done.1 = f32[2,20,24,256]{2,1,3,0:T(8,128)} copy-done((f32[2,20,24,256]{2,1,3,0:T(8,128)}, f32[2,20,24,256]{2,1,3,0:T(8,128)S(1)}, u32[]{:S(2)}) %copy-start.1) | copy-done | bytes 983064
  14.6 0.3 broadcast_select_fusion.5
  14.9 0.1 copy.138
  15.0 0.5 collective-permute-start
  15.5 0.9 collective-permute-done
  16.4 0.8 copy.143
  17.2 0.8 copy.144
  18.1 4.3 %pad_maximum_fusion.32 = f32[2,22,24,256]{2,1,3,0:T(8,128)S(1)} fusion(f32[2,1,24,256]{2,1,3,0:T(1,128)} %copy.144, f32[2,20,24,256]{2,1,3,0:T(8,128)} %copy-done.1, f32[2,1,24,256]{2,1,3,0:T(1,128)} %copy.143), kind=kLoop, calls=%fused_computation.48 | loop fusion | flops 540672 | bytes 2162688 | tf_op jit(solution)/shard_map/concatenate | solution.py:39
  22.4 6.2 %slice_select_fusion.2 = (f32[2,22,1,256]{2,1,3,0:T(8,128)}, f32[2,22,1,256]{2,1,3,0:T(8,128)}) fusion(f32[2,22,24,256]{2,1,3,0:T(8,128)S(1)} %pad_maximum_fusion.32, pred[]{:T(512)S(6)} %eq.20), kind=kLoop, calls=%fused_computation.58 | loop fusion | flops 22528 | bytes 180225 | tf_op jit(solution)/shard_map/jit(_where)/select_n | solution.py:30
  28.6 4.4 %copy.146 = f32[2,22,1,256]{3,1,2,0:T(8,128)S(1)} copy(f32[2,22,1,256]{2,1,3,0:T(8,128)} %get-tuple-element.29) | data formatting | bytes 90112 | tf_op jit(solution)/shard_map/jit(_where)/select_n | solution.py:30
  33.0 0.9 collective-permute-start.2
  33.9 4.4 %copy.145 = f32[2,22,1,256]{3,1,2,0:T(8,128)S(1)} copy(f32[2,22,1,256]{2,1,3,0:T(8,128)} %get-tuple-element.30) | data formatting | bytes 90112 | tf_op jit(solution)/shard_map/jit(_where)/select_n | solution.py:26
  38.3 5.8 %collective-permute-start.1 = (f32[2,22,1,256]{3,1,2,0:T(8,128)S(1)}, f32[2,22,1,256]{3,1,2,0:T(8,128)S(1)}, u32[]{:S(2)}, u32[]{:S(2)}) collective-permute-start(f32[2,22,1,256]{3,1,2,0:T(8,128)S(1)} %copy.145), channel_id=1, source_target_pairs={{0,4},{4,0},{8,12},{12,8},{1,5},{5,1},{9,13},{13,9},{2,6},{6,2},{1... | collective-permute-start | bytes 135176 | tf_op jit(solution)/shard_map/ppermute | solution.py:26
  44.1 4.1 %copy.148 = f32[2,22,1,256]{2,1,3,0:T(8,128)} copy(f32[2,22,1,256]{3,1,2,0:T(8,128)S(1)} %collective-permute-done.2) | data formatting | bytes 90112 | tf_op jit(solution)/shard_map/ppermute | solution.py:30
  48.2 0.0 collective-permute-done.1
  48.2 4.2 %copy.147 = f32[2,22,1,256]{2,1,3,0:T(8,128)} copy(f32[2,22,1,256]{3,1,2,0:T(8,128)S(1)} %collective-permute-done.1) | data formatting | bytes 90112 | tf_op jit(solution)/shard_map/ppermute | solution.py:26
  52.4 10.1 %broadcast_select_fusion.2 = (f32[2,22,1,256]{2,1,3,0:T(8,128)}, f32[2,22,1,256]{2,1,3,0:T(8,128)}) fusion(f32[2,22,1,256]{2,1,3,0:T(8,128)} %copy.148, f32[2,22,1,256]{2,1,3,0:T(8,128)} %copy.147, pred[]{:T(512)S(6)} %eq.20), kind=kLoop, calls=%fused_computation.64 | loop fusion | flops 22528 | bytes 180225 | tf_op jit(solution)/shard_map/jit(_where)/select_n | solution.py:31
  62.5 0.9 fusion.11
  63.5 1.6 collective-permute-start.3
  65.0 2.3 collective-permute-done.3
  67.4 31.4 %multiply_add_fusion.1 = (f32[2,22,24,256]{2,1,3,0:T(8,128)}, f32[2,22,24,256]{2,1,3,0:T(8,128)}) fusion(f32[2,22,1,256]{2,1,3,0:T(8,128)} %get-tuple-element.26, f32[2,1,24,256]{2,1,3,0:T(1,128)} %copy.144, f32[2,20,24,256]{2,1,3,0:T(8,128)S(1)} %bitcast.3, f32[2,1,24,256]{2,1,3,0:T(1,128)} %copy.143, f32[2,22,1,256]{2,1,3,0:T(8,128)} %get-tuple-element.25, ...), kind=kLoop, calls=%fused_computation.54 | loop fusion | flops 6488064 | bytes 3343296 | tf_op jit(solution)/shard_map/add | solution.py:47
  98.8 10.2 %fusion.9 = (f32[2,20,24,256]{2,1,3,0:T(8,128)S(1)}, f32[2,20,24,256]{2,1,3,0:T(8,128)}) fusion(f32[2,24,256]{1,2,0:T(8,128)S(1)} %copy.136, f32[20,24,256]{1,0,2:T(8,128)S(1)} %copy-done.3, f32[2,22,24,256]{2,1,3,0:T(8,128)} %get-tuple-element.21, f32[2,22,24,256]{2,1,3,0:T(8,128)} %get-tuple-element.22), kind=kLoop, calls=%fused_computation.61 | loop fusion | flops 1966080 | bytes 5455872 | tf_op jit(solution)/shard_map/mul | solution.py:72
  109.0 2.6 %copy-done = f32[2,20,24,256]{2,1,3,0:T(8,128)} copy-done((f32[2,20,24,256]{2,1,3,0:T(8,128)}, f32[2,20,24,256]{2,1,3,0:T(8,128)S(1)}, u32[]{:S(2)}) %copy-start) | copy-done | bytes 983064
  111.6 0.3 broadcast_select_fusion.4
  111.9 0.1 copy.151
  112.0 0.1 collective-permute-start.4
  112.1 1.2 collective-permute-done.4
  113.3 0.8 copy.156
  114.1 0.8 copy.157
  115.0 4.3 %pad_maximum_fusion.33 = f32[2,22,24,256]{2,1,3,0:T(8,128)S(1)} fusion(f32[2,1,24,256]{2,1,3,0:T(1,128)} %copy.157, f32[2,20,24,256]{2,1,3,0:T(8,128)} %copy-done, f32[2,1,24,256]{2,1,3,0:T(1,128)} %copy.156), kind=kLoop, calls=%fused_computation.49 | loop fusion | flops 540672 | bytes 2162688 | tf_op jit(solution)/shard_map/concatenate | solution.py:39
  119.3 6.3 %slice_select_fusion = (f32[2,22,1,256]{2,1,3,0:T(8,128)}, f32[2,22,1,256]{2,1,3,0:T(8,128)}) fusion(f32[2,22,24,256]{2,1,3,0:T(8,128)S(1)} %pad_maximum_fusion.33, pred[]{:T(512)S(6)} %eq.20), kind=kLoop, calls=%fused_computation.56 | loop fusion | flops 22528 | bytes 180225 | tf_op jit(solution)/shard_map/jit(_where)/select_n | solution.py:30
  125.5 4.4 %copy.159 = f32[2,22,1,256]{3,1,2,0:T(8,128)S(1)} copy(f32[2,22,1,256]{2,1,3,0:T(8,128)} %get-tuple-element.27) | data formatting | bytes 90112 | tf_op jit(solution)/shard_map/jit(_where)/select_n | solution.py:30
  130.0 0.7 collective-permute-start.6
  130.6 4.6 %copy.158 = f32[2,22,1,256]{3,1,2,0:T(8,128)S(1)} copy(f32[2,22,1,256]{2,1,3,0:T(8,128)} %get-tuple-element.28) | data formatting | bytes 90112 | tf_op jit(solution)/shard_map/jit(_where)/select_n | solution.py:26
  135.3 1.8 collective-permute-start.5
  137.1 4.1 %copy.161 = f32[2,22,1,256]{2,1,3,0:T(8,128)} copy(f32[2,22,1,256]{3,1,2,0:T(8,128)S(1)} %collective-permute-done.6) | data formatting | bytes 90112 | tf_op jit(solution)/shard_map/ppermute | solution.py:30
  141.2 4.2 %copy.160 = f32[2,22,1,256]{2,1,3,0:T(8,128)} copy(f32[2,22,1,256]{3,1,2,0:T(8,128)S(1)} %collective-permute-done.5) | data formatting | bytes 90112 | tf_op jit(solution)/shard_map/ppermute | solution.py:26
  145.4 10.1 %broadcast_select_fusion = (f32[2,22,1,256]{2,1,3,0:T(8,128)}, f32[2,22,1,256]{2,1,3,0:T(8,128)}) fusion(f32[2,22,1,256]{2,1,3,0:T(8,128)} %copy.161, f32[2,22,1,256]{2,1,3,0:T(8,128)} %copy.160, pred[]{:T(512)S(6)} %eq.20), kind=kLoop, calls=%fused_computation.62 | loop fusion | flops 22528 | bytes 180225 | tf_op jit(solution)/shard_map/jit(_where)/select_n | solution.py:31
  155.6 0.9 fusion.10
  156.5 1.6 collective-permute-start.7
  158.0 2.3 collective-permute-done.7
  160.4 31.4 %multiply_add_fusion = (f32[2,22,24,256]{2,1,3,0:T(8,128)}, f32[2,22,24,256]{2,1,3,0:T(8,128)}) fusion(f32[2,22,1,256]{2,1,3,0:T(8,128)} %get-tuple-element.24, f32[2,1,24,256]{2,1,3,0:T(1,128)} %copy.157, f32[2,20,24,256]{2,1,3,0:T(8,128)S(1)} %bitcast.1, f32[2,1,24,256]{2,1,3,0:T(1,128)} %copy.156, f32[2,22,1,256]{2,1,3,0:T(8,128)} %get-tuple-element.23, ...), kind=kLoop, calls=%fused_computation.51 | loop fusion | flops 6488064 | bytes 3343296 | tf_op jit(solution)/shard_map/add | solution.py:47
  191.8 0.0 copy-start.6
  191.8 14.4 %multiply_reduce_fusion.2 = (f32[2,256]{1,0:T(2,128)S(1)}, f32[2,256]{1,0:T(2,128)S(1)}, f32[2,256]{1,0:T(2,128)S(1)}, f32[2,256]{1,0:T(2,128)S(1)}) fusion(f32[2,20,24,256]{2,1,3,0:T(8,128)} %copy.137, f32[2,20,24,256]{2,1,3,0:T(8,128)} %get-tuple-element.20, f32[2,20,24,256]{2,1,3,0:T(8,128)S(1)} %bitcast.1, f32[2,22,24,256]{2,1,3,0:T(8,128)} %get-tuple-element.17, ...), kind=kLoop, calls=%fused_computation.55 | loop fusion | flops 4175872 | bytes 6447104 | tf_op jit(solution)/shard_map/reduce_sum | solution.py:77
  206.3 0.1 collective-permute-start.8
  206.4 1.2 collective-permute-done.8
  207.6 1.6 collective-permute-start.9
  209.1 2.2 collective-permute-done.9
  211.3 0.3 collective-permute-start.10
  211.6 3.4 %collective-permute-done.10 = f32[4,2,256]{2,0,1:T(4,128)S(1)} collective-permute-done((f32[4,2,256]{2,0,1:T(4,128)S(1)}, f32[4,2,256]{2,0,1:T(4,128)S(1)}, u32[]{:S(2)}, u32[]{:S(2)}) %collective-permute-start.10) | collective-permute-done | bytes 8224 | tf_op jit(solution)/shard_map/ppermute | solution.py:59
  215.0 1.1 collective-permute-start.11
  216.1 3.5 %collective-permute-done.11 = f32[4,2,256]{2,0,1:T(4,128)S(1)} collective-permute-done((f32[4,2,256]{2,0,1:T(4,128)S(1)}, f32[4,2,256]{2,0,1:T(4,128)S(1)}, u32[]{:S(2)}, u32[]{:S(2)}) %collective-permute-start.11) | collective-permute-done | bytes 8224 | tf_op jit(solution)/shard_map/ppermute | solution.py:59
  219.6 0.1 add_reduce_fusion
  219.6 0.2 slice_reduce_fusion
  219.9 1.1 broadcast_multiply_fusion.1
  221.0 5.0 %copy.165 = f32[2,20,24,256]{2,1,3,0:T(8,128)} copy(f32[2,20,24,256]{3,2,1,0:T(8,128)} %broadcast_multiply_fusion.1) | data formatting | bytes 1966080 | tf_op jit(solution)/shard_map/mul | solution.py:92
  226.0 7.2 %add_multiply_fusion = f32[2,20,24,256]{2,1,3,0:T(8,128)} fusion(f32[2,20,24,256]{2,1,3,0:T(8,128)} %copy.165, f32[2,20,24,256]{2,1,3,0:T(8,128)} %get-tuple-element.20, f32[2]{0:T(128)S(1)} %get-tuple-element.13, f32[2,24,256]{1,2,0:T(8,128)S(1)} %copy.136, f32[20,24,256]{1,0,2:T(8,128)S(1)} %copy-done.5), kind=kLoop, calls=%fused_computation.50 | loop fusion | flops 1720320 | bytes 3489800 | tf_op jit(solution)/shard_map/mul | solution.py:92
  233.2 5.3 %copy.166 = f32[2,20,24,256]{3,2,1,0:T(8,128)} copy(f32[2,20,24,256]{2,1,3,0:T(8,128)} %add_multiply_fusion) | data formatting | bytes 1966080 | tf_op jit(solution)/shard_map/mul | solution.py:92
  (40 shorter events, 0.2 us)
Async XLA Ops:
  0.0 6.8 %copy-start.7 = (f32[20]{0:T(128)S(1)}, f32[20]{0:T(128)}, u32[]{:S(2)}) copy-start(f32[20]{0:T(128)} %param.5) | copy-start | bytes 244
  7.1 4.8 %copy-start.2 = (f32[20,24,256]{1,0,2:T(8,128)}, f32[20,24,256]{1,0,2:T(8,128)S(1)}, u32[]{:S(2)}) copy-start(f32[20,24,256]{1,0,2:T(8,128)S(1)} %broadcast_multiply_fusion) | copy-start | bytes 1474564
  12.0 2.6 %copy-start.1 = (f32[2,20,24,256]{2,1,3,0:T(8,128)}, f32[2,20,24,256]{2,1,3,0:T(8,128)S(1)}, u32[]{:S(2)}) copy-start(f32[2,20,24,256]{2,1,3,0:T(8,128)S(1)} %multiply_multiply_fusion.2) | copy-start | bytes 2949124
  15.0 1.4 collective-permute-start
  33.0 11.1 %collective-permute-start.2 = (f32[2,22,1,256]{3,1,2,0:T(8,128)S(1)}, f32[2,22,1,256]{3,1,2,0:T(8,128)S(1)}, u32[]{:S(2)}, u32[]{:S(2)}) collective-permute-start(f32[2,22,1,256]{3,1,2,0:T(8,128)S(1)} %copy.146), channel_id=1, source_target_pairs={{4,8},{8,4},{5,9},{9,5},{6,10},{10,6},{7,11},{11,7},{20,24},{24,20... | collective-permute-start | bytes 135176 | tf_op jit(solution)/shard_map/ppermute | solution.py:30
  38.3 9.9 %collective-permute-start.1 = (f32[2,22,1,256]{3,1,2,0:T(8,128)S(1)}, f32[2,22,1,256]{3,1,2,0:T(8,128)S(1)}, u32[]{:S(2)}, u32[]{:S(2)}) collective-permute-start(f32[2,22,1,256]{3,1,2,0:T(8,128)S(1)} %copy.145), channel_id=1, source_target_pairs={{0,4},{4,0},{8,12},{12,8},{1,5},{5,1},{9,13},{13,9},{2,6},{6,2},{1... | collective-permute-start | bytes 135176 | tf_op jit(solution)/shard_map/ppermute | solution.py:26
  48.2 14.3 %slice-start.2 = ((s8[6291456]{0:T(1024)(128)(4,1)}), s8[2097152]{0:T(1024)(128)(4,1)S(1)}, s32[]{:S(2)}) async-start(s8[6291456]{0:T(1024)(128)(4,1)} %bitcast.2), calls=%async_computation.2 | async-start | bytes 4194304
  52.4 10.1 %slice-start.3 = ((s8[6291456]{0:T(1024)(128)(4,1)}), s8[4194304]{0:T(1024)(128)(4,1)S(1)}, s32[]{:S(2)}) async-start(s8[6291456]{0:T(1024)(128)(4,1)} %bitcast.2), calls=%async_computation.3 | async-start | bytes 8388608
  63.5 3.9 %collective-permute-start.3 = (f32[2,22,26,1]{2,1,3,0:T(8,128)S(1)}, f32[2,22,26,1]{2,1,3,0:T(8,128)S(1)}, u32[]{:S(2)}, u32[]{:S(2)}) collective-permute-start(f32[2,22,26,1]{2,1,3,0:T(8,128)S(1)} %fusion.11), channel_id=1, source_target_pairs={{0,2},{2,0},{1,3},{3,1},{4,6},{6,4},{5,7},{7,5},{8,10},{10,8},{9,1... | collective-permute-start | bytes 13736 | tf_op jit(solution)/shard_map/ppermute | solution.py:26
  67.4 31.4 %copy-start.3 = (f32[20,24,256]{1,0,2:T(8,128)S(1)}, f32[20,24,256]{1,0,2:T(8,128)}, u32[]{:S(2)}) copy-start(f32[20,24,256]{1,0,2:T(8,128)} %copy-done.2) | copy-start | bytes 1474564
  109.0 2.6 %copy-start = (f32[2,20,24,256]{2,1,3,0:T(8,128)}, f32[2,20,24,256]{2,1,3,0:T(8,128)S(1)}, u32[]{:S(2)}) copy-start(f32[2,20,24,256]{2,1,3,0:T(8,128)S(1)} %get-tuple-element.19) | copy-start | bytes 2949124
  112.0 1.3 collective-permute-start.4
  130.0 7.1 %collective-permute-start.6 = (f32[2,22,1,256]{3,1,2,0:T(8,128)S(1)}, f32[2,22,1,256]{3,1,2,0:T(8,128)S(1)}, u32[]{:S(2)}, u32[]{:S(2)}) collective-permute-start(f32[2,22,1,256]{3,1,2,0:T(8,128)S(1)} %copy.159), channel_id=1, source_target_pairs={{4,8},{8,4},{5,9},{9,5},{6,10},{10,6},{7,11},{11,7},{20,24},{24,20... | collective-permute-start | bytes 135176 | tf_op jit(solution)/shard_map/ppermute | solution.py:30
  135.3 5.9 %collective-permute-start.5 = (f32[2,22,1,256]{3,1,2,0:T(8,128)S(1)}, f32[2,22,1,256]{3,1,2,0:T(8,128)S(1)}, u32[]{:S(2)}, u32[]{:S(2)}) collective-permute-start(f32[2,22,1,256]{3,1,2,0:T(8,128)S(1)} %copy.158), channel_id=1, source_target_pairs={{0,4},{4,0},{8,12},{12,8},{1,5},{5,1},{9,13},{13,9},{2,6},{6,2},{1... | collective-permute-start | bytes 135176 | tf_op jit(solution)/shard_map/ppermute | solution.py:26
  141.2 14.3 %slice-start = ((s8[6291456]{0:T(1024)(128)(4,1)}), s8[2097152]{0:T(1024)(128)(4,1)S(1)}, s32[]{:S(2)}) async-start(s8[6291456]{0:T(1024)(128)(4,1)} %bitcast), calls=%async_computation | async-start | bytes 4194304
  145.4 10.1 %slice-start.1 = ((s8[6291456]{0:T(1024)(128)(4,1)}), s8[4194304]{0:T(1024)(128)(4,1)S(1)}, s32[]{:S(2)}) async-start(s8[6291456]{0:T(1024)(128)(4,1)} %bitcast), calls=%async_computation.1 | async-start | bytes 8388608
  156.5 3.9 %collective-permute-start.7 = (f32[2,22,26,1]{2,1,3,0:T(8,128)S(1)}, f32[2,22,26,1]{2,1,3,0:T(8,128)S(1)}, u32[]{:S(2)}, u32[]{:S(2)}) collective-permute-start(f32[2,22,26,1]{2,1,3,0:T(8,128)S(1)} %fusion.10), channel_id=1, source_target_pairs={{0,2},{2,0},{1,3},{3,1},{4,6},{6,4},{5,7},{7,5},{8,10},{10,8},{9,1... | collective-permute-start | bytes 13736 | tf_op jit(solution)/shard_map/ppermute | solution.py:26
  160.4 31.4 %copy-start.4 = (f32[20,24,256]{1,0,2:T(8,128)S(1)}, f32[20,24,256]{1,0,2:T(8,128)}, u32[]{:S(2)}) copy-start(f32[20,24,256]{1,0,2:T(8,128)} %copy-done.2) | copy-start | bytes 1474564
  191.8 28.1 %copy-start.6 = (f32[2,20,24,256]{3,2,1,0:T(8,128)S(1)}, f32[2,20,24,256]{3,2,1,0:T(8,128)}, u32[]{:S(2)}) copy-start(f32[2,20,24,256]{3,2,1,0:T(8,128)} %param.4) | copy-start | bytes 2949124
  206.2 19.8 %copy-start.5 = (f32[20,24,256]{1,0,2:T(8,128)S(1)}, f32[20,24,256]{1,0,2:T(8,128)}, u32[]{:S(2)}) copy-start(f32[20,24,256]{1,0,2:T(8,128)} %copy-done.2) | copy-start | bytes 1474564
  206.3 1.2 collective-permute-start.8
  207.6 3.7 %collective-permute-start.9 = (f32[4,2,256]{2,0,1:T(4,128)S(1)}, f32[4,2,256]{2,0,1:T(4,128)S(1)}, u32[]{:S(2)}, u32[]{:S(2)}) collective-permute-start(f32[4,2,256]{2,0,1:T(4,128)S(1)} %fusion.12), channel_id=1, source_target_pairs={{0,2},{2,0},{1,3},{3,1},{4,6},{6,4},{5,7},{7,5},{8,10},{10,8},{9,1... | collective-permute-start | bytes 24584 | tf_op jit(solution)/shard_map/ppermute | solution.py:59
  211.3 3.7 %collective-permute-start.10 = (f32[4,2,256]{2,0,1:T(4,128)S(1)}, f32[4,2,256]{2,0,1:T(4,128)S(1)}, u32[]{:S(2)}, u32[]{:S(2)}) collective-permute-start(f32[4,2,256]{2,0,1:T(4,128)S(1)} %fusion.16), channel_id=1, source_target_pairs={{0,4},{4,0},{8,12},{12,8},{1,5},{5,1},{9,13},{13,9},{2,6},{6,2},{1... | collective-permute-start | bytes 24584 | tf_op jit(solution)/shard_map/ppermute | solution.py:59
  215.0 4.5 %collective-permute-start.11 = (f32[4,2,256]{2,0,1:T(4,128)S(1)}, f32[4,2,256]{2,0,1:T(4,128)S(1)}, u32[]{:S(2)}, u32[]{:S(2)}) collective-permute-start(f32[4,2,256]{2,0,1:T(4,128)S(1)} %add.135), channel_id=1, source_target_pairs={{0,8},{4,12},{8,0},{12,4},{1,9},{5,13},{9,1},{13,5},{2,10},{6,14},... | collective-permute-start | bytes 24584 | tf_op jit(solution)/shard_map/ppermute | solution.py:59

commit v2 on v1

v2 whole, which is shorter than its diff:
```python
import functools

import jax
import jax.numpy as jnp
from jax import lax
from jax.experimental import pallas as pl
from jax.experimental.pallas import tpu as pltpu
from jax.sharding import PartitionSpec as P

weight_vert = 2.0
weight_cross = 0.3
gain_bound = 1.6
total_weight = 10.4
diag_shift = 0.5
source_scale = 8.0

LANES = 128
GRANT = 8 << 20


def line_pairs(count, first):
    pairs = []
    for low in range(first, count - 1, 2):
        pairs += [(low, low + 1), (low + 1, low)]
    return pairs


def neighbours(low_edge, high_edge, axis):
    count, index = lax.axis_size(axis), lax.axis_index(axis)
    if count == 1:
        return jnp.zeros_like(low_edge), jnp.zeros_like(high_edge)
    even = index % 2 == 0
    first = lax.ppermute(jnp.where(even, high_edge, low_edge), axis, line_pairs(count, 0))
    if count == 2:
        second = jnp.zeros_like(first)
    else:
        second = lax.ppermute(jnp.where(even, low_edge, high_edge), axis, line_pairs(count, 1))
    return jnp.where(even, second, first), jnp.where(even, first, second)


def flipped(values, sizes, axes, bits):
    shape = [sizes[axis] for axis in axes]
    pairs = []
    for flat in range(functools.reduce(lambda a, b: a * b, shape, 1)):
        place, rest = [], flat
        for size in reversed(shape):
            place.insert(0, rest % size)
            rest //= size
        target = 0
        for where, size, bit in zip(place, shape, bits):
            target = target * size + (where ^ bit)
        pairs.append((flat, target))
    return lax.ppermute(values, axes, pairs)


def total(values):
    sizes = {axis: lax.axis_size(axis) for axis in ("layer", "col", "tile")}
    assert all(size & (size - 1) == 0 for size in sizes.values())
    first = 1
    if sizes["col"] > 1 and sizes["layer"] == 2:
        values = (
            values
            + flipped(values, sizes, ("layer",), (1,))
            + flipped(values, sizes, ("col",), (1,))
            + flipped(values, sizes, ("col", "layer"), (1, 1))
        )
        first = 2
    else:
        values = values + flipped(values, sizes, ("layer",), (1,))
    for axis, bit in (("col", first), ("tile", 1)):
        while bit < sizes[axis]:
            values = values + flipped(values, sizes, (axis,), (bit,))
            bit *= 2
    return values


def tiles_of(plane):
    return [plane[:, at : at + LANES] for at in range(0, plane.shape[1], LANES)]


def sides(tiles, low_row, high_row, low_col, high_col):
    rows, lanes = tiles[0].shape
    row = lax.broadcasted_iota(jnp.int32, (rows, lanes), 0)
    lane = lax.broadcasted_iota(jnp.int32, (rows, lanes), 1)
    ahead = [pltpu.roll(tile, lanes - 1, 1) for tile in tiles]
    behind = [pltpu.roll(tile, 1, 1) for tile in tiles]
    ahead.append(0.0 if high_col is None else high_col)
    behind.insert(0, 0.0 if low_col is None else low_col)
    out = []
    for i, tile in enumerate(tiles):
        below = jnp.where(row == rows - 1, 0.0 if high_row is None else high_row[i], pltpu.roll(tile, rows - 1, 0))
        above = jnp.where(row == 0, 0.0 if low_row is None else low_row[i], pltpu.roll(tile, 1, 0))
        right = jnp.where(lane == lanes - 1, ahead[i + 1], ahead[i])
        left = jnp.where(lane == 0, behind[i], behind[i + 1])
        out.append((below + above) + (right + left))
    return out


def levels(tiles, side):
    return [weight_vert * tile + weight_cross * s for tile, s in zip(tiles, side)]


def gains(level, column, multiplier):
    metric = level * column * multiplier
    scale = metric / (gain_bound * total_weight * metric + diag_shift)
    return metric, scale


def edges_out(k, tiles, rows_low, rows_high, packs):
    rows, lanes = tiles[0].shape
    for i, tile in enumerate(tiles):
        at = i * (rows_low.shape[0] // len(tiles)) + k
        rows_low[pl.ds(at, 1), :] = tile[0:1]
        rows_high[pl.ds(at, 1), :] = tile[rows - 1 : rows]
    lane = lax.broadcasted_iota(jnp.int32, (rows, lanes), 1)
    low, high = packs
    low = jnp.where(lane == k, pltpu.roll(tiles[0], k, 1), low)
    high = jnp.where(lane == k, pltpu.roll(tiles[-1], k + 1, 1), high)
    return low, high


def weighted_kernel(
    own, other, profile_own, profile_other, column, error, weighted, gain, rows_low, rows_high, cols_low, cols_high, sums
):
    layer = lax.axis_index("layer")
    half, rows, width = own.shape[1:]
    columns = column[...]
    multiplier = 1.0 + 0.002 * error[layer].astype(jnp.float32)

    def part(source, profile, base, carry):
        def step(at, carry):
            packs, acc = carry
            k = base + at
            metric, scale = gains(profile[at], columns, multiplier)
            g = metric * scale
            forcing = source_scale * source[layer, at]
            u = g * forcing
            weighted[k] = u
            gain[k] = g
            packs = edges_out(k, tiles_of(u), rows_low, rows_high, packs)
            return packs, acc + u * forcing

        return lax.fori_loop(0, half, step, carry, unroll=4)

    zeros = jnp.zeros((rows, LANES), jnp.float32)
    carry = ((zeros, zeros), jnp.zeros((rows, width), jnp.float32))
    carry = part(own, profile_own, layer * half, carry)
    (low, high), acc = part(other, profile_other, (1 - layer) * half, carry)
    cols_low[...] = low
    cols_high[...] = high
    sums[...] = acc


def image_kernel(
    weighted,
    gain,
    low_rows,
    high_rows,
    low_cols,
    high_cols,
    kept,
    sent,
    again,
    rows_low,
    rows_high,
    cols_low,
    cols_high,
    sums,
):
    layer = lax.axis_index("layer")
    count, rows, width = weighted.shape
    half = count // 2
    base = layer * half
    starts = [i * count for i in range(width // LANES)]
    pack_low, pack_high = low_cols[...], high_cols[...]

    def emit(k, u, image, packs, acc):
        both = jnp.concatenate(image, axis=1)
        ub = gain[k] * both
        again[k] = ub
        inside = (k >= base) & (k < base + half)

        @pl.when(inside)
        def _():
            kept[k - base] = both

        @pl.when(jnp.logical_not(inside))
        def _():
            sent[k - (half - base)] = both

        packs = edges_out(k, tiles_of(ub), rows_low, rows_high, packs)
        return packs, (acc[0] + u * both, acc[1] + ub * both)

    def step(k, carry):
        side_before, level_twice, level_before, packs, acc = carry
        tiles = tiles_of(weighted[k])
        low_row = [low_rows[pl.ds(start + k, 1), :] for start in starts]
        high_row = [high_rows[pl.ds(start + k, 1), :] for start in starts]
        low_col = pltpu.roll(pack_low, lax.rem(LANES - k, LANES), 1)
        high_col = pltpu.roll(pack_high, LANES - 1 - k, 1)
        side = sides(tiles, low_row, high_row, low_col, high_col)
        level = levels(tiles, side)
        image = [s + a + b for s, a, b in zip(side_before, level_twice, level)]
        before = jnp.maximum(k - 1, 0)
        packs, acc = emit(before, weighted[before], image, packs, acc)
        return side, level_before, level, packs, acc

    zero = [jnp.zeros((rows, LANES), jnp.float32) for _ in starts]
    pack = jnp.zeros((rows, LANES), jnp.float32)
    full = jnp.zeros((rows, width), jnp.float32)
    first_tiles = tiles_of(weighted[0])
    first = sides(
        first_tiles,
        [low_rows[start : start + 1, :] for start in starts],
        [high_rows[start : start + 1, :] for start in starts],
        pack_low,
        pltpu.roll(pack_high, LANES - 1, 1),
    )
    carry = (first, zero, levels(first_tiles, first), (pack, pack), (full, full))
    side, level_twice, _, packs, acc = lax.fori_loop(1, count, step, carry, unroll=3)
    image = [s + a for s, a in zip(side, level_twice)]
    packs, acc = emit(count - 1, weighted[count - 1], image, packs, acc)
    cols_low[...], cols_high[...] = packs
    sums[0], sums[1] = acc


def quadratic_kernel(again, sums):
    count, rows, width = again.shape

    def step(k, carry):
        before, acc = carry
        plane = again[k]
        tiles = tiles_of(plane)
        side = sides(tiles, None, None, None, None)
        level = jnp.concatenate(levels(tiles, side), axis=1)
        acc = acc + plane * jnp.concatenate(side, axis=1) + 2.0 * before * level
        return plane, acc

    zero = jnp.zeros((rows, width), jnp.float32)
    _, acc = lax.fori_loop(0, count, step, (zero, zero), unroll=4)
    sums[...] = acc


def near(values, axis, count):
    size = values.shape[axis]
    place = lax.rem(lax.broadcasted_iota(jnp.int32, values.shape, axis), count)
    up = jnp.where(place == count - 1, 0.0, pltpu.roll(values, size - 1, axis))
    down = jnp.where(place == 0, 0.0, pltpu.roll(values, 1, axis))
    return values + weight_cross * (up + down)


def collect_kernel(
    rows_low, rows_high, cols_low, cols_high, low_rows, high_rows, low_cols, high_cols, sum_a, sum_b, sum_c, out
):
    layer = lax.axis_index("layer")
    count = rows_low.shape[0] // (sum_a.shape[1] // LANES)
    cross_rows = rows_low[...] * near(low_rows[...], 0, count) + rows_high[...] * near(high_rows[...], 0, count)
    cross_cols = cols_low[...] * near(low_cols[...], 1, LANES) + cols_high[...] * near(high_cols[...], 1, LANES)

    def line(values):
        values = jnp.sum(values, axis=0, keepdims=True)
        return functools.reduce(lambda a, b: a + b, tiles_of(values))

    out[...] = jnp.zeros_like(out)
    out[pl.ds(8 * layer, 1), :] = line(sum_a[...])
    out[pl.ds(8 * layer + 1, 1), :] = line(sum_b[0])
    out[pl.ds(8 * layer + 2, 1), :] = line(sum_b[1])
    out[pl.ds(8 * layer + 3, 1), :] = line(sum_c[...]) + line(cross_rows) + line(cross_cols)


def final_kernel(source, profile, column, error, kept, other, sums, out):
    layer = lax.axis_index("layer")
    half = source.shape[1]
    columns = column[...]

    def factors(base):
        values = jnp.sum(sums[pl.ds(base, 8), :], axis=1, keepdims=True)
        zz, zb, bb, bbb = (values[i : i + 1] for i in range(4))
        delta = zz - zb
        alpha = zz / delta
        rest = -zb / delta
        beta = (zz * bb - zb * zb) / (delta * delta)
        gamma = zz * beta
        delta_next = gamma - (rest * rest * zb + 2.0 * alpha * rest * bb + alpha * alpha * bbb)
        alpha_next = gamma / (delta_next - beta * gamma / alpha)
        return source_scale * (alpha + alpha_next * (rest + beta)), alpha_next * alpha

    for which, image in ((layer, kept), (1 - layer, other)):
        multiplier = 1.0 + 0.002 * error[which].astype(jnp.float32)
        first, second = factors(8 * which)

        def step(k, _):
            _, scale = gains(profile[k], columns, multiplier)
            out[which, k] = scale * (first * source[which, k] + second * image[k])
            return 0

        lax.fori_loop(0, half, step, 0, unroll=4)


def call(kernel, out_shape, args, name, scalars=()):
    vmem = pl.BlockSpec(memory_space=pltpu.VMEM)
    smem = pl.BlockSpec(memory_space=pltpu.SMEM)
    return pl.pallas_call(
        kernel,
        out_shape=[jax.ShapeDtypeStruct(shape, jnp.float32) for shape in out_shape],
        in_specs=[smem if i in scalars else vmem for i in range(len(args))],
        out_specs=[vmem] * len(out_shape),
        compiler_params=pltpu.CompilerParams(vmem_limit_bytes=GRANT),
        name=name,
    )(*args)


def local(source, profile, column, terrain_height_error):
    copies, half, rows, width = source.shape
    count = 2 * half
    assert lax.axis_size("layer") == copies == 2 and count <= LANES and width % LANES == 0
    swap = [(0, 1), (1, 0)]
    other = lax.ppermute(source, "layer", swap)
    profile_other = lax.ppermute(profile, "layer", swap)
    block, row, pack = (count, rows, width), (width // LANES * count, LANES), (rows, LANES)
    weighted, gain, rows_low, rows_high, cols_low, cols_high, sum_a = call(
        weighted_kernel,
        [block, block, row, row, pack, pack, (rows, width)],
        (source, other, profile, profile_other, column, terrain_height_error),
        "weighted",
        (2, 3),
    )
    low_rows, high_rows = neighbours(rows_low, rows_high, "tile")
    low_cols, high_cols = neighbours(cols_low, cols_high, "col")
    part = (half, rows, width)
    kept, sent, again, rows_low, rows_high, cols_low, cols_high, sum_b = call(
        image_kernel,
        [part, part, block, row, row, pack, pack, (2, rows, width)],
        (weighted, gain, low_rows, high_rows, low_cols, high_cols),
        "image",
    )
    low_rows, high_rows = neighbours(rows_low, rows_high, "tile")
    low_cols, high_cols = neighbours(cols_low, cols_high, "col")
    received = lax.ppermute(sent, "layer", swap)
    (sum_c,) = call(quadratic_kernel, [(rows, width)], (again,), "quadratic")
    (sums,) = call(
        collect_kernel,
        [(16, LANES)],
        (rows_low, rows_high, cols_low, cols_high, low_rows, high_rows, low_cols, high_cols, sum_a, sum_b, sum_c),
        "collect",
    )
    sums = total(sums)
    (out,) = call(
        final_kernel,
        [source.shape],
        (source, profile, column, terrain_height_error, kept, received, sums),
        "final",
        (1,),
    )
    return out


def solution(mesh):
    placed = (
        P("group", "layer", "tile", "col"),
        P("layer"),
        P(("group", "tile"), "col"),
        P("group", "tile", "col"),
    )
    return jax.shard_map(
        local,
        mesh=mesh,
        in_specs=placed,
        out_specs=P("group", "layer", "tile", "col"),
        check_vma=False,
    )
```

time: 239 us -> 44.2 us (0.18)
  other arithmetic: 146 us -> 0.07 us
  local copies, waits for them, and re-layouts: 59.9 us -> 1.95 us
  Pallas kernels: 0 us -> 10.2 us
  waiting for transfers between devices: 17 us -> 10.7 us
  starting transfers between devices: 15.9 us -> 20.8 us
    add x6 -> x3, other arithmetic: 63.7 us -> 0.01 us  [the longest x2 0.01 us: total(): values = values + flipped(values, sizes, (axis,), (bit,))]
    mul x7 -> x0, other arithmetic: 23.6 us -> none  [the longest x1 10.2 us: local(): again = gain * image]
    select_n x10 -> x0, local copies, waits for them, and re-layouts: 21.4 us -> none  [the longest x4 9.26 us: neighbours(): jnp.where(even, high_edge, low_edge)]
    select_n x6 -> x4, other arithmetic: 20.3 us -> 0.03 us  [neighbours(): return (jnp.where(even, second, first), jnp.where(even, first, second))]
    ppermute x4 -> x0, local copies, waits for them, and re-layouts: 16.6 us -> none  [the longest x2 8.37 us: neighbours(): lax.ppermute(jnp.where(even, high_edge, low_edge), axis, line_pairs(count...]
    reduce_sum x2 -> x0, other arithmetic: 14.5 us -> none  [the longest x1 14.4 us: local(): jnp.sum(weighted * forcing, axis=lanes)]
    select_n x2 -> x0, other arithmetic: 12.4 us -> none  [neighbours(): jnp.where(even, low_edge, high_edge)]
    mul x2 -> x0, local copies, waits for them, and re-layouts: 10.3 us -> none  [the longest x1 5.32 us: local(): scale * ((alpha + alpha_next * (rest + beta)) * forcing + alpha_next * al...]
  transfers between devices with their start and end apart: 12 -> 14, of which waited for: 8 -> 7; matrix products, arithmetic and copies ran while one was open for 7% -> 0% of each run, Pallas kernels for 0% -> 3%
where the time goes in v2:
time: 44.2 us; the launch traced here: 44 us
  starting transfers between devices  20.8 us (47%)
  waiting for transfers between devices  10.7 us (24%)
  Pallas kernels  10.2 us (23%)
  local copies, waits for them, and re-layouts  1.95 us (4%)
    pallas_call x5, Pallas kernels, call(): pl.pallas_call(kernel, out_shape=[jax.ShapeDtypeStruct(shape, jnp.float32...  10.2 us
    ppermute x4, starting transfers between devices, neighbours(): lax.ppermute(jnp.where(even, high_edge, low_edge), axis, line_pairs(count...  9.81 us
    ppermute x5, starting transfers between devices, flipped(): return lax.ppermute(values, axes, pairs)  9.08 us
    ppermute x5, waiting for transfers between devices, flipped(): return lax.ppermute(values, axes, pairs)  5.43 us
    ppermute x4, waiting for transfers between devices, neighbours(): lax.ppermute(jnp.where(even, high_edge, low_edge), axis, line_pairs(count...  2.97 us
    ppermute x1, waiting for transfers between devices, local(): profile_other = lax.ppermute(profile, 'layer', swap)  2.34 us
    unnamed x12, local copies, waits for them, and re-layouts  1.95 us
    ppermute x2, starting transfers between devices, neighbours(): lax.ppermute(jnp.where(even, low_edge, high_edge), axis, line_pairs(count...  1.3 us
  transfers between devices with their start and end apart: 14, of which 7 were waited for; matrix products, arithmetic and copies ran while one was open for 0% of the time, Pallas kernels for 3%

profile of v2, /device:TPU:0, one launch (start us, length us, event | category | flops | bytes accessed | tf_op | source)
XLA Modules:
  0.0 44.0 jit_solution(7155780173768786937)
XLA Ops:
  0.0 0.0 copy-start.2
  0.0 0.5 %collective-permute-start = (f32[2,20,24,256]{3,2,1,0:T(8,128)}, f32[2,20,24,256]{3,2,1,0:T(8,128)S(1)}, u32[]{:S(2)}, u32[]{:S(2)}) collective-permute-start(f32[2,20,24,256]{3,2,1,0:T(8,128)} %source.1), channel_id=1, source_target_pairs={{0,1},{1,0},{2,3},{3,2},{4,5},{5,4},{6,7},{7,6},{8,9},{9,8},{10,11... | collective-permute-start | bytes 2949128 | tf_op jit(solution)/shard_map/ppermute | solution.py:318
  0.5 0.1 collective-permute-start.1
  0.6 0.0 copy-start.5
  0.6 2.3 %collective-permute-done.1.profile_other = f32[20]{0:T(128)S(1)} collective-permute-done((f32[20]{0:T(128)}, f32[20]{0:T(128)S(1)}, u32[]{:S(2)}, u32[]{:S(2)}) %collective-permute-start.1) | collective-permute-done | bytes 112 | tf_op jit(solution)/shard_map/ppermute | solution.py:319
  2.9 0.0 collective-permute-done.other
  2.9 0.0 copy-done.2
  2.9 0.0 copy-done.5
  2.9 0.0 copy-start
  2.9 1.2 %copy-done = f32[2,20,24,256]{3,2,1,0:T(8,128)S(1)} copy-done((f32[2,20,24,256]{3,2,1,0:T(8,128)S(1)}, f32[2,20,24,256]{3,2,1,0:T(8,128)}, u32[]{:S(2)}) %copy-start) | copy-done | bytes 983064
  4.1 0.0 copy-start.3
  4.1 0.7 %copy-done.3 = f32[24,256]{1,0:T(8,128)S(1)} copy-done((f32[24,256]{1,0:T(8,128)S(1)}, f32[24,256]{1,0:T(8,128)}, u32[]{:S(2)}) %copy-start.3) | copy-done | bytes 24600
  4.9 1.7 %weighted.1 = (f32[40,24,256]{2,1,0:T(8,128)S(1)}, f32[40,24,256]{2,1,0:T(8,128)S(1)}, f32[80,128]{1,0:T(8,128)S(1)}, f32[80,128]{1,0:T(8,128)S(1)}, f32[24,128]...) custom-call(f32[2,20,24,256]{3,2,1,0:T(8,128)S(1)} %copy-done, ...), custom_call_target="tpu_custom_call" | custom-call | tf_op jit(solution)/shard_map/weighted/pallas_call | solution.py:303
  6.6 2.9 %collective-permute-start.4 = (f32[24,128]{1,0:T(8,128)S(1)}, f32[24,128]{1,0:T(8,128)S(1)}, u32[]{:S(2)}, u32[]{:S(2)}) collective-permute-start(f32[24,128]{1,0:T(8,128)S(1)} %broadcast_select_fusion.13), channel_id=1, source_target_pairs={{0,2},{2,0},{1,3},{3,1},{4,6},{6,4},{5,7},{7,5},{8,10},{10,8},{9,1... | collective-permute-start | bytes 36872 | tf_op jit(solution)/shard_map/ppermute | solution.py:33
  9.5 1.6 %collective-permute-start.3 = (f32[80,128]{1,0:T(8,128)S(1)}, f32[80,128]{1,0:T(8,128)S(1)}, u32[]{:S(2)}, u32[]{:S(2)}) collective-permute-start(f32[80,128]{1,0:T(8,128)S(1)} %get-tuple-element.41), channel_id=1, source_target_pairs={{0,4},{4,0},{8,12},{12,8},{1,5},{5,1},{9,13},{13,9},{2,6},{6,2},{1... | collective-permute-start | bytes 122888 | tf_op jit(solution)/shard_map/ppermute | solution.py:33
  11.1 0.7 %collective-permute-start.2 = (f32[80,128]{1,0:T(8,128)S(1)}, f32[80,128]{1,0:T(8,128)S(1)}, u32[]{:S(2)}, u32[]{:S(2)}) collective-permute-start(f32[80,128]{1,0:T(8,128)S(1)} %get-tuple-element.42), channel_id=1, source_target_pairs={{4,8},{8,4},{5,9},{9,5},{6,10},{10,6},{7,11},{11,7},{20,24},{24,20... | collective-permute-start | bytes 122888 | tf_op jit(solution)/shard_map/ppermute | solution.py:37
  11.8 0.0 collective-permute-done.4
  11.8 1.7 %collective-permute-done.3 = f32[80,128]{1,0:T(8,128)S(1)} collective-permute-done((f32[80,128]{1,0:T(8,128)S(1)}, f32[80,128]{1,0:T(8,128)S(1)}, u32[]{:S(2)}, u32[]{:S(2)}) %collective-permute-start.3) | collective-permute-done | bytes 40992 | tf_op jit(solution)/shard_map/ppermute | solution.py:33
  13.6 0.0 collective-permute-done.2
  13.6 4.9 %image.1 = (f32[20,24,256]{2,1,0:T(8,128)S(1)}, f32[20,24,256]{2,1,0:T(8,128)S(1)}, f32[40,24,256]{2,1,0:T(8,128)S(1)}, f32[80,128]{1,0:T(8,128)S(1)}, f32[80,12...) custom-call(f32[40,24,256]{2,1,0:T(8,128)S(1)} %get-tuple-element.20.weighted, ...), custom_call_target="tpu_custom_call" | custom-call | tf_op jit(solution)/shard_map/image/pallas_call | solution.py:303
  18.5 0.0 copy-start.1
  18.5 0.2 collective-permute-start.8
  18.7 1.3 %quadratic.1.sum_c = f32[24,256]{1,0:T(8,128)S(1)} custom-call(f32[40,24,256]{2,1,0:T(8,128)S(1)} %get-tuple-element.34.again), custom_call_target="tpu_custom_call" | custom-call | tf_op jit(solution)/shard_map/quadratic/pallas_call | solution.py:303
  20.0 5.1 %collective-permute-start.7 = (f32[80,128]{1,0:T(8,128)S(1)}, f32[80,128]{1,0:T(8,128)S(1)}, u32[]{:S(2)}, u32[]{:S(2)}) collective-permute-start(f32[80,128]{1,0:T(8,128)S(1)} %get-tuple-element.37), channel_id=1, source_target_pairs={{0,4},{4,0},{8,12},{12,8},{1,5},{5,1},{9,13},{13,9},{2,6},{6,2},{1... | collective-permute-start | bytes 122888 | tf_op jit(solution)/shard_map/ppermute | solution.py:33
  25.1 0.7 %collective-permute-start.6 = (f32[80,128]{1,0:T(8,128)S(1)}, f32[80,128]{1,0:T(8,128)S(1)}, u32[]{:S(2)}, u32[]{:S(2)}) collective-permute-start(f32[80,128]{1,0:T(8,128)S(1)} %get-tuple-element.38), channel_id=1, source_target_pairs={{4,8},{8,4},{5,9},{9,5},{6,10},{10,6},{7,11},{11,7},{20,24},{24,20... | collective-permute-start | bytes 122888 | tf_op jit(solution)/shard_map/ppermute | solution.py:37
  25.7 0.1 collective-permute-start.5
  25.8 0.0 collective-permute-done.8
  25.8 1.2 %collective-permute-done.7 = f32[80,128]{1,0:T(8,128)S(1)} collective-permute-done((f32[80,128]{1,0:T(8,128)S(1)}, f32[80,128]{1,0:T(8,128)S(1)}, u32[]{:S(2)}, u32[]{:S(2)}) %collective-permute-start.7) | collective-permute-done | bytes 40992 | tf_op jit(solution)/shard_map/ppermute | solution.py:33
  27.1 0.0 collective-permute-done.6
  27.1 0.1 collect.1
  27.2 0.4 collective-permute-start.11
  27.6 1.2 %collective-permute-start.10 = (f32[16,128]{1,0:T(8,128)S(1)}, f32[16,128]{1,0:T(8,128)S(1)}, u32[]{:S(2)}, u32[]{:S(2)}) collective-permute-start(f32[16,128]{1,0:T(8,128)S(1)} %collect.1), channel_id=1, source_target_pairs={{0,2},{2,0},{1,3},{3,1},{4,6},{6,4},{5,7},{7,5},{8,10},{10,8},{9,1... | collective-permute-start | bytes 24584 | tf_op jit(solution)/shard_map/ppermute | solution.py:53
  28.8 0.3 collective-permute-start.9
  29.1 1.3 %collective-permute-done.11 = f32[16,128]{1,0:T(8,128)S(1)} collective-permute-done((f32[16,128]{1,0:T(8,128)S(1)}, f32[16,128]{1,0:T(8,128)S(1)}, u32[]{:S(2)}, u32[]{:S(2)}) %collective-permute-start.11) | collective-permute-done | bytes 8224 | tf_op jit(solution)/shard_map/ppermute | solution.py:53
  30.3 0.9 %collective-permute-done.10 = f32[16,128]{1,0:T(8,128)S(1)} collective-permute-done((f32[16,128]{1,0:T(8,128)S(1)}, f32[16,128]{1,0:T(8,128)S(1)}, u32[]{:S(2)}, u32[]{:S(2)}) %collective-permute-start.10) | collective-permute-done | bytes 8224 | tf_op jit(solution)/shard_map/ppermute | solution.py:53
  31.3 0.0 collective-permute-done.9
  31.3 0.0 copy-start.4
  31.3 3.7 %collective-permute-start.12 = (f32[16,128]{1,0:T(8,128)S(1)}, f32[16,128]{1,0:T(8,128)S(1)}, u32[]{:S(2)}, u32[]{:S(2)}) collective-permute-start(f32[16,128]{1,0:T(8,128)S(1)} %add_add_fusion), channel_id=1, source_target_pairs={{0,4},{4,0},{8,12},{12,8},{1,5},{5,1},{9,13},{13,9},{2,6},{6,2},{1... | collective-permute-start | bytes 24584 | tf_op jit(solution)/shard_map/ppermute | solution.py:53
  35.0 1.6 %collective-permute-done.12 = f32[16,128]{1,0:T(8,128)S(1)} collective-permute-done((f32[16,128]{1,0:T(8,128)S(1)}, f32[16,128]{1,0:T(8,128)S(1)}, u32[]{:S(2)}, u32[]{:S(2)}) %collective-permute-start.12) | collective-permute-done | bytes 8224 | tf_op jit(solution)/shard_map/ppermute | solution.py:53
  36.6 3.5 %collective-permute-start.13 = (f32[16,128]{1,0:T(8,128)S(1)}, f32[16,128]{1,0:T(8,128)S(1)}, u32[]{:S(2)}, u32[]{:S(2)}) collective-permute-start(f32[16,128]{1,0:T(8,128)S(1)} %add.29), channel_id=1, source_target_pairs={{0,8},{4,12},{8,0},{12,4},{1,9},{5,13},{9,1},{13,5},{2,10},{6,14},... | collective-permute-start | bytes 24584 | tf_op jit(solution)/shard_map/ppermute | solution.py:53
  40.1 1.6 %collective-permute-done.13 = f32[16,128]{1,0:T(8,128)S(1)} collective-permute-done((f32[16,128]{1,0:T(8,128)S(1)}, f32[16,128]{1,0:T(8,128)S(1)}, u32[]{:S(2)}, u32[]{:S(2)}) %collective-permute-start.13) | collective-permute-done | bytes 8224 | tf_op jit(solution)/shard_map/ppermute | solution.py:53
  41.7 0.0 collective-permute-done.5.other
  41.7 0.0 copy-done.1
  41.7 0.0 copy-done.4
  41.7 2.2 %final.1 = f32[2,20,24,256]{3,2,1,0:T(8,128)} custom-call(f32[2,20,24,256]{3,2,1,0:T(8,128)S(1)} %copy-done.1, f32[20]{0:T(128)S(1)} %copy-done.5, f32[24,256]{1,0:T(8,128)S(1)} %copy-done.4, s32[2,24,256]{2,1,0:T(8,128)S(1)} %copy-done.2, f32[20,24,256]{2,1,0:T(8,128)S(1)} %get-tuple-element.26.kept, f32[20,24,256]{2,1,0:T(8,128)S(1)} %collective-permute-done.5.other, ...), custom_call_target="tpu_custom_call" | custom-call | tf_op jit(solution)/shard_map/final/pallas_call | solution.py:303
  (11 shorter events, 0.1 us)
Async XLA Ops:
  0.0 2.9 %copy-start.2 = (s32[2,24,256]{2,1,0:T(8,128)S(1)}, s32[2,24,256]{2,1,0:T(8,128)}, u32[]{:S(2)}) copy-start(s32[2,24,256]{2,1,0:T(8,128)} %error.3) | copy-start | bytes 147460
  0.0 2.9 %collective-permute-start = (f32[2,20,24,256]{3,2,1,0:T(8,128)}, f32[2,20,24,256]{3,2,1,0:T(8,128)S(1)}, u32[]{:S(2)}, u32[]{:S(2)}) collective-permute-start(f32[2,20,24,256]{3,2,1,0:T(8,128)} %source.1), channel_id=1, source_target_pairs={{0,1},{1,0},{2,3},{3,2},{4,5},{5,4},{6,7},{7,6},{8,9},{9,8},{10,11... | collective-permute-start | bytes 2949128 | tf_op jit(solution)/shard_map/ppermute | solution.py:318
  0.5 2.4 %collective-permute-start.1 = (f32[20]{0:T(128)}, f32[20]{0:T(128)S(1)}, u32[]{:S(2)}, u32[]{:S(2)}) collective-permute-start(f32[20]{0:T(128)} %profile.1), channel_id=1, source_target_pairs={{0,1},{1,0},{2,3},{3,2},{4,5},{5,4},{6,7},{7,6},{8,9},{9,8},{10,11... | collective-permute-start | bytes 248 | tf_op jit(solution)/shard_map/ppermute | solution.py:319
  0.6 2.3 %copy-start.5 = (f32[20]{0:T(128)S(1)}, f32[20]{0:T(128)}, u32[]{:S(2)}) copy-start(f32[20]{0:T(128)} %profile.1) | copy-start | bytes 244
  2.9 1.2 %copy-start = (f32[2,20,24,256]{3,2,1,0:T(8,128)S(1)}, f32[2,20,24,256]{3,2,1,0:T(8,128)}, u32[]{:S(2)}) copy-start(f32[2,20,24,256]{3,2,1,0:T(8,128)} %source.1) | copy-start | bytes 2949124
  4.1 0.7 %copy-start.3 = (f32[24,256]{1,0:T(8,128)S(1)}, f32[24,256]{1,0:T(8,128)}, u32[]{:S(2)}) copy-start(f32[24,256]{1,0:T(8,128)} %column.3) | copy-start | bytes 73732
  6.6 5.2 %collective-permute-start.4 = (f32[24,128]{1,0:T(8,128)S(1)}, f32[24,128]{1,0:T(8,128)S(1)}, u32[]{:S(2)}, u32[]{:S(2)}) collective-permute-start(f32[24,128]{1,0:T(8,128)S(1)} %broadcast_select_fusion.13), channel_id=1, source_target_pairs={{0,2},{2,0},{1,3},{3,1},{4,6},{6,4},{5,7},{7,5},{8,10},{10,8},{9,1... | collective-permute-start | bytes 36872 | tf_op jit(solution)/shard_map/ppermute | solution.py:33
  9.5 4.1 %collective-permute-start.3 = (f32[80,128]{1,0:T(8,128)S(1)}, f32[80,128]{1,0:T(8,128)S(1)}, u32[]{:S(2)}, u32[]{:S(2)}) collective-permute-start(f32[80,128]{1,0:T(8,128)S(1)} %get-tuple-element.41), channel_id=1, source_target_pairs={{0,4},{4,0},{8,12},{12,8},{1,5},{5,1},{9,13},{13,9},{2,6},{6,2},{1... | collective-permute-start | bytes 122888 | tf_op jit(solution)/shard_map/ppermute | solution.py:33
  11.1 2.4 %collective-permute-start.2 = (f32[80,128]{1,0:T(8,128)S(1)}, f32[80,128]{1,0:T(8,128)S(1)}, u32[]{:S(2)}, u32[]{:S(2)}) collective-permute-start(f32[80,128]{1,0:T(8,128)S(1)} %get-tuple-element.42), channel_id=1, source_target_pairs={{4,8},{8,4},{5,9},{9,5},{6,10},{10,6},{7,11},{11,7},{20,24},{24,20... | collective-permute-start | bytes 122888 | tf_op jit(solution)/shard_map/ppermute | solution.py:37
  18.5 23.2 %copy-start.1 = (f32[2,20,24,256]{3,2,1,0:T(8,128)S(1)}, f32[2,20,24,256]{3,2,1,0:T(8,128)}, u32[]{:S(2)}) copy-start(f32[2,20,24,256]{3,2,1,0:T(8,128)} %source.1) | copy-start | bytes 2949124
  18.5 7.3 %collective-permute-start.8 = (f32[24,128]{1,0:T(8,128)S(1)}, f32[24,128]{1,0:T(8,128)S(1)}, u32[]{:S(2)}, u32[]{:S(2)}) collective-permute-start(f32[24,128]{1,0:T(8,128)S(1)} %broadcast_select_fusion.12), channel_id=1, source_target_pairs={{0,2},{2,0},{1,3},{3,1},{4,6},{6,4},{5,7},{7,5},{8,10},{10,8},{9,1... | collective-permute-start | bytes 36872 | tf_op jit(solution)/shard_map/ppermute | solution.py:33
  20.0 7.1 %collective-permute-start.7 = (f32[80,128]{1,0:T(8,128)S(1)}, f32[80,128]{1,0:T(8,128)S(1)}, u32[]{:S(2)}, u32[]{:S(2)}) collective-permute-start(f32[80,128]{1,0:T(8,128)S(1)} %get-tuple-element.37), channel_id=1, source_target_pairs={{0,4},{4,0},{8,12},{12,8},{1,5},{5,1},{9,13},{13,9},{2,6},{6,2},{1... | collective-permute-start | bytes 122888 | tf_op jit(solution)/shard_map/ppermute | solution.py:33
  25.1 2.0 %collective-permute-start.6 = (f32[80,128]{1,0:T(8,128)S(1)}, f32[80,128]{1,0:T(8,128)S(1)}, u32[]{:S(2)}, u32[]{:S(2)}) collective-permute-start(f32[80,128]{1,0:T(8,128)S(1)} %get-tuple-element.38), channel_id=1, source_target_pairs={{4,8},{8,4},{5,9},{9,5},{6,10},{10,6},{7,11},{11,7},{20,24},{24,20... | collective-permute-start | bytes 122888 | tf_op jit(solution)/shard_map/ppermute | solution.py:37
  25.7 16.0 %collective-permute-start.5 = (f32[20,24,256]{2,1,0:T(8,128)S(1)}, f32[20,24,256]{2,1,0:T(8,128)S(1)}, u32[]{:S(2)}, u32[]{:S(2)}) collective-permute-start(f32[20,24,256]{2,1,0:T(8,128)S(1)} %get-tuple-element.27), channel_id=1, source_target_pairs={{0,1},{1,0},{2,3},{3,2},{4,5},{5,4},{6,7},{7,6},{8,9},{9,8},{10,11... | collective-permute-start | bytes 1474568 | tf_op jit(solution)/shard_map/ppermute | solution.py:339
  27.2 3.2 %collective-permute-start.11 = (f32[16,128]{1,0:T(8,128)S(1)}, f32[16,128]{1,0:T(8,128)S(1)}, u32[]{:S(2)}, u32[]{:S(2)}) collective-permute-start(f32[16,128]{1,0:T(8,128)S(1)} %collect.1), channel_id=1, source_target_pairs={{0,3},{1,2},{2,1},{3,0},{4,7},{5,6},{6,5},{7,4},{8,11},{9,10},{10,... | collective-permute-start | bytes 24584 | tf_op jit(solution)/shard_map/ppermute | solution.py:53
  27.6 3.7 %collective-permute-start.10 = (f32[16,128]{1,0:T(8,128)S(1)}, f32[16,128]{1,0:T(8,128)S(1)}, u32[]{:S(2)}, u32[]{:S(2)}) collective-permute-start(f32[16,128]{1,0:T(8,128)S(1)} %collect.1), channel_id=1, source_target_pairs={{0,2},{2,0},{1,3},{3,1},{4,6},{6,4},{5,7},{7,5},{8,10},{10,8},{9,1... | collective-permute-start | bytes 24584 | tf_op jit(solution)/shard_map/ppermute | solution.py:53
  28.8 2.5 %collective-permute-start.9 = (f32[16,128]{1,0:T(8,128)S(1)}, f32[16,128]{1,0:T(8,128)S(1)}, u32[]{:S(2)}, u32[]{:S(2)}) collective-permute-start(f32[16,128]{1,0:T(8,128)S(1)} %collect.1), channel_id=1, source_target_pairs={{0,1},{1,0},{2,3},{3,2},{4,5},{5,4},{6,7},{7,6},{8,9},{9,8},{10,11... | collective-permute-start | bytes 24584 | tf_op jit(solution)/shard_map/ppermute | solution.py:53
  31.3 10.5 %copy-start.4 = (f32[24,256]{1,0:T(8,128)S(1)}, f32[24,256]{1,0:T(8,128)}, u32[]{:S(2)}) copy-start(f32[24,256]{1,0:T(8,128)} %column.3) | copy-start | bytes 73732
  31.3 5.3 %collective-permute-start.12 = (f32[16,128]{1,0:T(8,128)S(1)}, f32[16,128]{1,0:T(8,128)S(1)}, u32[]{:S(2)}, u32[]{:S(2)}) collective-permute-start(f32[16,128]{1,0:T(8,128)S(1)} %add_add_fusion), channel_id=1, source_target_pairs={{0,4},{4,0},{8,12},{12,8},{1,5},{5,1},{9,13},{13,9},{2,6},{6,2},{1... | collective-permute-start | bytes 24584 | tf_op jit(solution)/shard_map/ppermute | solution.py:53
  36.6 5.1 %collective-permute-start.13 = (f32[16,128]{1,0:T(8,128)S(1)}, f32[16,128]{1,0:T(8,128)S(1)}, u32[]{:S(2)}, u32[]{:S(2)}) collective-permute-start(f32[16,128]{1,0:T(8,128)S(1)} %add.29), channel_id=1, source_target_pairs={{0,8},{4,12},{8,0},{12,4},{1,9},{5,13},{9,1},{13,5},{2,10},{6,14},... | collective-permute-start | bytes 24584 | tf_op jit(solution)/shard_map/ppermute | solution.py:53

commit v3 on v1

v3 whole, which is shorter than its diff:
```python
import functools

import jax
import jax.numpy as jnp
from jax import lax
from jax.experimental import pallas as pl
from jax.experimental.pallas import tpu as pltpu
from jax.sharding import PartitionSpec as P

weight_vert = 2.0
weight_cross = 0.3
gain_bound = 1.6
total_weight = 10.4
diag_shift = 0.5
source_scale = 8.0

LANES = 128
GRANT = 8 << 20


def line_pairs(count, first):
    pairs = []
    for low in range(first, count - 1, 2):
        pairs += [(low, low + 1), (low + 1, low)]
    return pairs


def exchanged(for_pairs, for_others, axis):
    count = lax.axis_size(axis)
    if count == 1:
        return jnp.zeros_like(for_pairs), jnp.zeros_like(for_others)
    first = lax.ppermute(for_pairs, axis, line_pairs(count, 0))
    if count == 2:
        return first, jnp.zeros_like(first)
    return first, lax.ppermute(for_others, axis, line_pairs(count, 1))


def flipped(values, sizes, axes, bits):
    shape = [sizes[axis] for axis in axes]
    pairs = []
    for flat in range(functools.reduce(lambda a, b: a * b, shape, 1)):
        place, rest = [], flat
        for size in reversed(shape):
            place.insert(0, rest % size)
            rest //= size
        target = 0
        for where, size, bit in zip(place, shape, bits):
            target = target * size + (where ^ bit)
        pairs.append((flat, target))
    return lax.ppermute(values, axes, pairs)


def total(values):
    sizes = {axis: lax.axis_size(axis) for axis in ("layer", "col", "tile")}
    assert all(size & (size - 1) == 0 for size in sizes.values())
    first = 1
    if sizes["col"] > 1 and sizes["layer"] == 2:
        values = (
            values
            + flipped(values, sizes, ("layer",), (1,))
            + flipped(values, sizes, ("col",), (1,))
            + flipped(values, sizes, ("col", "layer"), (1, 1))
        )
        first = 2
    else:
        values = values + flipped(values, sizes, ("layer",), (1,))
    for axis, bit in (("col", first), ("tile", 1)):
        while bit < sizes[axis]:
            values = values + flipped(values, sizes, (axis,), (bit,))
            bit *= 2
    return values


def tiles_of(plane):
    return [plane[:, at : at + LANES] for at in range(0, plane.shape[1], LANES)]


def iota(shape, axis):
    return lax.broadcasted_iota(jnp.int32, shape, axis)


def turned(values, by, axis):
    by %= values.shape[axis]
    return pltpu.roll(values, by, axis) if by else values


def sides(tiles, low_col, high_col):
    rows, lanes = tiles[0].shape
    row, lane = iota((rows, lanes), 0), iota((rows, lanes), 1)
    ahead = [turned(tile, -1, 1) for tile in tiles] + [0.0 if high_col is None else high_col]
    behind = [0.0 if low_col is None else low_col] + [turned(tile, 1, 1) for tile in tiles]
    out = []
    for i, tile in enumerate(tiles):
        below = jnp.where(row == rows - 1, 0.0, turned(tile, -1, 0))
        above = jnp.where(row == 0, 0.0, turned(tile, 1, 0))
        right = jnp.where(lane == lanes - 1, ahead[i + 1], ahead[i])
        left = jnp.where(lane == 0, behind[i], behind[i + 1])
        out.append((below + above) + (right + left))
    return out


def levels(tiles, side):
    return [weight_vert * tile + weight_cross * s for tile, s in zip(tiles, side)]


def gains(metric):
    scale = metric / (gain_bound * total_weight * metric + diag_shift)
    return metric * scale, scale


def folded(values):
    return functools.reduce(lambda a, b: a + b, [values[at : at + 8] for at in range(0, values.shape[0], 8)])


def dot(left, right):
    return functools.reduce(lambda a, b: a + b, [folded(a * b) for a, b in zip(left, right)])


def keep_rows(k, tiles, low, high, count):
    rows = tiles[0].shape[0]
    for i, tile in enumerate(tiles):
        if low is not None:
            low[pl.ds(i * count + k, 1), :] = tile[0:1]
        if high is not None:
            high[pl.ds(i * count + k, 1), :] = tile[rows - 1 : rows]


def multiplier_of(error, which):
    return 1.0 + 0.002 * error[which].astype(jnp.float32)


def weighted_kernel(own, *refs):
    source, profile, column, error = refs[:4]
    weighted, gain, strip_low, strip_high, cols_low, cols_high, prof, sums = refs[-8:]
    layer = lax.axis_index("layer")
    half, rows, width = source.shape[1:]
    count, tiles = 2 * half, width // LANES
    base = layer * half if own else (1 - layer) * half
    columns = column[...] * multiplier_of(error, layer)
    lane = iota((rows, LANES), 1)

    def step(at, carry):
        first, second, last, acc = carry
        k = base + at
        g, _ = gains(profile[at] * columns)
        forcing = source_scale * source[layer, at]
        u = g * forcing
        weighted[k] = u
        gain[k] = g
        parts = tiles_of(u)
        keep_rows(k, parts, strip_low, strip_high, count)
        for i, part in enumerate(parts):
            strip_low[pl.ds((tiles + i) * count + k, 1), :] = part[1:2]
        prof[pl.ds(k, 1), :] = jnp.full((1, LANES), profile[at])
        first = jnp.where(lane == k, pltpu.roll(parts[0], k, 1), first)
        second = jnp.where(lane == k, pltpu.roll(parts[0], lax.rem(k + LANES - 1, LANES), 1), second)
        last = jnp.where(lane == k, pltpu.roll(parts[-1], k + 1, 1), last)
        return first, second, last, acc + dot(parts, tiles_of(forcing))

    if own:
        zeros = jnp.zeros((rows, LANES), jnp.float32)
        edge = tiles_of(columns)
        carry = (jnp.where(lane == LANES - 1, turned(edge[0], -1, 1), 0.0), zeros, zeros, jnp.zeros((8, LANES), jnp.float32))
        for i, tile in enumerate(edge):
            strip_low[2 * tiles * count + 2 + i : 2 * tiles * count + 3 + i, :] = tile[0:1]
    else:
        low, high, acc = refs[8], refs[9], refs[11]
        carry = (low[0:rows], low[rows:], high[0:rows], acc[...])
    first, second, last, acc = lax.fori_loop(0, half, step, carry, unroll=4)
    cols_low[0:rows] = first
    cols_low[rows:] = second
    cols_high[0:rows] = last
    cols_high[rows:] = jnp.zeros_like(last)
    sums[...] = acc


def join_kernel(nr, strip_low, strip_high, pair_cols, other_cols, for_pairs, for_others):
    rows = pair_cols.shape[0] // 2
    first, second = pair_cols[...], other_cols[...]
    even = lax.axis_index("col") % 2 == 0
    low_cols, high_cols = jnp.where(even, second, first), jnp.where(even, first, second)
    at = iota(strip_low.shape, 0)
    low, high = strip_low[...], strip_high[...]
    low = jnp.where(at == 2 * nr, low_cols[0:1], jnp.where(at == 2 * nr + 1, high_cols[0:1], low))
    high = jnp.where(at == 2 * nr + 1, high_cols[rows - 1 : rows], high)
    even = lax.axis_index("tile") % 2 == 0
    for_pairs[...] = jnp.where(even, high, low)
    for_others[...] = jnp.where(even, low, high)


def inner_kernel(weighted, gain, pair_cols, other_cols, image, q_low, q_high, g_low, g_high, k_low, k_high, pack, sums, again):
    count, rows, width = weighted.shape
    even = lax.axis_index("col") % 2 == 0
    first, second = pair_cols[0:rows], other_cols[0:rows]
    pack_low, pack_high = jnp.where(even, second, first), jnp.where(even, first, second)
    lane = iota((rows, LANES), 1)
    zero = [jnp.zeros((rows, LANES), jnp.float32) for _ in range(width // LANES)]
    one = jnp.zeros((8, LANES), jnp.float32)

    def applied(read, columns, emit, carry):
        def step(k, state):
            side_before, level_twice, level_before, carry = state
            tiles = tiles_of(read[k])
            side = sides(tiles, *columns(k))
            level = levels(tiles, side)
            found = [s + a + b for s, a, b in zip(side_before, level_twice, level)]
            return side, level_before, level, emit(k - 1, found, carry)

        tiles = tiles_of(read[0])
        side = sides(tiles, *columns(0))
        state = (side, zero, levels(tiles, side), carry)
        side, level_twice, _, carry = lax.fori_loop(1, count, step, state, unroll=3)
        return emit(count - 1, [s + a for s, a in zip(side, level_twice)], carry)

    def outside(k):
        return pltpu.roll(pack_low, lax.rem(LANES - k, LANES), 1), pltpu.roll(pack_high, LANES - 1 - k, 1)

    def first_image(k, found, carry):
        packed, zb, bb = carry
        u, g = tiles_of(weighted[k]), tiles_of(gain[k])
        ub = [a * b for a, b in zip(g, found)]
        for i, (q, v) in enumerate(zip(found, ub)):
            image[k, :, i * LANES : (i + 1) * LANES] = q
            again[k, :, i * LANES : (i + 1) * LANES] = v
        keep_rows(k, found, q_low, q_high, count)
        keep_rows(k, g, g_low, g_high, count)
        packed = jnp.where(lane == k, pltpu.roll(ub[-1], k + 1, 1), packed)
        return packed, zb + dot(u, found), bb + dot(ub, found)

    packed, zb, bb = applied(weighted, outside, first_image, (zero[0], one, one))
    pack[...] = packed

    def second_image(k, found, bbb):
        keep_rows(k, found, k_low, k_high, count)
        return bbb + dot(tiles_of(again[k]), found)

    bbb = applied(again, lambda k: (None, None), second_image, one)
    sums[0], sums[1], sums[2] = zb, bb, bbb


def shifts(values, axis):
    size = values.shape[axis]
    place = iota(values.shape, axis)
    up = jnp.where(place == size - 1, 0.0, turned(values, -1, axis))
    down = jnp.where(place == 0, 0.0, turned(values, 1, axis))
    return up + down


def near(values, axis):
    return values + weight_cross * shifts(values, axis)


def along(tiles, left, right):
    lane = iota(tiles[0].shape, 1)
    ahead = [turned(tile, -1, 1) for tile in tiles] + [right]
    behind = [left] + [turned(tile, 1, 1) for tile in tiles]
    return [
        jnp.where(lane == LANES - 1, ahead[i + 1], ahead[i]) + jnp.where(lane == 0, behind[i], behind[i + 1])
        for i in range(len(tiles))
    ]


def finish_kernel(
    pair_strip,
    other_strip,
    strip_low,
    strip_high,
    q_low,
    q_high,
    g_low,
    g_high,
    k_low,
    k_high,
    pack,
    cols_high,
    pair_cols,
    other_cols,
    prof,
    sum_zz,
    sum_rest,
    out,
    add_low,
    add_high,
):
    count = prof.shape[0]
    nr = q_low.shape[0]
    tiles = nr // count
    rows = pack.shape[0]
    even = lax.axis_index("tile") % 2 == 0
    first, second = pair_strip[...], other_strip[...]
    low, high = jnp.where(even, second, first), jnp.where(even, first, second)
    even = lax.axis_index("col") % 2 == 0
    high_cols = jnp.where(even, pair_cols[...], other_cols[...])

    def blocks(values, start=0):
        return [values[start + i * count : start + (i + 1) * count] for i in range(tiles)]

    shape = (count, LANES)
    diagonal = iota(shape, 0) == iota(shape, 1)

    def to_column(line):
        return jnp.sum(jnp.where(diagonal, line, 0.0), axis=1, keepdims=True)

    def to_line(column):
        return jnp.sum(jnp.where(diagonal, column, 0.0), axis=0, keepdims=True)

    def total(left, right):
        return dot(left, right)

    zb, bb, bbb = sum_rest[0], sum_rest[1], sum_rest[2]
    outer = []
    for halo, u, q, g, ka, add in (
        (low, strip_low, q_low, g_low, k_low, add_low),
        (high, strip_high, q_high, g_high, k_high, add_high),
    ):
        h = [near(block, 0) for block in blocks(halo)]
        for i, block in enumerate(h):
            add[i * count : (i + 1) * count, :] = block
        u, q, g, ka = blocks(u[...]), blocks(q[...]), blocks(g[...]), blocks(ka[...])
        e = [a * b for a, b in zip(g, h)]
        side = along(e, 0.0, 0.0)
        ke = [s + shifts(weight_vert * a + weight_cross * s, 0) for a, s in zip(e, side)]
        zb = zb + total(u, h)
        bb = bb + total(e, [2.0 * a + b for a, b in zip(q, h)])
        bbb = bbb + total(e, [2.0 * a + b for a, b in zip(ka, ke)])
        outer.append((u, e, [a * b + c for a, b, c in zip(g, q, e)]))
    (_, e_low, _), (u_last, e_high, ub_last) = outer

    u_next, u_after = blocks(high), blocks(high, nr)
    side = along(u_next, to_column(high[2 * nr : 2 * nr + 1]), to_column(high[2 * nr + 1 : 2 * nr + 2]))
    side = [s + a + b for s, a, b in zip(side, u_last, u_after)]
    q_next = [s + shifts(weight_vert * a + weight_cross * s, 0) for a, s in zip(u_next, side)]
    level = prof[...]
    for i in range(tiles):
        g, _ = gains(level * high[2 * nr + 2 + i : 2 * nr + 3 + i])
        bbb = bbb + 2.0 * folded(ub_last[i] * near(g * q_next[i], 0))

    lane, row = iota((rows, LANES), 1), iota((rows, LANES), 0)
    held = lane < count
    u_next = jnp.where(held, high_cols[0:rows], 0.0)
    up = jnp.where(row == 0, jnp.where(held, low[2 * nr + 1 : 2 * nr + 2], 0.0), turned(u_next, 1, 0))
    down = jnp.where(row == rows - 1, jnp.where(held, high[2 * nr + 1 : 2 * nr + 2], 0.0), turned(u_next, -1, 0))
    side = cols_high[0:rows] + high_cols[rows:] + up + down
    q_next = side + shifts(weight_vert * u_next + weight_cross * side, 1)
    g, _ = gains(to_line(level) * high_cols[0:rows, LANES - 1 :])
    ub = pack[...]
    ub = ub + jnp.where(row == 0, to_line(e_low[-1][:, LANES - 1 :]), 0.0)
    ub = ub + jnp.where(row == rows - 1, to_line(e_high[-1][:, LANES - 1 :]), 0.0)
    bbb = bbb + 2.0 * folded(ub * near(g * q_next, 1))

    layer = lax.axis_index("layer")
    out[...] = jnp.zeros_like(out)
    for i, values in enumerate((sum_zz[...], zb, bb, bbb)):
        out[pl.ds(8 * layer + i, 1), :] = jnp.sum(values, axis=0, keepdims=True)


def ready_kernel(source, profile_own, profile_other, column, error, image, add_low, add_high, base, kept, sent):
    layer = lax.axis_index("layer")
    half, rows, width = source.shape[1:]
    count = 2 * half
    mine = column[...] * multiplier_of(error, layer)
    theirs = column[...] * multiplier_of(error, 1 - layer)
    row = iota((rows, LANES), 0)

    def store(ref, where, scale, k):
        scale, plane = tiles_of(scale), tiles_of(image[k])
        for i, q in enumerate(plane):
            q = q + jnp.where(row == 0, add_low[pl.ds(i * count + k, 1), :], 0.0)
            q = q + jnp.where(row == rows - 1, add_high[pl.ds(i * count + k, 1), :], 0.0)
            ref[where, :, i * LANES : (i + 1) * LANES] = scale[i] * q

    def step(at, _):
        _, scale = gains(profile_other[at] * mine)
        store(sent, at, scale, (1 - layer) * half + at)
        _, scale = gains(profile_own[at] * mine)
        store(kept, at, scale, layer * half + at)
        base[layer, at] = scale * (source_scale * source[layer, at])
        _, scale = gains(profile_own[at] * theirs)
        base[1 - layer, at] = scale * (source_scale * source[1 - layer, at])
        return 0

    lax.fori_loop(0, half, step, 0, unroll=2)


def final_kernel(base, kept, received, sums, out, factors):
    layer = lax.axis_index("layer")
    which, at = pl.program_id(0), pl.program_id(1)
    size, rows, width = out.shape[1:]

    @pl.when((which == 0) & (at == 0))
    def _():
        for each in range(2):
            values = jnp.sum(sums[8 * each : 8 * each + 8], axis=1, keepdims=True)
            zz, zb, bb, bbb = (values[i : i + 1] for i in range(4))
            delta = zz - zb
            alpha = zz / delta
            rest = -zb / delta
            beta = (zz * bb - zb * zb) / (delta * delta)
            gamma = zz * beta
            delta_next = gamma - (rest * rest * zb + 2.0 * alpha * rest * bb + alpha * alpha * bbb)
            alpha_next = gamma / (delta_next - beta * gamma / alpha)
            factors[each, 0] = jnp.broadcast_to(alpha + alpha_next * (rest + beta), (8, LANES))
            factors[each, 1] = jnp.broadcast_to(alpha_next * alpha, (8, LANES))

    first = jnp.broadcast_to(factors[which, 0][0:1, 0:1], (rows, width))
    second = jnp.broadcast_to(factors[which, 1][0:1, 0:1], (rows, width))

    def fill(image):
        for i in range(size):
            k = at * size + i
            out[0, i] = first * base[which, k] + second * image[k]

    @pl.when(which == layer)
    def _():
        fill(kept)

    @pl.when(which != layer)
    def _():
        fill(received)


VMEM = pl.BlockSpec(memory_space=pltpu.VMEM)
SMEM = pl.BlockSpec(memory_space=pltpu.SMEM)


def call(kernel, out_shape, args, name, scalars=(), scratch=(), aliases=None, cost=0):
    return pl.pallas_call(
        kernel,
        out_shape=[jax.ShapeDtypeStruct(shape, jnp.float32) for shape in out_shape],
        in_specs=[SMEM if i in scalars else VMEM for i in range(len(args))],
        out_specs=[VMEM] * len(out_shape),
        scratch_shapes=[pltpu.VMEM(shape, jnp.float32) for shape in scratch],
        input_output_aliases=aliases or {},
        compiler_params=pltpu.CompilerParams(vmem_limit_bytes=GRANT),
        cost_estimate=pl.CostEstimate(flops=cost, bytes_accessed=cost, transcendentals=0) if cost else None,
        name=name,
    )(*args)


def local(source, profile, column, terrain_height_error):
    copies, half, rows, width = source.shape
    count, tiles = 2 * half, width // LANES
    assert lax.axis_size("layer") == copies == 2 and count < LANES and width % LANES == 0
    assert count % 8 == 0 and rows % 8 == 0 and rows > 2
    swap = [(0, 1), (1, 0)]
    other = lax.ppermute(source, "layer", swap)
    profile_other = lax.ppermute(profile, "layer", swap)
    nr = tiles * count
    block, row, pack = (count, rows, width), (nr, LANES), (rows, LANES)
    strip = (-(-(2 * nr + 2 + tiles) // 8) * 8, LANES)
    shapes = [block, block, strip, strip, (2 * rows, LANES), (2 * rows, LANES), (count, LANES), (8, LANES)]
    begun = call(
        functools.partial(weighted_kernel, True),
        shapes,
        (source, profile, column, terrain_height_error),
        "weighted_own",
        (1,),
    )
    weighted, gain, strip_low, strip_high, cols_low, cols_high, prof, sum_zz = call(
        functools.partial(weighted_kernel, False),
        shapes,
        (other, profile_other, column, terrain_height_error, *begun),
        "weighted_other",
        (1,),
        aliases={4 + i: i for i in range(8)},
    )
    even = lax.axis_index("col") % 2 == 0
    pair_cols, other_cols = exchanged(
        jnp.where(even, cols_high, cols_low), jnp.where(even, cols_low, cols_high), "col"
    )
    for_pairs, for_others = call(
        functools.partial(join_kernel, nr), [strip, strip], (strip_low, strip_high, pair_cols, other_cols), "join"
    )
    pair_strip, other_strip = exchanged(for_pairs, for_others, "tile")
    image, q_low, q_high, g_low, g_high, k_low, k_high, packed, sum_rest = call(
        inner_kernel,
        [block, row, row, row, row, row, row, pack, (3, 8, LANES)],
        (weighted, gain, pair_cols, other_cols),
        "inner",
        scratch=(block,),
    )
    sums, add_low, add_high = call(
        finish_kernel,
        [(16, LANES), row, row],
        (
            pair_strip,
            other_strip,
            strip_low,
            strip_high,
            q_low,
            q_high,
            g_low,
            g_high,
            k_low,
            k_high,
            packed,
            cols_high,
            pair_cols,
            other_cols,
            prof,
            sum_zz,
            sum_rest,
        ),
        "finish",
    )
    part = (half, rows, width)
    base, kept, sent = call(
        ready_kernel,
        [source.shape, part, part],
        (source, profile, profile_other, column, terrain_height_error, image, add_low, add_high),
        "ready",
        (1, 2),
    )
    received = lax.ppermute(sent, "layer", swap)
    sums = total(sums)
    size = half // 2 if half % 2 == 0 else half
    return pl.pallas_call(
        final_kernel,
        out_shape=jax.ShapeDtypeStruct(source.shape, jnp.float32),
        grid=(2, half // size),
        in_specs=[VMEM] * 4,
        out_specs=pl.BlockSpec((1, size, rows, width), lambda i, j: (i, j, 0, 0)),
        scratch_shapes=[pltpu.VMEM((2, 2, 8, LANES), jnp.float32)],
        compiler_params=pltpu.CompilerParams(vmem_limit_bytes=GRANT),
        name="final",
    )(base, kept, received, sums)


def solution(mesh):
    placed = (
        P("group", "layer", "tile", "col"),
        P("layer"),
        P(("group", "tile"), "col"),
        P("group", "tile", "col"),
    )
    return jax.shard_map(
        local,
        mesh=mesh,
        in_specs=placed,
        out_specs=P("group", "layer", "tile", "col"),
        check_vma=False,
    )
```

time: 239 us -> 37.4 us (0.16)
  other arithmetic: 146 us -> 0.02 us
  local copies, waits for them, and re-layouts: 59.9 us -> 3.19 us
  Pallas kernels: 0 us -> 9.55 us
  waiting for transfers between devices: 17 us -> 9.26 us
    add x6 -> x3, other arithmetic: 63.7 us -> 0.01 us  [the longest x2 0.01 us: total(): values = values + flipped(values, sizes, (axis,), (bit,))]
    select_n x12 -> x1, other arithmetic: 35.1 us -> 0.01 us  [local(): jnp.where(even, cols_high, cols_low)]
    mul x7 -> x0, other arithmetic: 23.6 us -> none  [the longest x1 10.2 us: local(): again = gain * image]
    select_n x10 -> x0, local copies, waits for them, and re-layouts: 21.4 us -> none  [the longest x4 9.26 us: neighbours(): jnp.where(even, high_edge, low_edge)]
    ppermute x4 -> x0, local copies, waits for them, and re-layouts: 16.6 us -> none  [the longest x2 8.37 us: neighbours(): lax.ppermute(jnp.where(even, high_edge, low_edge), axis, line_pairs(count...]
    reduce_sum x2 -> x0, other arithmetic: 14.5 us -> none  [the longest x1 14.4 us: local(): jnp.sum(weighted * forcing, axis=lanes)]
    mul x2 -> x0, local copies, waits for them, and re-layouts: 10.3 us -> none  [the longest x1 5.32 us: local(): scale * ((alpha + alpha_next * (rest + beta)) * forcing + alpha_next * al...]
    pallas_call x0 -> x7, Pallas kernels: none -> 9.55 us  [the longest x6 7.73 us: call(): pl.pallas_call(kernel, out_shape=[jax.ShapeDtypeStruct(shape, jnp.float32...]
  transfers between devices with their start and end apart: 12 -> 11, of which waited for: 8 -> 5; matrix products, arithmetic and copies ran while one was open for 7% -> 0% of each run, Pallas kernels for 0% -> 14%
where the time goes in v3:
time: 37.4 us; the launch traced here: 37 us
  starting transfers between devices  14.9 us (40%)
  Pallas kernels  9.55 us (26%)
  waiting for transfers between devices  9.26 us (25%)
  local copies, waits for them, and re-layouts  3.19 us (9%)
    ppermute x5, starting transfers between devices, flipped(): return lax.ppermute(values, axes, pairs)  8.44 us
    pallas_call x6, Pallas kernels, call(): pl.pallas_call(kernel, out_shape=[jax.ShapeDtypeStruct(shape, jnp.float32...  7.73 us
    ppermute x5, waiting for transfers between devices, flipped(): return lax.ppermute(values, axes, pairs)  7.44 us
    ppermute x2, starting transfers between devices, exchanged(): first = lax.ppermute(for_pairs, axis, line_pairs(count, 0))  5.16 us
    unnamed x12, local copies, waits for them, and re-layouts  3.19 us
    pallas_call x1, Pallas kernels, local(): pl.pallas_call(final_kernel, out_shape=jax.ShapeDtypeStruct(source.shape,...  1.82 us
    ppermute x2, waiting for transfers between devices, exchanged(): first = lax.ppermute(for_pairs, axis, line_pairs(count, 0))  1.81 us
  transfers between devices with their start and end apart: 11, of which 5 were waited for; matrix products, arithmetic and copies ran while one was open for 0% of the time, Pallas kernels for 14%

profile of v3, /device:TPU:0, one launch (start us, length us, event | category | flops | bytes accessed | tf_op | source)
XLA Modules:
  0.0 37.0 jit_solution(11820798196532723930)
XLA Ops:
  0.0 0.0 copy-start.4
  0.0 0.5 %collective-permute-start.1 = (f32[2,20,24,256]{3,2,1,0:T(8,128)}, f32[2,20,24,256]{3,2,1,0:T(8,128)S(1)}, u32[]{:S(2)}, u32[]{:S(2)}) collective-permute-start(f32[2,20,24,256]{3,2,1,0:T(8,128)} %source.1), channel_id=1, source_target_pairs={{0,1},{1,0},{2,3},{3,2},{4,5},{5,4},{6,7},{7,6},{8,9},{9,8},{10,11... | collective-permute-start | bytes 2949128 | tf_op jit(solution)/shard_map/ppermute | solution.py:446
  0.5 0.1 collective-permute-start
  0.6 0.0 copy-start.5
  0.6 0.2 copy-done.4
  0.7 0.5 %copy-done.5 = f32[20]{0:T(128)S(1)} copy-done((f32[20]{0:T(128)S(1)}, f32[20]{0:T(128)}, u32[]{:S(2)}) %copy-start.5) | copy-done | bytes 104
  1.2 0.0 copy-start
  1.2 1.2 %copy-done = f32[2,20,24,256]{3,2,1,0:T(8,128)S(1)} copy-done((f32[2,20,24,256]{3,2,1,0:T(8,128)S(1)}, f32[2,20,24,256]{3,2,1,0:T(8,128)}, u32[]{:S(2)}) %copy-start) | copy-done | bytes 983064
  2.4 0.0 copy-start.2
  2.4 0.8 %copy-done.2 = s32[2,24,256]{2,1,0:T(8,128)S(1)} copy-done((s32[2,24,256]{2,1,0:T(8,128)S(1)}, s32[2,24,256]{2,1,0:T(8,128)}, u32[]{:S(2)}) %copy-start.2) | copy-done | bytes 49176
  3.2 1.2 %weighted_own.1 = (f32[40,24,256]{2,1,0:T(8,128)S(1)}, f32[40,24,256]{2,1,0:T(8,128)S(1)}, f32[168,128]{1,0:T(8,128)S(1)}, f32[168,128]{1,0:T(8,128)S(1)}, f32[4...) custom-call(f32[2,20,24,256]{3,2,1,0:T(8,128)S(1)} %copy-done, ...), custom_call_target="tpu_custom_call" | custom-call | tf_op jit(solution)/shard_map/weighted_own/pallas_call | solution.py:427
  4.4 0.0 collective-permute-done.refs_1_.profile_other
  4.5 0.0 collective-permute-done.1.refs_0_
  4.5 1.2 %weighted_other.1 = (f32[40,24,256]{2,1,0:T(8,128)S(1)}, f32[40,24,256]{2,1,0:T(8,128)S(1)}, f32[168,128]{1,0:T(8,128)S(1)}, f32[168,128]{1,0:T(8,128)S(1)}, f32...) custom-call(f32[2,20,24,256]{3,2,1,0:T(8,128)S(1)} %collective-permu, ...), custom_call_target="tpu_custom_call", output_to_operand_aliasing={{0}: (4, {}), {1}: (5, {}), {2}: (6, {}), {3}: (7, {}), {4}... | custom-call | tf_op jit(solution)/shard_map/weighted_other/pallas_call | solution.py:427
  5.7 3.0 %collective-permute-start.2 = (f32[48,128]{1,0:T(8,128)S(1)}, f32[48,128]{1,0:T(8,128)S(1)}, u32[]{:S(2)}, u32[]{:S(2)}) collective-permute-start(f32[48,128]{1,0:T(8,128)S(1)} %broadcast_select_fusion), channel_id=1, source_target_pairs={{0,2},{2,0},{1,3},{3,1},{4,6},{6,4},{5,7},{7,5},{8,10},{10,8},{9,1... | collective-permute-start | bytes 73736 | tf_op jit(solution)/shard_map/ppermute | solution.py:32
  8.6 1.8 %collective-permute-done.2.pair_cols = f32[48,128]{1,0:T(8,128)S(1)} collective-permute-done((f32[48,128]{1,0:T(8,128)S(1)}, f32[48,128]{1,0:T(8,128)S(1)}, u32[]{:S(2)}, u32[]{:S(2)}) %collective-permute-start.2) | collective-permute-done | bytes 24608 | tf_op jit(solution)/shard_map/ppermute | solution.py:32
  10.5 2.2 %collective-permute-start.3 = (f32[168,128]{1,0:T(8,128)S(1)}, f32[168,128]{1,0:T(8,128)S(1)}, u32[]{:S(2)}, u32[]{:S(2)}) collective-permute-start(f32[168,128]{1,0:T(8,128)S(1)} %get-tuple-element.53), channel_id=1, source_target_pairs={{0,4},{4,0},{8,12},{12,8},{1,5},{5,1},{9,13},{13,9},{2,6},{6,2},{1... | collective-permute-start | bytes 258056 | tf_op jit(solution)/shard_map/ppermute | solution.py:32
  12.7 0.7 %collective-permute-start.4 = (f32[168,128]{1,0:T(8,128)S(1)}, f32[168,128]{1,0:T(8,128)S(1)}, u32[]{:S(2)}, u32[]{:S(2)}) collective-permute-start(f32[168,128]{1,0:T(8,128)S(1)} %get-tuple-element.54), channel_id=1, source_target_pairs={{4,8},{8,4},{5,9},{9,5},{6,10},{10,6},{7,11},{11,7},{20,24},{24,20... | collective-permute-start | bytes 258056 | tf_op jit(solution)/shard_map/ppermute | solution.py:35
  13.3 0.0 copy-start.1
  13.3 4.0 %inner.1 = (f32[40,24,256]{2,1,0:T(8,128)S(1)}, f32[80,128]{1,0:T(8,128)S(1)}, f32[80,128]{1,0:T(8,128)S(1)}, f32[80,128]{1,0:T(8,128)S(1)}, f32[80,128]{1,0:T(8...) custom-call(f32[40,24,256]{2,1,0:T(8,128)S(1)} %get-tuple-element.46, ...), custom_call_target="tpu_custom_call" | custom-call | tf_op jit(solution)/shard_map/inner/pallas_call | solution.py:427
  17.4 0.0 collective-permute-done.3.pair_strip
  17.4 0.0 collective-permute-done.4.other_strip
  17.4 0.0 copy-start.3
  17.4 0.3 finish.1
  17.6 0.0 copy-done.1
  17.7 0.5 %copy-done.3 = s32[2,24,256]{2,1,0:T(8,128)S(1)} copy-done((s32[2,24,256]{2,1,0:T(8,128)S(1)}, s32[2,24,256]{2,1,0:T(8,128)}, u32[]{:S(2)}) %copy-start.3) | copy-done | bytes 49176
  18.2 1.0 %ready.1 = (f32[2,20,24,256]{3,2,1,0:T(8,128)S(1)}, f32[20,24,256]{2,1,0:T(8,128)S(1)}, f32[20,24,256]{2,1,0:T(8,128)S(1)}) custom-call(f32[2,20,24,256]{3,2,1,0:T(8,128)S(1)} %copy-done.1, f32[20]{0:T(128)S(1)} %copy-done.5, f32[20]{0:T(128)S(1)} %collective-permute-done.refs_1_.profile_other, f32[24,256]{1,0:T(8,128)S(1)} %copy-done.4, ...), custom_call_target="tpu_custom_call" | custom-call | tf_op jit(solution)/shard_map/ready/pallas_call | solution.py:427
  19.2 0.1 collective-permute-start.5
  19.3 1.6 %collective-permute-start.8 = (f32[16,128]{1,0:T(8,128)S(1)}, f32[16,128]{1,0:T(8,128)S(1)}, u32[]{:S(2)}, u32[]{:S(2)}) collective-permute-start(f32[16,128]{1,0:T(8,128)S(1)} %get-tuple-element.70), channel_id=1, source_target_pairs={{0,3},{1,2},{2,1},{3,0},{4,7},{5,6},{6,5},{7,4},{8,11},{9,10},{10,... | collective-permute-start | bytes 24584 | tf_op jit(solution)/shard_map/ppermute | solution.py:50
  20.9 0.5 %collective-permute-start.7 = (f32[16,128]{1,0:T(8,128)S(1)}, f32[16,128]{1,0:T(8,128)S(1)}, u32[]{:S(2)}, u32[]{:S(2)}) collective-permute-start(f32[16,128]{1,0:T(8,128)S(1)} %get-tuple-element.70), channel_id=1, source_target_pairs={{0,2},{2,0},{1,3},{3,1},{4,6},{6,4},{5,7},{7,5},{8,10},{10,8},{9,1... | collective-permute-start | bytes 24584 | tf_op jit(solution)/shard_map/ppermute | solution.py:50
  21.4 0.0 collective-permute-start.6
  21.4 1.0 %collective-permute-done.8 = f32[16,128]{1,0:T(8,128)S(1)} collective-permute-done((f32[16,128]{1,0:T(8,128)S(1)}, f32[16,128]{1,0:T(8,128)S(1)}, u32[]{:S(2)}, u32[]{:S(2)}) %collective-permute-start.8) | collective-permute-done | bytes 8224 | tf_op jit(solution)/shard_map/ppermute | solution.py:50
  22.5 2.1 %collective-permute-done.7 = f32[16,128]{1,0:T(8,128)S(1)} collective-permute-done((f32[16,128]{1,0:T(8,128)S(1)}, f32[16,128]{1,0:T(8,128)S(1)}, u32[]{:S(2)}, u32[]{:S(2)}) %collective-permute-start.7) | collective-permute-done | bytes 8224 | tf_op jit(solution)/shard_map/ppermute | solution.py:50
  24.6 0.0 collective-permute-done.6
  24.6 4.5 %collective-permute-start.9 = (f32[16,128]{1,0:T(8,128)S(1)}, f32[16,128]{1,0:T(8,128)S(1)}, u32[]{:S(2)}, u32[]{:S(2)}) collective-permute-start(f32[16,128]{1,0:T(8,128)S(1)} %add_add_fusion), channel_id=1, source_target_pairs={{0,4},{4,0},{8,12},{12,8},{1,5},{5,1},{9,13},{13,9},{2,6},{6,2},{1... | collective-permute-start | bytes 24584 | tf_op jit(solution)/shard_map/ppermute | solution.py:50
  29.0 1.6 %collective-permute-done.9 = f32[16,128]{1,0:T(8,128)S(1)} collective-permute-done((f32[16,128]{1,0:T(8,128)S(1)}, f32[16,128]{1,0:T(8,128)S(1)}, u32[]{:S(2)}, u32[]{:S(2)}) %collective-permute-start.9) | collective-permute-done | bytes 8224 | tf_op jit(solution)/shard_map/ppermute | solution.py:50
  30.7 1.9 %collective-permute-start.10 = (f32[16,128]{1,0:T(8,128)S(1)}, f32[16,128]{1,0:T(8,128)S(1)}, u32[]{:S(2)}, u32[]{:S(2)}) collective-permute-start(f32[16,128]{1,0:T(8,128)S(1)} %add.23), channel_id=1, source_target_pairs={{0,8},{4,12},{8,0},{12,4},{1,9},{5,13},{9,1},{13,5},{2,10},{6,14},... | collective-permute-start | bytes 24584 | tf_op jit(solution)/shard_map/ppermute | solution.py:50
  32.5 2.7 %collective-permute-done.10 = f32[16,128]{1,0:T(8,128)S(1)} collective-permute-done((f32[16,128]{1,0:T(8,128)S(1)}, f32[16,128]{1,0:T(8,128)S(1)}, u32[]{:S(2)}, u32[]{:S(2)}) %collective-permute-start.10) | collective-permute-done | bytes 8224 | tf_op jit(solution)/shard_map/ppermute | solution.py:50
  35.2 0.0 collective-permute-done.5.received
  35.2 1.8 %final.1 = f32[2,20,24,256]{3,2,1,0:T(8,128)} custom-call(f32[2,20,24,256]{3,2,1,0:T(8,128)S(1)} %get-tuple-element.67.base, f32[20,24,256]{2,1,0:T(8,128)S(1)} %get-tuple-element.68.kept, f32[20,24,256]{2,1,0:T(8,128)S(1)} %collective-permute-done.5.received, f32[16,128]{1,0:T(8,128)S(1)} %add.24.sums), custom_call_target="tpu_custom_call" | custom-call | tf_op jit(solution)/shard_map/final/pallas_call | solution.py:517
  (6 shorter events, 0.0 us)
Async XLA Ops:
  0.0 0.7 %copy-start.4 = (f32[24,256]{1,0:T(8,128)S(1)}, f32[24,256]{1,0:T(8,128)}, u32[]{:S(2)}) copy-start(f32[24,256]{1,0:T(8,128)} %column.1) | copy-start | bytes 73732
  0.0 4.5 %collective-permute-start.1 = (f32[2,20,24,256]{3,2,1,0:T(8,128)}, f32[2,20,24,256]{3,2,1,0:T(8,128)S(1)}, u32[]{:S(2)}, u32[]{:S(2)}) collective-permute-start(f32[2,20,24,256]{3,2,1,0:T(8,128)} %source.1), channel_id=1, source_target_pairs={{0,1},{1,0},{2,3},{3,2},{4,5},{5,4},{6,7},{7,6},{8,9},{9,8},{10,11... | collective-permute-start | bytes 2949128 | tf_op jit(solution)/shard_map/ppermute | solution.py:446
  0.5 4.0 %collective-permute-start = (f32[20]{0:T(128)}, f32[20]{0:T(128)S(1)}, u32[]{:S(2)}, u32[]{:S(2)}) collective-permute-start(f32[20]{0:T(128)} %profile_own.1), channel_id=1, source_target_pairs={{0,1},{1,0},{2,3},{3,2},{4,5},{5,4},{6,7},{7,6},{8,9},{9,8},{10,11... | collective-permute-start | bytes 248 | tf_op jit(solution)/shard_map/ppermute | solution.py:447
  0.6 0.7 %copy-start.5 = (f32[20]{0:T(128)S(1)}, f32[20]{0:T(128)}, u32[]{:S(2)}) copy-start(f32[20]{0:T(128)} %profile_own.1) | copy-start | bytes 244
  1.2 1.2 %copy-start = (f32[2,20,24,256]{3,2,1,0:T(8,128)S(1)}, f32[2,20,24,256]{3,2,1,0:T(8,128)}, u32[]{:S(2)}) copy-start(f32[2,20,24,256]{3,2,1,0:T(8,128)} %source.1) | copy-start | bytes 2949124
  2.4 0.8 %copy-start.2 = (s32[2,24,256]{2,1,0:T(8,128)S(1)}, s32[2,24,256]{2,1,0:T(8,128)}, u32[]{:S(2)}) copy-start(s32[2,24,256]{2,1,0:T(8,128)} %error.1) | copy-start | bytes 147460
  5.7 4.8 %collective-permute-start.2 = (f32[48,128]{1,0:T(8,128)S(1)}, f32[48,128]{1,0:T(8,128)S(1)}, u32[]{:S(2)}, u32[]{:S(2)}) collective-permute-start(f32[48,128]{1,0:T(8,128)S(1)} %broadcast_select_fusion), channel_id=1, source_target_pairs={{0,2},{2,0},{1,3},{3,1},{4,6},{6,4},{5,7},{7,5},{8,10},{10,8},{9,1... | collective-permute-start | bytes 73736 | tf_op jit(solution)/shard_map/ppermute | solution.py:32
  10.5 6.9 %collective-permute-start.3 = (f32[168,128]{1,0:T(8,128)S(1)}, f32[168,128]{1,0:T(8,128)S(1)}, u32[]{:S(2)}, u32[]{:S(2)}) collective-permute-start(f32[168,128]{1,0:T(8,128)S(1)} %get-tuple-element.53), channel_id=1, source_target_pairs={{0,4},{4,0},{8,12},{12,8},{1,5},{5,1},{9,13},{13,9},{2,6},{6,2},{1... | collective-permute-start | bytes 258056 | tf_op jit(solution)/shard_map/ppermute | solution.py:32
  12.7 4.7 %collective-permute-start.4 = (f32[168,128]{1,0:T(8,128)S(1)}, f32[168,128]{1,0:T(8,128)S(1)}, u32[]{:S(2)}, u32[]{:S(2)}) collective-permute-start(f32[168,128]{1,0:T(8,128)S(1)} %get-tuple-element.54), channel_id=1, source_target_pairs={{4,8},{8,4},{5,9},{9,5},{6,10},{10,6},{7,11},{11,7},{20,24},{24,20... | collective-permute-start | bytes 258056 | tf_op jit(solution)/shard_map/ppermute | solution.py:35
  13.3 4.3 %copy-start.1 = (f32[2,20,24,256]{3,2,1,0:T(8,128)S(1)}, f32[2,20,24,256]{3,2,1,0:T(8,128)}, u32[]{:S(2)}) copy-start(f32[2,20,24,256]{3,2,1,0:T(8,128)} %source.1) | copy-start | bytes 2949124
  17.4 0.8 %copy-start.3 = (s32[2,24,256]{2,1,0:T(8,128)S(1)}, s32[2,24,256]{2,1,0:T(8,128)}, u32[]{:S(2)}) copy-start(s32[2,24,256]{2,1,0:T(8,128)} %error.1) | copy-start | bytes 147460
  19.2 16.0 %collective-permute-start.5 = (f32[20,24,256]{2,1,0:T(8,128)S(1)}, f32[20,24,256]{2,1,0:T(8,128)S(1)}, u32[]{:S(2)}, u32[]{:S(2)}) collective-permute-start(f32[20,24,256]{2,1,0:T(8,128)S(1)} %get-tuple-element.69), channel_id=1, source_target_pairs={{0,1},{1,0},{2,3},{3,2},{4,5},{5,4},{6,7},{7,6},{8,9},{9,8},{10,11... | collective-permute-start | bytes 1474568 | tf_op jit(solution)/shard_map/ppermute | solution.py:514
  19.3 3.1 %collective-permute-start.8 = (f32[16,128]{1,0:T(8,128)S(1)}, f32[16,128]{1,0:T(8,128)S(1)}, u32[]{:S(2)}, u32[]{:S(2)}) collective-permute-start(f32[16,128]{1,0:T(8,128)S(1)} %get-tuple-element.70), channel_id=1, source_target_pairs={{0,3},{1,2},{2,1},{3,0},{4,7},{5,6},{6,5},{7,4},{8,11},{9,10},{10,... | collective-permute-start | bytes 24584 | tf_op jit(solution)/shard_map/ppermute | solution.py:50
  20.9 3.7 %collective-permute-start.7 = (f32[16,128]{1,0:T(8,128)S(1)}, f32[16,128]{1,0:T(8,128)S(1)}, u32[]{:S(2)}, u32[]{:S(2)}) collective-permute-start(f32[16,128]{1,0:T(8,128)S(1)} %get-tuple-element.70), channel_id=1, source_target_pairs={{0,2},{2,0},{1,3},{3,1},{4,6},{6,4},{5,7},{7,5},{8,10},{10,8},{9,1... | collective-permute-start | bytes 24584 | tf_op jit(solution)/shard_map/ppermute | solution.py:50
  21.4 3.1 %collective-permute-start.6 = (f32[16,128]{1,0:T(8,128)S(1)}, f32[16,128]{1,0:T(8,128)S(1)}, u32[]{:S(2)}, u32[]{:S(2)}) collective-permute-start(f32[16,128]{1,0:T(8,128)S(1)} %get-tuple-element.70), channel_id=1, source_target_pairs={{0,1},{1,0},{2,3},{3,2},{4,5},{5,4},{6,7},{7,6},{8,9},{9,8},{10,11... | collective-permute-start | bytes 24584 | tf_op jit(solution)/shard_map/ppermute | solution.py:50
  24.6 6.1 %collective-permute-start.9 = (f32[16,128]{1,0:T(8,128)S(1)}, f32[16,128]{1,0:T(8,128)S(1)}, u32[]{:S(2)}, u32[]{:S(2)}) collective-permute-start(f32[16,128]{1,0:T(8,128)S(1)} %add_add_fusion), channel_id=1, source_target_pairs={{0,4},{4,0},{8,12},{12,8},{1,5},{5,1},{9,13},{13,9},{2,6},{6,2},{1... | collective-permute-start | bytes 24584 | tf_op jit(solution)/shard_map/ppermute | solution.py:50
  30.7 4.5 %collective-permute-start.10 = (f32[16,128]{1,0:T(8,128)S(1)}, f32[16,128]{1,0:T(8,128)S(1)}, u32[]{:S(2)}, u32[]{:S(2)}) collective-permute-start(f32[16,128]{1,0:T(8,128)S(1)} %add.23), channel_id=1, source_target_pairs={{0,8},{4,12},{8,0},{12,4},{1,9},{5,13},{9,1},{13,5},{2,10},{6,14},... | collective-permute-start | bytes 24584 | tf_op jit(solution)/shard_map/ppermute | solution.py:50

commit v4 on v3

--- a/solution.py
+++ b/solution.py
@@ -6,6 +6,7 @@
 from jax.experimental import pallas as pl
 from jax.experimental.pallas import tpu as pltpu
 from jax.sharding import PartitionSpec as P
+
 
 weight_vert = 2.0
 weight_cross = 0.3
@@ -64,11 +65,15 @@
         first = 2
     else:
         values = values + flipped(values, sizes, ("layer",), (1,))
-    for axis, bit in (("col", first), ("tile", 1)):
-        while bit < sizes[axis]:
-            values = values + flipped(values, sizes, (axis,), (bit,))
-            bit *= 2
-    return values
+
+    def later(values):
+        for axis, bit in (("col", first), ("tile", 1)):
+            while bit < sizes[axis]:
+                values = values + flipped(values, sizes, (axis,), (bit,))
+                bit *= 2
+        return values
+
+    return values, later
 
 
 def tiles_of(plane):
@@ -84,11 +89,11 @@
     return pltpu.roll(values, by, axis) if by else values
 
 
-def sides(tiles, low_col, high_col):
+def sides(tiles):
     rows, lanes = tiles[0].shape
     row, lane = iota((rows, lanes), 0), iota((rows, lanes), 1)
-    ahead = [turned(tile, -1, 1) for tile in tiles] + [0.0 if high_col is None else high_col]
-    behind = [0.0 if low_col is None else low_col] + [turned(tile, 1, 1) for tile in tiles]
+    ahead = [turned(tile, -1, 1) for tile in tiles] + [0.0]
+    behind = [0.0] + [turned(tile, 1, 1) for tile in tiles]
     out = []
     for i, tile in enumerate(tiles):
         below = jnp.where(row == rows - 1, 0.0, turned(tile, -1, 0))
@@ -125,25 +130,17 @@
             high[pl.ds(i * count + k, 1), :] = tile[rows - 1 : rows]
 
 
-def multiplier_of(error, which):
-    return 1.0 + 0.002 * error[which].astype(jnp.float32)
-
-
-def weighted_kernel(own, *refs):
-    source, profile, column, error = refs[:4]
-    weighted, gain, strip_low, strip_high, cols_low, cols_high, prof, sums = refs[-8:]
-    layer = lax.axis_index("layer")
-    half, rows, width = source.shape[1:]
-    count, tiles = 2 * half, width // LANES
-    base = layer * half if own else (1 - layer) * half
-    columns = column[...] * multiplier_of(error, layer)
+def weigh(base, read, profile, columns, carry, refs):
+    weighted, gain, strip_low, strip_high, prof = refs
+    rows, width = columns.shape
+    count, tiles = weighted.shape[0], width // LANES
     lane = iota((rows, LANES), 1)
 
     def step(at, carry):
         first, second, last, acc = carry
         k = base + at
         g, _ = gains(profile[at] * columns)
-        forcing = source_scale * source[layer, at]
+        forcing = source_scale * read(at)
         u = g * forcing
         weighted[k] = u
         gain[k] = g
@@ -157,16 +154,51 @@
         last = jnp.where(lane == k, pltpu.roll(parts[-1], k + 1, 1), last)
         return first, second, last, acc + dot(parts, tiles_of(forcing))
 
-    if own:
-        zeros = jnp.zeros((rows, LANES), jnp.float32)
-        edge = tiles_of(columns)
-        carry = (jnp.where(lane == LANES - 1, turned(edge[0], -1, 1), 0.0), zeros, zeros, jnp.zeros((8, LANES), jnp.float32))
-        for i, tile in enumerate(edge):
-            strip_low[2 * tiles * count + 2 + i : 2 * tiles * count + 3 + i, :] = tile[0:1]
-    else:
-        low, high, acc = refs[8], refs[9], refs[11]
-        carry = (low[0:rows], low[rows:], high[0:rows], acc[...])
-    first, second, last, acc = lax.fori_loop(0, half, step, carry, unroll=4)
+    return lax.fori_loop(0, weighted.shape[0] // 2, step, carry, unroll=5)
+
+
+def own_kernel(
+    source, profile, factors, weighted, gain, strip_low, strip_high, cols_low, cols_high, prof, sums
+):
+    layer = lax.axis_index("layer")
+    half, rows, width = source.shape[1:]
+    count, tiles = 2 * half, width // LANES
+    columns = factors[layer]
+    lane = iota((rows, LANES), 1)
+    zeros = jnp.zeros((rows, LANES), jnp.float32)
+    edge = tiles_of(columns)
+    carry = (jnp.where(lane == LANES - 1, turned(edge[0], -1, 1), 0.0), zeros, zeros, jnp.zeros((8, LANES), jnp.float32))
+    for i, tile in enumerate(edge):
+        strip_low[2 * tiles * count + 2 + i : 2 * tiles * count + 3 + i, :] = tile[0:1]
+    first, second, last, acc = weigh(
+        layer * half,
+        lambda at: source[layer, at],
+        profile,
+        columns,
+        carry,
+        (weighted, gain, strip_low, strip_high, prof),
+    )
+    cols_low[0:rows] = first
+    cols_low[rows:] = second
+    cols_high[0:rows] = last
+    cols_high[rows:] = jnp.zeros_like(last)
+    sums[...] = acc
+
+
+def other_kernel(source, profile, factors, *refs):
+    low, high, acc = refs[4], refs[5], refs[7]
+    weighted, gain, strip_low, strip_high, cols_low, cols_high, prof, sums = refs[8:]
+    layer = lax.axis_index("layer")
+    half, rows = source.shape[1:3]
+    carry = (low[0:rows], low[rows:], high[0:rows], acc[...])
+    first, second, last, acc = weigh(
+        (1 - layer) * half,
+        lambda at: source[layer, at],
+        profile,
+        factors[layer],
+        carry,
+        (weighted, gain, strip_low, strip_high, prof),
+    )
     cols_low[0:rows] = first
     cols_low[rows:] = second
     cols_high[0:rows] = last
@@ -188,56 +220,6 @@
     for_others[...] = jnp.where(even, low, high)
 
 
-def inner_kernel(weighted, gain, pair_cols, other_cols, image, q_low, q_high, g_low, g_high, k_low, k_high, pack, sums, again):
-    count, rows, width = weighted.shape
-    even = lax.axis_index("col") % 2 == 0
-    first, second = pair_cols[0:rows], other_cols[0:rows]
-    pack_low, pack_high = jnp.where(even, second, first), jnp.where(even, first, second)
-    lane = iota((rows, LANES), 1)
-    zero = [jnp.zeros((rows, LANES), jnp.float32) for _ in range(width // LANES)]
-    one = jnp.zeros((8, LANES), jnp.float32)
-
-    def applied(read, columns, emit, carry):
-        def step(k, state):
-            side_before, level_twice, level_before, carry = state
-            tiles = tiles_of(read[k])
-            side = sides(tiles, *columns(k))
-            level = levels(tiles, side)
-            found = [s + a + b for s, a, b in zip(side_before, level_twice, level)]
-            return side, level_before, level, emit(k - 1, found, carry)
-
-        tiles = tiles_of(read[0])
-        side = sides(tiles, *columns(0))
-        state = (side, zero, levels(tiles, side), carry)
-        side, level_twice, _, carry = lax.fori_loop(1, count, step, state, unroll=3)
-        return emit(count - 1, [s + a for s, a in zip(side, level_twice)], carry)
-
-    def outside(k):
-        return pltpu.roll(pack_low, lax.rem(LANES - k, LANES), 1), pltpu.roll(pack_high, LANES - 1 - k, 1)
-
-    def first_image(k, found, carry):
-        packed, zb, bb = carry
-        u, g = tiles_of(weighted[k]), tiles_of(gain[k])
-        ub = [a * b for a, b in zip(g, found)]
-        for i, (q, v) in enumerate(zip(found, ub)):
-            image[k, :, i * LANES : (i + 1) * LANES] = q
-            again[k, :, i * LANES : (i + 1) * LANES] = v
-        keep_rows(k, found, q_low, q_high, count)
-        keep_rows(k, g, g_low, g_high, count)
-        packed = jnp.where(lane == k, pltpu.roll(ub[-1], k + 1, 1), packed)
-        return packed, zb + dot(u, found), bb + dot(ub, found)
-
-    packed, zb, bb = applied(weighted, outside, first_image, (zero[0], one, one))
-    pack[...] = packed
-
-    def second_image(k, found, bbb):
-        keep_rows(k, found, k_low, k_high, count)
-        return bbb + dot(tiles_of(again[k]), found)
-
-    bbb = applied(again, lambda k: (None, None), second_image, one)
-    sums[0], sums[1], sums[2] = zb, bb, bbb
-
-
 def shifts(values, axis):
     size = values.shape[axis]
     place = iota(values.shape, axis)
@@ -248,6 +230,73 @@
 
 def near(values, axis):
     return values + weight_cross * shifts(values, axis)
+
+
+def swept(count, width, rows, plane, emit, carry):
+    zero = [jnp.zeros((rows, LANES), jnp.float32) for _ in range(width // LANES)]
+
+    def step(k, state):
+        side_before, level_twice, level_before, carry = state
+        tiles, carry = plane(k, carry)
+        side = sides(tiles)
+        level = levels(tiles, side)
+        found = [s + a + b for s, a, b in zip(side_before, level_twice, level)]
+        return side, level_before, level, emit(k - 1, found, carry)
+
+    tiles, carry = plane(0, carry)
+    side = sides(tiles)
+    state = (side, zero, levels(tiles, side), carry)
+    side, level_twice, _, carry = lax.fori_loop(1, count, step, state, unroll=13)
+    return emit(count - 1, [s + a for s, a in zip(side, level_twice)], carry)
+
+
+def put(ref, k, tiles):
+    for i, tile in enumerate(tiles):
+        ref[k, :, i * LANES : (i + 1) * LANES] = tile
+
+
+def image_kernel(weighted, gain, image, g_low, g_high):
+    count, rows, width = weighted.shape
+
+    def plane(k, carry):
+        return tiles_of(weighted[k]), carry
+
+    def emit(k, found, carry):
+        put(image, k, found)
+        keep_rows(k, tiles_of(gain[k]), g_low, g_high, count)
+        return carry
+
+    swept(count, width, rows, plane, emit, 0)
+
+
+def inner_kernel(begun, weighted, gain, pair_cols, other_cols, image, q_low, q_high, k_low, k_high, pack, sums, again):
+    count, rows, width = weighted.shape
+    even = lax.axis_index("col") % 2 == 0
+    lane = iota((rows, LANES), 1)
+    first, second = pair_cols[0:rows], other_cols[0:rows]
+    add_low = near(jnp.where((lane < count), jnp.where(even, second, first), 0.0), 1)
+    add_high = near(jnp.where((lane < count), jnp.where(even, first, second), 0.0), 1)
+    one = jnp.zeros((8, LANES), jnp.float32)
+
+    def plane(k, carry):
+        packed, zb, bb, bbb = carry
+        u, g, q = tiles_of(weighted[k]), tiles_of(gain[k]), tiles_of(begun[k])
+        q[0] = q[0] + jnp.where(lane == 0, pltpu.roll(add_low, lax.rem(LANES - k, LANES), 1), 0.0)
+        q[-1] = q[-1] + jnp.where(lane == LANES - 1, pltpu.roll(add_high, LANES - 1 - k, 1), 0.0)
+        ub = [a * b for a, b in zip(g, q)]
+        put(image, k, q)
+        put(again, k, ub)
+        keep_rows(k, q, q_low, q_high, count)
+        packed = jnp.where(lane == k, pltpu.roll(ub[-1], (k + 1) % LANES, 1), packed)
+        return ub, (packed, zb + dot(u, q), bb + dot(ub, q), bbb)
+
+    def emit(k, found, carry):
+        keep_rows(k, found, k_low, k_high, count)
+        return *carry[:3], carry[3] + dot(tiles_of(again[k]), found)
+
+    packed, zb, bb, bbb = swept(count, width, rows, plane, emit, (jnp.zeros((rows, LANES), jnp.float32), one, one, one))
+    pack[...] = packed
+    sums[0], sums[1], sums[2] = zb, bb, bbb
 
 
 def along(tiles, left, right):
@@ -354,12 +403,11 @@
         out[pl.ds(8 * layer + i, 1), :] = jnp.sum(values, axis=0, keepdims=True)
 
 
-def ready_kernel(source, profile_own, profile_other, column, error, image, add_low, add_high, base, kept, sent):
+def ready_kernel(source, profile_own, profile_other, factors, image, add_low, add_high, _, base, kept, sent):
     layer = lax.axis_index("layer")
-    half, rows, width = source.shape[1:]
+    half, rows, _ = source.shape[1:]
     count = 2 * half
-    mine = column[...] * multiplier_of(error, layer)
-    theirs = column[...] * multiplier_of(error, 1 - layer)
+    mine, theirs = factors[layer], factors[1 - layer]
     row = iota((rows, LANES), 0)
 
     def store(ref, where, scale, k):
@@ -379,7 +427,7 @@
         base[1 - layer, at] = scale * (source_scale * source[1 - layer, at])
         return 0
 
-    lax.fori_loop(0, half, step, 0, unroll=2)
+    lax.fori_loop(0, half, step, 0, unroll=4)
 
 
 def final_kernel(base, kept, received, sums, out, factors):
@@ -423,7 +471,7 @@
 SMEM = pl.BlockSpec(memory_space=pltpu.SMEM)
 
 
-def call(kernel, out_shape, args, name, scalars=(), scratch=(), aliases=None, cost=0):
+def call(kernel, out_shape, args, scalars=(), scratch=(), aliases=None, cost=0):
     return pl.pallas_call(
         kernel,
         out_shape=[jax.ShapeDtypeStruct(shape, jnp.float32) for shape in out_shape],
@@ -433,11 +481,10 @@
         input_output_aliases=aliases or {},
         compiler_params=pltpu.CompilerParams(vmem_limit_bytes=GRANT),
         cost_estimate=pl.CostEstimate(flops=cost, bytes_accessed=cost, transcendentals=0) if cost else None,
-        name=name,
     )(*args)
 
 
-def local(source, profile, column, terrain_height_error):
+def solve(source, profile, column, terrain_height_error):
     copies, half, rows, width = source.shape
     count, tiles = 2 * half, width // LANES
     assert lax.axis_size("layer") == copies == 2 and count < LANES and width % LANES == 0
@@ -449,34 +496,24 @@
     block, row, pack = (count, rows, width), (nr, LANES), (rows, LANES)
     strip = (-(-(2 * nr + 2 + tiles) // 8) * 8, LANES)
     shapes = [block, block, strip, strip, (2 * rows, LANES), (2 * rows, LANES), (count, LANES), (8, LANES)]
-    begun = call(
-        functools.partial(weighted_kernel, True),
-        shapes,
-        (source, profile, column, terrain_height_error),
-        "weighted_own",
-        (1,),
-    )
+    factors = column * (1.0 + 0.002 * terrain_height_error.astype(jnp.float32))
+    begun = call(own_kernel, shapes, (source, profile, factors), (1,))
     weighted, gain, strip_low, strip_high, cols_low, cols_high, prof, sum_zz = call(
-        functools.partial(weighted_kernel, False),
-        shapes,
-        (other, profile_other, column, terrain_height_error, *begun),
-        "weighted_other",
-        (1,),
-        aliases={4 + i: i for i in range(8)},
+        other_kernel, shapes, (other, profile_other, factors, *begun), (1,), aliases={3 + i: i for i in range(8)}
     )
     even = lax.axis_index("col") % 2 == 0
     pair_cols, other_cols = exchanged(
         jnp.where(even, cols_high, cols_low), jnp.where(even, cols_low, cols_high), "col"
     )
+    image, g_low, g_high = call(image_kernel, [block, row, row], (weighted, gain))
     for_pairs, for_others = call(
-        functools.partial(join_kernel, nr), [strip, strip], (strip_low, strip_high, pair_cols, other_cols), "join"
+        functools.partial(join_kernel, nr), [strip, strip], (strip_low, strip_high, pair_cols, other_cols)
     )
     pair_strip, other_strip = exchanged(for_pairs, for_others, "tile")
-    image, q_low, q_high, g_low, g_high, k_low, k_high, packed, sum_rest = call(
+    image, q_low, q_high, k_low, k_high, packed, sum_rest = call(
         inner_kernel,
-        [block, row, row, row, row, row, row, pack, (3, 8, LANES)],
-        (weighted, gain, pair_cols, other_cols),
-        "inner",
+        [block, row, row, row, row, pack, (3, 8, LANES)],
+        (image, weighted, gain, pair_cols, other_cols),
         scratch=(block,),
     )
     sums, add_low, add_high = call(
@@ -501,18 +538,17 @@
             sum_zz,
             sum_rest,
         ),
-        "finish",
     )
     part = (half, rows, width)
+    sums, later = total(sums)
     base, kept, sent = call(
         ready_kernel,
         [source.shape, part, part],
-        (source, profile, profile_other, column, terrain_height_error, image, add_low, add_high),
-        "ready",
+        (source, profile, profile_other, factors, image, add_low, add_high, sums),
         (1, 2),
     )
     received = lax.ppermute(sent, "layer", swap)
-    sums = total(sums)
+    sums = later(sums)
     size = half // 2 if half % 2 == 0 else half
     return pl.pallas_call(
         final_kernel,
@@ -534,7 +570,7 @@
         P("group", "tile", "col"),
     )
     return jax.shard_map(
-        local,
+        solve,
         mesh=mesh,
         in_specs=placed,
         out_specs=P("group", "layer", "tile", "col"),

time: 37.4 us -> 34.2 us (0.914)
  local copies, waits for them, and re-layouts: 3.19 us -> 1.21 us
  waiting for transfers between devices: 9.26 us -> 7.45 us
  other arithmetic: 0.02 us -> 0.84 us
  Pallas kernels: 9.55 us -> 8.79 us
  starting transfers between devices: 14.9 us -> 15.5 us
    unnamed x12 -> x6, local copies, waits for them, and re-layouts: 3.19 us -> 1.21 us
    ppermute x5, waiting for transfers between devices: 7.44 us -> 5.64 us  [flipped(): return lax.ppermute(values, axes, pairs)]
    mul x0 -> x1, other arithmetic: none -> 0.82 us  [solve(): factors = column * (1.0 + 0.002 * terrain_height_error.astype(jnp.float32))]
    pallas_call x6 -> x7, Pallas kernels: 7.73 us -> 6.99 us  [call(): pl.pallas_call(kernel, out_shape=[jax.ShapeDtypeStruct(shape, jnp.float32...]
  transfers between devices with their start and end apart: 11 -> 11, of which waited for: 5 -> 5; matrix products, arithmetic and copies ran while one was open for 0% -> 2% of each run, Pallas kernels for 14% -> 13%
where the time goes in v4:
time: 34.2 us; the launch traced here: 34 us
  starting transfers between devices  15.5 us (45%)
  Pallas kernels  8.79 us (26%)
  waiting for transfers between devices  7.45 us (22%)
  local copies, waits for them, and re-layouts  1.21 us (4%)
  other arithmetic  0.84 us (2%)
    ppermute x5, starting transfers between devices, flipped(): return lax.ppermute(values, axes, pairs)  8.72 us
    pallas_call x7, Pallas kernels, call(): pl.pallas_call(kernel, out_shape=[jax.ShapeDtypeStruct(shape, jnp.float32...  6.99 us
    ppermute x5, waiting for transfers between devices, flipped(): return lax.ppermute(values, axes, pairs)  5.64 us
    ppermute x2, starting transfers between devices, exchanged(): first = lax.ppermute(for_pairs, axis, line_pairs(count, 0))  5.2 us
    ppermute x2, waiting for transfers between devices, exchanged(): first = lax.ppermute(for_pairs, axis, line_pairs(count, 0))  1.81 us
    pallas_call x1, Pallas kernels, solve(): pl.pallas_call(final_kernel, out_shape=jax.ShapeDtypeStruct(source.shape,...  1.79 us
    unnamed x6, local copies, waits for them, and re-layouts  1.21 us
    mul x1, other arithmetic, solve(): factors = column * (1.0 + 0.002 * terrain_height_error.astype(jnp.float32))  0.82 us
  transfers between devices with their start and end apart: 11, of which 5 were waited for; matrix products, arithmetic and copies ran while one was open for 2% of the time, Pallas kernels for 13%

profile of v4, /device:TPU:0, one launch (start us, length us, event | category | flops | bytes accessed | tf_op | source)
XLA Modules:
  0.0 34.0 jit_solution(1061757438937921138)
XLA Ops:
  0.0 0.5 %collective-permute-start.1 = (f32[2,20,24,256]{3,2,1,0:T(8,128)}, f32[2,20,24,256]{3,2,1,0:T(8,128)S(1)}, u32[]{:S(2)}, u32[]{:S(2)}) collective-permute-start(f32[2,20,24,256]{3,2,1,0:T(8,128)} %source.3), channel_id=1, source_target_pairs={{0,1},{1,0},{2,3},{3,2},{4,5},{5,4},{6,7},{7,6},{8,9},{9,8},{10,11... | collective-permute-start | bytes 2949128 | tf_op jit(solution)/shard_map/ppermute | solution.py:493
  0.5 0.0 collective-permute-start
  0.5 0.0 copy-start.2
  0.5 0.8 %add_multiply_fusion.factors = f32[2,24,256]{2,1,0:T(8,128)S(1)} fusion(s32[2,24,256]{2,1,0:T(8,128)} %param.7, f32[24,256]{1,0:T(8,128)} %param.6), kind=kLoop, calls=%fused_computation | loop fusion | flops 49152 | bytes 122880 | tf_op jit(solution)/shard_map/mul | solution.py:499
  1.3 0.0 copy-done.2
  1.4 0.0 copy-start
  1.4 1.2 %copy-done = f32[2,20,24,256]{3,2,1,0:T(8,128)S(1)} copy-done((f32[2,20,24,256]{3,2,1,0:T(8,128)S(1)}, f32[2,20,24,256]{3,2,1,0:T(8,128)}, u32[]{:S(2)}) %copy-start) | copy-done | bytes 983064
  2.6 1.1 %shard_map.46 = (f32[40,24,256]{2,1,0:T(8,128)S(1)}, f32[40,24,256]{2,1,0:T(8,128)S(1)}, f32[168,128]{1,0:T(8,128)S(1)}, f32[168,128]{1,0:T(8,128)S(1)}, f32[48,...) custom-call(f32[2,20,24,256]{3,2,1,0:T(8,128)S(1)} %copy-done, ...), custom_call_target="tpu_custom_call" | custom-call | tf_op jit(solution)/shard_map/pallas_call | solution.py:475
  3.7 0.0 collective-permute-done.profile.profile_other
  3.7 0.0 collective-permute-done.1.source
  3.7 1.1 %shard_map.47 = (f32[40,24,256]{2,1,0:T(8,128)S(1)}, f32[40,24,256]{2,1,0:T(8,128)S(1)}, f32[168,128]{1,0:T(8,128)S(1)}, f32[168,128]{1,0:T(8,128)S(1)}, f32[48,...) custom-call(f32[2,20,24,256]{3,2,1,0:T(8,128)S(1)} %collective-permu, ...), custom_call_target="tpu_custom_call", output_to_operand_aliasing={{0}: (3, {}), {1}: (4, {}), {2}: (5, {}), {3}: (6, {}), {4}... | custom-call | tf_op jit(solution)/shard_map/pallas_call | solution.py:475
  4.8 3.0 %collective-permute-start.2 = (f32[48,128]{1,0:T(8,128)S(1)}, f32[48,128]{1,0:T(8,128)S(1)}, u32[]{:S(2)}, u32[]{:S(2)}) collective-permute-start(f32[48,128]{1,0:T(8,128)S(1)} %broadcast_select_fusion), channel_id=1, source_target_pairs={{0,2},{2,0},{1,3},{3,1},{4,6},{6,4},{5,7},{7,5},{8,10},{10,8},{9,1... | collective-permute-start | bytes 73736 | tf_op jit(solution)/shard_map/ppermute | solution.py:33
  7.9 1.8 %collective-permute-done.2.pair_cols = f32[48,128]{1,0:T(8,128)S(1)} collective-permute-done((f32[48,128]{1,0:T(8,128)S(1)}, f32[48,128]{1,0:T(8,128)S(1)}, u32[]{:S(2)}, u32[]{:S(2)}) %collective-permute-start.2) | collective-permute-done | bytes 24608 | tf_op jit(solution)/shard_map/ppermute | solution.py:33
  9.7 2.2 %collective-permute-start.3 = (f32[168,128]{1,0:T(8,128)S(1)}, f32[168,128]{1,0:T(8,128)S(1)}, u32[]{:S(2)}, u32[]{:S(2)}) collective-permute-start(f32[168,128]{1,0:T(8,128)S(1)} %get-tuple-element.55), channel_id=1, source_target_pairs={{0,4},{4,0},{8,12},{12,8},{1,5},{5,1},{9,13},{13,9},{2,6},{6,2},{1... | collective-permute-start | bytes 258056 | tf_op jit(solution)/shard_map/ppermute | solution.py:33
  11.9 0.7 %collective-permute-start.4 = (f32[168,128]{1,0:T(8,128)S(1)}, f32[168,128]{1,0:T(8,128)S(1)}, u32[]{:S(2)}, u32[]{:S(2)}) collective-permute-start(f32[168,128]{1,0:T(8,128)S(1)} %get-tuple-element.56), channel_id=1, source_target_pairs={{4,8},{8,4},{5,9},{9,5},{6,10},{10,6},{7,11},{11,7},{20,24},{24,20... | collective-permute-start | bytes 258056 | tf_op jit(solution)/shard_map/ppermute | solution.py:36
  12.5 0.8 %shard_map.48 = (f32[40,24,256]{2,1,0:T(8,128)S(1)}, f32[80,128]{1,0:T(8,128)S(1)}, f32[80,128]{1,0:T(8,128)S(1)}) custom-call(f32[40,24,256]{2,1,0:T(8,128)S(1)} %get-tuple-element.47.weighted, f32[40,24,256]{2,1,0:T(8,128)S(1)} %get-tuple-element.48.gain), custom_call_target="tpu_custom_call" | custom-call | tf_op jit(solution)/shard_map/pallas_call | solution.py:475
  13.4 0.0 copy-start.1
  13.4 2.6 %shard_map.49 = (f32[40,24,256]{2,1,0:T(8,128)S(1)}, f32[80,128]{1,0:T(8,128)S(1)}, f32[80,128]{1,0:T(8,128)S(1)}, f32[80,128]{1,0:T(8,128)S(1)}, f32[80,128]{1,...) custom-call(f32[40,24,256]{2,1,0:T(8,128)S(1)} %get-tuple-element.49.begun, ...), custom_call_target="tpu_custom_call" | custom-call | tf_op jit(solution)/shard_map/pallas_call | solution.py:475
  16.0 0.0 collective-permute-done.3.pair_strip
  16.0 0.0 collective-permute-done.4.other_strip
  16.0 0.3 shard_map.51
  16.3 0.1 collective-permute-start.7
  16.4 1.6 %collective-permute-start.6 = (f32[16,128]{1,0:T(8,128)S(1)}, f32[16,128]{1,0:T(8,128)S(1)}, u32[]{:S(2)}, u32[]{:S(2)}) collective-permute-start(f32[16,128]{1,0:T(8,128)S(1)} %get-tuple-element.69), channel_id=1, source_target_pairs={{0,2},{2,0},{1,3},{3,1},{4,6},{6,4},{5,7},{7,5},{8,10},{10,8},{9,1... | collective-permute-start | bytes 24584 | tf_op jit(solution)/shard_map/ppermute | solution.py:51
  17.9 0.3 collective-permute-start.5
  18.2 1.3 %collective-permute-done.7 = f32[16,128]{1,0:T(8,128)S(1)} collective-permute-done((f32[16,128]{1,0:T(8,128)S(1)}, f32[16,128]{1,0:T(8,128)S(1)}, u32[]{:S(2)}, u32[]{:S(2)}) %collective-permute-start.7) | collective-permute-done | bytes 8224 | tf_op jit(solution)/shard_map/ppermute | solution.py:51
  19.5 0.6 %collective-permute-done.6 = f32[16,128]{1,0:T(8,128)S(1)} collective-permute-done((f32[16,128]{1,0:T(8,128)S(1)}, f32[16,128]{1,0:T(8,128)S(1)}, u32[]{:S(2)}, u32[]{:S(2)}) %collective-permute-start.6) | collective-permute-done | bytes 8224 | tf_op jit(solution)/shard_map/ppermute | solution.py:51
  20.1 0.0 collective-permute-done.5
  20.1 0.0 copy-done.1
  20.1 1.0 %shard_map.52 = (f32[2,20,24,256]{3,2,1,0:T(8,128)S(1)}, f32[20,24,256]{2,1,0:T(8,128)S(1)}, f32[20,24,256]{2,1,0:T(8,128)S(1)}) custom-call(f32[2,20,24,256]{3,2,1,0:T(8,128)S(1)} %copy-done.1, f32[20]{0:T(128)S(1)} %copy-done.2, f32[20]{0:T(128)S(1)} %collective-permute-done.profile.profile_other, f32[2,24,256]{2,1,0:T(8,128)S(1)} %add_multiply_fusion.factors, ...), custom_call_target="tpu_custom_call" | custom-call | tf_op jit(solution)/shard_map/pallas_call | solution.py:475
  21.2 0.4 %collective-permute-start.8 = (f32[20,24,256]{2,1,0:T(8,128)S(1)}, f32[20,24,256]{2,1,0:T(8,128)S(1)}, u32[]{:S(2)}, u32[]{:S(2)}) collective-permute-start(f32[20,24,256]{2,1,0:T(8,128)S(1)} %get-tuple-element.72), channel_id=1, source_target_pairs={{0,1},{1,0},{2,3},{3,2},{4,5},{5,4},{6,7},{7,6},{8,9},{9,8},{10,11... | collective-permute-start | bytes 1474568 | tf_op jit(solution)/shard_map/ppermute | solution.py:550
  21.6 4.4 %collective-permute-start.9 = (f32[16,128]{1,0:T(8,128)S(1)}, f32[16,128]{1,0:T(8,128)S(1)}, u32[]{:S(2)}, u32[]{:S(2)}) collective-permute-start(f32[16,128]{1,0:T(8,128)S(1)} %add_add_fusion._), channel_id=1, source_target_pairs={{0,4},{4,0},{8,12},{12,8},{1,5},{5,1},{9,13},{13,9},{2,6},{6,2},{1... | collective-permute-start | bytes 24584 | tf_op jit(solution)/shard_map/ppermute | solution.py:51
  26.0 1.6 %collective-permute-done.9 = f32[16,128]{1,0:T(8,128)S(1)} collective-permute-done((f32[16,128]{1,0:T(8,128)S(1)}, f32[16,128]{1,0:T(8,128)S(1)}, u32[]{:S(2)}, u32[]{:S(2)}) %collective-permute-start.9) | collective-permute-done | bytes 8224 | tf_op jit(solution)/shard_map/ppermute | solution.py:51
  27.6 2.4 %collective-permute-start.10 = (f32[16,128]{1,0:T(8,128)S(1)}, f32[16,128]{1,0:T(8,128)S(1)}, u32[]{:S(2)}, u32[]{:S(2)}) collective-permute-start(f32[16,128]{1,0:T(8,128)S(1)} %add.31), channel_id=1, source_target_pairs={{0,8},{4,12},{8,0},{12,4},{1,9},{5,13},{9,1},{13,5},{2,10},{6,14},... | collective-permute-start | bytes 24584 | tf_op jit(solution)/shard_map/ppermute | solution.py:51
  30.0 2.1 %collective-permute-done.10 = f32[16,128]{1,0:T(8,128)S(1)} collective-permute-done((f32[16,128]{1,0:T(8,128)S(1)}, f32[16,128]{1,0:T(8,128)S(1)}, u32[]{:S(2)}, u32[]{:S(2)}) %collective-permute-start.10) | collective-permute-done | bytes 8224 | tf_op jit(solution)/shard_map/ppermute | solution.py:51
  32.2 0.0 collective-permute-done.8.received
  32.2 1.8 %final.1 = f32[2,20,24,256]{3,2,1,0:T(8,128)} custom-call(f32[2,20,24,256]{3,2,1,0:T(8,128)S(1)} %get-tuple-element.70.base, f32[20,24,256]{2,1,0:T(8,128)S(1)} %get-tuple-element.71.kept, f32[20,24,256]{2,1,0:T(8,128)S(1)} %collective-permute-done.8.received, f32[16,128]{1,0:T(8,128)S(1)} %add.32.sums), custom_call_target="tpu_custom_call" | custom-call | tf_op jit(solution)/shard_map/final/pallas_call | solution.py:553
  (6 shorter events, 0.0 us)
Async XLA Ops:
  0.0 3.7 %collective-permute-start.1 = (f32[2,20,24,256]{3,2,1,0:T(8,128)}, f32[2,20,24,256]{3,2,1,0:T(8,128)S(1)}, u32[]{:S(2)}, u32[]{:S(2)}) collective-permute-start(f32[2,20,24,256]{3,2,1,0:T(8,128)} %source.3), channel_id=1, source_target_pairs={{0,1},{1,0},{2,3},{3,2},{4,5},{5,4},{6,7},{7,6},{8,9},{9,8},{10,11... | collective-permute-start | bytes 2949128 | tf_op jit(solution)/shard_map/ppermute | solution.py:493
  0.5 3.2 %collective-permute-start = (f32[20]{0:T(128)}, f32[20]{0:T(128)S(1)}, u32[]{:S(2)}, u32[]{:S(2)}) collective-permute-start(f32[20]{0:T(128)} %profile_own.1), channel_id=1, source_target_pairs={{0,1},{1,0},{2,3},{3,2},{4,5},{5,4},{6,7},{7,6},{8,9},{9,8},{10,11... | collective-permute-start | bytes 248 | tf_op jit(solution)/shard_map/ppermute | solution.py:494
  0.5 0.8 %copy-start.2 = (f32[20]{0:T(128)S(1)}, f32[20]{0:T(128)}, u32[]{:S(2)}) copy-start(f32[20]{0:T(128)} %profile_own.1) | copy-start | bytes 244
  1.4 1.2 %copy-start = (f32[2,20,24,256]{3,2,1,0:T(8,128)S(1)}, f32[2,20,24,256]{3,2,1,0:T(8,128)}, u32[]{:S(2)}) copy-start(f32[2,20,24,256]{3,2,1,0:T(8,128)} %source.3) | copy-start | bytes 2949124
  4.8 4.8 %collective-permute-start.2 = (f32[48,128]{1,0:T(8,128)S(1)}, f32[48,128]{1,0:T(8,128)S(1)}, u32[]{:S(2)}, u32[]{:S(2)}) collective-permute-start(f32[48,128]{1,0:T(8,128)S(1)} %broadcast_select_fusion), channel_id=1, source_target_pairs={{0,2},{2,0},{1,3},{3,1},{4,6},{6,4},{5,7},{7,5},{8,10},{10,8},{9,1... | collective-permute-start | bytes 73736 | tf_op jit(solution)/shard_map/ppermute | solution.py:33
  9.7 6.3 %collective-permute-start.3 = (f32[168,128]{1,0:T(8,128)S(1)}, f32[168,128]{1,0:T(8,128)S(1)}, u32[]{:S(2)}, u32[]{:S(2)}) collective-permute-start(f32[168,128]{1,0:T(8,128)S(1)} %get-tuple-element.55), channel_id=1, source_target_pairs={{0,4},{4,0},{8,12},{12,8},{1,5},{5,1},{9,13},{13,9},{2,6},{6,2},{1... | collective-permute-start | bytes 258056 | tf_op jit(solution)/shard_map/ppermute | solution.py:33
  11.9 4.2 %collective-permute-start.4 = (f32[168,128]{1,0:T(8,128)S(1)}, f32[168,128]{1,0:T(8,128)S(1)}, u32[]{:S(2)}, u32[]{:S(2)}) collective-permute-start(f32[168,128]{1,0:T(8,128)S(1)} %get-tuple-element.56), channel_id=1, source_target_pairs={{4,8},{8,4},{5,9},{9,5},{6,10},{10,6},{7,11},{11,7},{20,24},{24,20... | collective-permute-start | bytes 258056 | tf_op jit(solution)/shard_map/ppermute | solution.py:36
  13.4 6.8 %copy-start.1 = (f32[2,20,24,256]{3,2,1,0:T(8,128)S(1)}, f32[2,20,24,256]{3,2,1,0:T(8,128)}, u32[]{:S(2)}) copy-start(f32[2,20,24,256]{3,2,1,0:T(8,128)} %source.3) | copy-start | bytes 2949124
  16.3 3.2 %collective-permute-start.7 = (f32[16,128]{1,0:T(8,128)S(1)}, f32[16,128]{1,0:T(8,128)S(1)}, u32[]{:S(2)}, u32[]{:S(2)}) collective-permute-start(f32[16,128]{1,0:T(8,128)S(1)} %get-tuple-element.69), channel_id=1, source_target_pairs={{0,3},{1,2},{2,1},{3,0},{4,7},{5,6},{6,5},{7,4},{8,11},{9,10},{10,... | collective-permute-start | bytes 24584 | tf_op jit(solution)/shard_map/ppermute | solution.py:51
  16.4 3.7 %collective-permute-start.6 = (f32[16,128]{1,0:T(8,128)S(1)}, f32[16,128]{1,0:T(8,128)S(1)}, u32[]{:S(2)}, u32[]{:S(2)}) collective-permute-start(f32[16,128]{1,0:T(8,128)S(1)} %get-tuple-element.69), channel_id=1, source_target_pairs={{0,2},{2,0},{1,3},{3,1},{4,6},{6,4},{5,7},{7,5},{8,10},{10,8},{9,1... | collective-permute-start | bytes 24584 | tf_op jit(solution)/shard_map/ppermute | solution.py:51
  17.9 2.2 %collective-permute-start.5 = (f32[16,128]{1,0:T(8,128)S(1)}, f32[16,128]{1,0:T(8,128)S(1)}, u32[]{:S(2)}, u32[]{:S(2)}) collective-permute-start(f32[16,128]{1,0:T(8,128)S(1)} %get-tuple-element.69), channel_id=1, source_target_pairs={{0,1},{1,0},{2,3},{3,2},{4,5},{5,4},{6,7},{7,6},{8,9},{9,8},{10,11... | collective-permute-start | bytes 24584 | tf_op jit(solution)/shard_map/ppermute | solution.py:51
  21.2 11.0 %collective-permute-start.8 = (f32[20,24,256]{2,1,0:T(8,128)S(1)}, f32[20,24,256]{2,1,0:T(8,128)S(1)}, u32[]{:S(2)}, u32[]{:S(2)}) collective-permute-start(f32[20,24,256]{2,1,0:T(8,128)S(1)} %get-tuple-element.72), channel_id=1, source_target_pairs={{0,1},{1,0},{2,3},{3,2},{4,5},{5,4},{6,7},{7,6},{8,9},{9,8},{10,11... | collective-permute-start | bytes 1474568 | tf_op jit(solution)/shard_map/ppermute | solution.py:550
  21.6 6.0 %collective-permute-start.9 = (f32[16,128]{1,0:T(8,128)S(1)}, f32[16,128]{1,0:T(8,128)S(1)}, u32[]{:S(2)}, u32[]{:S(2)}) collective-permute-start(f32[16,128]{1,0:T(8,128)S(1)} %add_add_fusion._), channel_id=1, source_target_pairs={{0,4},{4,0},{8,12},{12,8},{1,5},{5,1},{9,13},{13,9},{2,6},{6,2},{1... | collective-permute-start | bytes 24584 | tf_op jit(solution)/shard_map/ppermute | solution.py:51
  27.6 4.5 %collective-permute-start.10 = (f32[16,128]{1,0:T(8,128)S(1)}, f32[16,128]{1,0:T(8,128)S(1)}, u32[]{:S(2)}, u32[]{:S(2)}) collective-permute-start(f32[16,128]{1,0:T(8,128)S(1)} %add.31), channel_id=1, source_target_pairs={{0,8},{4,12},{8,0},{12,4},{1,9},{5,13},{9,1},{13,5},{2,10},{6,14},... | collective-permute-start | bytes 24584 | tf_op jit(solution)/shard_map/ppermute | solution.py:51

commit v5 on v4

--- a/solution.py
+++ b/solution.py
@@ -27,13 +27,28 @@
 
 
 def exchanged(for_pairs, for_others, axis):
-    count = lax.axis_size(axis)
-    if count == 1:
-        return jnp.zeros_like(for_pairs), jnp.zeros_like(for_others)
-    first = lax.ppermute(for_pairs, axis, line_pairs(count, 0))
-    if count == 2:
-        return first, jnp.zeros_like(first)
-    return first, lax.ppermute(for_others, axis, line_pairs(count, 1))
+    count, layers = lax.axis_size(axis), lax.axis_size("layer")
+    received = []
+    for first, values in ((0, for_pairs), (1, for_others)):
+        partner = dict(line_pairs(count, first))
+        if not partner:
+            received.append(jnp.zeros_like(values))
+            continue
+        pairs = []
+        for place in range(count):
+            for layer in range(layers):
+                target = (partner[place], layer) if place in partner else (place, layers - 1 - layer)
+                pairs.append((place * layers + layer, target[0] * layers + target[1]))
+        received.append(lax.ppermute(values, (axis, "layer"), pairs))
+    return received
+
+
+def halves(first, second, axis):
+    place, count = lax.axis_index(axis), lax.axis_size(axis)
+    even = place % 2 == 0
+    low = jnp.where(place > 0, jnp.where(even, second, first), 0.0)
+    high = jnp.where(place < count - 1, jnp.where(even, first, second), 0.0)
+    return low, high
 
 
 def flipped(values, sizes, axes, bits):
@@ -208,9 +223,7 @@
 
 def join_kernel(nr, strip_low, strip_high, pair_cols, other_cols, for_pairs, for_others):
     rows = pair_cols.shape[0] // 2
-    first, second = pair_cols[...], other_cols[...]
-    even = lax.axis_index("col") % 2 == 0
-    low_cols, high_cols = jnp.where(even, second, first), jnp.where(even, first, second)
+    low_cols, high_cols = halves(pair_cols[...], other_cols[...], "col")
     at = iota(strip_low.shape, 0)
     low, high = strip_low[...], strip_high[...]
     low = jnp.where(at == 2 * nr, low_cols[0:1], jnp.where(at == 2 * nr + 1, high_cols[0:1], low))
@@ -271,15 +284,14 @@
 
 def inner_kernel(begun, weighted, gain, pair_cols, other_cols, image, q_low, q_high, k_low, k_high, pack, sums, again):
     count, rows, width = weighted.shape
-    even = lax.axis_index("col") % 2 == 0
     lane = iota((rows, LANES), 1)
-    first, second = pair_cols[0:rows], other_cols[0:rows]
-    add_low = near(jnp.where((lane < count), jnp.where(even, second, first), 0.0), 1)
-    add_high = near(jnp.where((lane < count), jnp.where(even, first, second), 0.0), 1)
+    low, high = halves(pair_cols[0:rows], other_cols[0:rows], "col")
+    add_low = near(jnp.where(lane < count, low, 0.0), 1)
+    add_high = near(jnp.where(lane < count, high, 0.0), 1)
     one = jnp.zeros((8, LANES), jnp.float32)
 
-    def plane(k, carry):
-        packed, zb, bb, bbb = carry
+    def step(k, carry):
+        packed, zb, bb = carry
         u, g, q = tiles_of(weighted[k]), tiles_of(gain[k]), tiles_of(begun[k])
         q[0] = q[0] + jnp.where(lane == 0, pltpu.roll(add_low, lax.rem(LANES - k, LANES), 1), 0.0)
         q[-1] = q[-1] + jnp.where(lane == LANES - 1, pltpu.roll(add_high, LANES - 1 - k, 1), 0.0)
@@ -287,14 +299,15 @@
         put(image, k, q)
         put(again, k, ub)
         keep_rows(k, q, q_low, q_high, count)
-        packed = jnp.where(lane == k, pltpu.roll(ub[-1], (k + 1) % LANES, 1), packed)
-        return ub, (packed, zb + dot(u, q), bb + dot(ub, q), bbb)
-
-    def emit(k, found, carry):
+        packed = jnp.where(lane == k, pltpu.roll(ub[-1], k + 1, 1), packed)
+        return packed, zb + dot(u, q), bb + dot(ub, q)
+
+    def emit(k, found, bbb):
         keep_rows(k, found, k_low, k_high, count)
-        return *carry[:3], carry[3] + dot(tiles_of(again[k]), found)
-
-    packed, zb, bb, bbb = swept(count, width, rows, plane, emit, (jnp.zeros((rows, LANES), jnp.float32), one, one, one))
+        return bbb + dot(tiles_of(again[k]), found)
+
+    packed, zb, bb = lax.fori_loop(0, count, step, (jnp.zeros((rows, LANES), jnp.float32), one, one), unroll=8)
+    bbb = swept(count, width, rows, lambda k, carry: (tiles_of(again[k]), carry), emit, one)
     pack[...] = packed
     sums[0], sums[1], sums[2] = zb, bb, bbb
 
@@ -335,11 +348,8 @@
     nr = q_low.shape[0]
     tiles = nr // count
     rows = pack.shape[0]
-    even = lax.axis_index("tile") % 2 == 0
-    first, second = pair_strip[...], other_strip[...]
-    low, high = jnp.where(even, second, first), jnp.where(even, first, second)
-    even = lax.axis_index("col") % 2 == 0
-    high_cols = jnp.where(even, pair_cols[...], other_cols[...])
+    low, high = halves(pair_strip[...], other_strip[...], "tile")
+    _, high_cols = halves(pair_cols[...], other_cols[...], "col")
 
     def blocks(values, start=0):
         return [values[start + i * count : start + (i + 1) * count] for i in range(tiles)]
@@ -400,7 +410,7 @@
     layer = lax.axis_index("layer")
     out[...] = jnp.zeros_like(out)
     for i, values in enumerate((sum_zz[...], zb, bb, bbb)):
-        out[pl.ds(8 * layer + i, 1), :] = jnp.sum(values, axis=0, keepdims=True)
+        out[pl.ds(2 * i + layer, 1), :] = jnp.sum(values, axis=0, keepdims=True)
 
 
 def ready_kernel(source, profile_own, profile_other, factors, image, add_low, add_high, _, base, kept, sent):
@@ -437,21 +447,21 @@
 
     @pl.when((which == 0) & (at == 0))
     def _():
-        for each in range(2):
-            values = jnp.sum(sums[8 * each : 8 * each + 8], axis=1, keepdims=True)
-            zz, zb, bb, bbb = (values[i : i + 1] for i in range(4))
-            delta = zz - zb
-            alpha = zz / delta
-            rest = -zb / delta
-            beta = (zz * bb - zb * zb) / (delta * delta)
-            gamma = zz * beta
-            delta_next = gamma - (rest * rest * zb + 2.0 * alpha * rest * bb + alpha * alpha * bbb)
-            alpha_next = gamma / (delta_next - beta * gamma / alpha)
-            factors[each, 0] = jnp.broadcast_to(alpha + alpha_next * (rest + beta), (8, LANES))
-            factors[each, 1] = jnp.broadcast_to(alpha_next * alpha, (8, LANES))
-
-    first = jnp.broadcast_to(factors[which, 0][0:1, 0:1], (rows, width))
-    second = jnp.broadcast_to(factors[which, 1][0:1, 0:1], (rows, width))
+        values = jnp.sum(sums[...], axis=1, keepdims=True)
+        zz, zb, bb, bbb = (values[2 * i : 2 * i + 2] for i in range(4))
+        delta = zz - zb
+        alpha = zz / delta
+        rest = -zb / delta
+        beta = (zz * bb - zb * zb) / (delta * delta)
+        gamma = zz * beta
+        delta_next = gamma - (rest * rest * zb + 2.0 * alpha * rest * bb + alpha * alpha * bbb)
+        alpha_next = gamma / (delta_next - beta * gamma / alpha)
+        factors[0] = jnp.broadcast_to(alpha + alpha_next * (rest + beta), (2, LANES))
+        factors[1] = jnp.broadcast_to(alpha_next * alpha, (2, LANES))
+
+    first = factors[0, pl.ds(which, 1), :][:, 0:1]
+    second = factors[1, pl.ds(which, 1), :][:, 0:1]
+    first, second = jnp.broadcast_to(first, (rows, width)), jnp.broadcast_to(second, (rows, width))
 
     def fill(image):
         for i in range(size):
@@ -518,7 +528,7 @@
     )
     sums, add_low, add_high = call(
         finish_kernel,
-        [(16, LANES), row, row],
+        [(8, LANES), row, row],
         (
             pair_strip,
             other_strip,
@@ -556,7 +566,7 @@
         grid=(2, half // size),
         in_specs=[VMEM] * 4,
         out_specs=pl.BlockSpec((1, size, rows, width), lambda i, j: (i, j, 0, 0)),
-        scratch_shapes=[pltpu.VMEM((2, 2, 8, LANES), jnp.float32)],
+        scratch_shapes=[pltpu.VMEM((2, 2, LANES), jnp.float32)],
         compiler_params=pltpu.CompilerParams(vmem_limit_bytes=GRANT),
         name="final",
     )(base, kept, received, sums)

time: 34.2 us -> 31.7 us (0.927)
  starting transfers between devices: 15.5 us -> 13.2 us
  Pallas kernels: 8.79 us -> 7.92 us
  waiting for transfers between devices: 7.45 us -> 8.16 us
    ppermute x5, starting transfers between devices: 8.72 us -> 7.43 us  [flipped(): return lax.ppermute(values, axes, pairs)]
    pallas_call x7, Pallas kernels: 6.99 us -> 6.09 us  [call(): pl.pallas_call(kernel, out_shape=[jax.ShapeDtypeStruct(shape, jnp.float32...]
    ppermute x5, waiting for transfers between devices: 5.64 us -> 6.34 us  [flipped(): return lax.ppermute(values, axes, pairs)]
    ppermute x3, starting transfers between devices: 5.86 us -> 5.21 us  [exchanged(): received.append(lax.ppermute(values, (axis, 'layer'), pairs))]
    ppermute x1, starting transfers between devices: 0.44 us -> 0.07 us  [solve(): received = lax.ppermute(sent, 'layer', swap)]
  transfers between devices with their start and end apart: 11 -> 11, of which waited for: 5 -> 5; matrix products, arithmetic and copies ran while one was open for 2% -> 3% of each run, Pallas kernels for 13% -> 12%
where the time goes in v5:
time: 31.7 us; the launch traced here: 31.5 us
  starting transfers between devices  13.2 us (42%)
  waiting for transfers between devices  8.16 us (26%)
  Pallas kernels  7.92 us (25%)
  local copies, waits for them, and re-layouts  1.21 us (4%)
  other arithmetic  0.84 us (3%)
    ppermute x5, starting transfers between devices, flipped(): return lax.ppermute(values, axes, pairs)  7.43 us
    ppermute x5, waiting for transfers between devices, flipped(): return lax.ppermute(values, axes, pairs)  6.34 us
    pallas_call x7, Pallas kernels, call(): pl.pallas_call(kernel, out_shape=[jax.ShapeDtypeStruct(shape, jnp.float32...  6.09 us
    ppermute x3, starting transfers between devices, exchanged(): received.append(lax.ppermute(values, (axis, 'layer'), pairs))  5.21 us
    pallas_call x1, Pallas kernels, solve(): pl.pallas_call(final_kernel, out_shape=jax.ShapeDtypeStruct(source.shape,...  1.82 us
    ppermute x3, waiting for transfers between devices, exchanged(): received.append(lax.ppermute(values, (axis, 'layer'), pairs))  1.81 us
    unnamed x6, local copies, waits for them, and re-layouts  1.21 us
    mul x1, other arithmetic, solve(): factors = column * (1.0 + 0.002 * terrain_height_error.astype(jnp.float32))  0.82 us
  transfers between devices with their start and end apart: 11, of which 5 were waited for; matrix products, arithmetic and copies ran while one was open for 3% of the time, Pallas kernels for 12%

profile of v5, /device:TPU:0, one launch (start us, length us, event | category | flops | bytes accessed | tf_op | source)
XLA Modules:
  0.0 31.5 jit_solution(10390139036023507479)
XLA Ops:
  0.0 0.5 %collective-permute-start.1 = (f32[2,20,24,256]{3,2,1,0:T(8,128)}, f32[2,20,24,256]{3,2,1,0:T(8,128)S(1)}, u32[]{:S(2)}, u32[]{:S(2)}) collective-permute-start(f32[2,20,24,256]{3,2,1,0:T(8,128)} %source.3), channel_id=1, source_target_pairs={{0,1},{1,0},{2,3},{3,2},{4,5},{5,4},{6,7},{7,6},{8,9},{9,8},{10,11... | collective-permute-start | bytes 2949128 | tf_op jit(solution)/shard_map/ppermute | solution.py:503
  0.5 0.0 collective-permute-start
  0.5 0.0 copy-start.2
  0.5 0.8 %add_multiply_fusion.factors = f32[2,24,256]{2,1,0:T(8,128)S(1)} fusion(s32[2,24,256]{2,1,0:T(8,128)} %param.7, f32[24,256]{1,0:T(8,128)} %param.6), kind=kLoop, calls=%fused_computation | loop fusion | flops 49152 | bytes 122880 | tf_op jit(solution)/shard_map/mul | solution.py:509
  1.3 0.0 copy-done.2
  1.4 0.0 copy-start
  1.4 1.2 %copy-done = f32[2,20,24,256]{3,2,1,0:T(8,128)S(1)} copy-done((f32[2,20,24,256]{3,2,1,0:T(8,128)S(1)}, f32[2,20,24,256]{3,2,1,0:T(8,128)}, u32[]{:S(2)}) %copy-start) | copy-done | bytes 983064
  2.6 1.1 %shard_map.46 = (f32[40,24,256]{2,1,0:T(8,128)S(1)}, f32[40,24,256]{2,1,0:T(8,128)S(1)}, f32[168,128]{1,0:T(8,128)S(1)}, f32[168,128]{1,0:T(8,128)S(1)}, f32[48,...) custom-call(f32[2,20,24,256]{3,2,1,0:T(8,128)S(1)} %copy-done, ...), custom_call_target="tpu_custom_call" | custom-call | tf_op jit(solution)/shard_map/pallas_call | solution.py:485
  3.7 0.0 collective-permute-done.profile.profile_other
  3.7 0.0 collective-permute-done.1.source
  3.7 1.1 %shard_map.47 = (f32[40,24,256]{2,1,0:T(8,128)S(1)}, f32[40,24,256]{2,1,0:T(8,128)S(1)}, f32[168,128]{1,0:T(8,128)S(1)}, f32[168,128]{1,0:T(8,128)S(1)}, f32[48,...) custom-call(f32[2,20,24,256]{3,2,1,0:T(8,128)S(1)} %collective-permu, ...), custom_call_target="tpu_custom_call", output_to_operand_aliasing={{0}: (3, {}), {1}: (4, {}), {2}: (5, {}), {3}: (6, {}), {4}... | custom-call | tf_op jit(solution)/shard_map/pallas_call | solution.py:485
  4.8 3.0 %collective-permute-start.2 = (f32[48,128]{1,0:T(8,128)S(1)}, f32[48,128]{1,0:T(8,128)S(1)}, u32[]{:S(2)}, u32[]{:S(2)}) collective-permute-start(f32[48,128]{1,0:T(8,128)S(1)} %broadcast_select_fusion), channel_id=1, source_target_pairs={{0,2},{1,3},{2,0},{3,1},{4,6},{5,7},{6,4},{7,5},{8,10},{9,11},{10,... | collective-permute-start | bytes 73736 | tf_op jit(solution)/shard_map/ppermute | solution.py:42
  7.9 1.8 %collective-permute-done.2.pair_cols = f32[48,128]{1,0:T(8,128)S(1)} collective-permute-done((f32[48,128]{1,0:T(8,128)S(1)}, f32[48,128]{1,0:T(8,128)S(1)}, u32[]{:S(2)}, u32[]{:S(2)}) %collective-permute-start.2) | collective-permute-done | bytes 24608 | tf_op jit(solution)/shard_map/ppermute | solution.py:42
  9.7 2.2 %collective-permute-start.3 = (f32[168,128]{1,0:T(8,128)S(1)}, f32[168,128]{1,0:T(8,128)S(1)}, u32[]{:S(2)}, u32[]{:S(2)}) collective-permute-start(f32[168,128]{1,0:T(8,128)S(1)} %get-tuple-element.55), channel_id=1, source_target_pairs={{0,4},{1,5},{4,0},{5,1},{8,12},{9,13},{12,8},{13,9},{2,6},{3,7},{6... | collective-permute-start | bytes 258056 | tf_op jit(solution)/shard_map/ppermute | solution.py:42
  11.9 0.0 collective-permute-start.4
  11.9 0.8 %shard_map.48 = (f32[40,24,256]{2,1,0:T(8,128)S(1)}, f32[80,128]{1,0:T(8,128)S(1)}, f32[80,128]{1,0:T(8,128)S(1)}) custom-call(f32[40,24,256]{2,1,0:T(8,128)S(1)} %get-tuple-element.47.weighted, f32[40,24,256]{2,1,0:T(8,128)S(1)} %get-tuple-element.48.gain), custom_call_target="tpu_custom_call" | custom-call | tf_op jit(solution)/shard_map/pallas_call | solution.py:485
  12.7 0.0 copy-start.1
  12.7 1.8 %shard_map.49 = (f32[40,24,256]{2,1,0:T(8,128)S(1)}, f32[80,128]{1,0:T(8,128)S(1)}, f32[80,128]{1,0:T(8,128)S(1)}, f32[80,128]{1,0:T(8,128)S(1)}, f32[80,128]{1,...) custom-call(f32[40,24,256]{2,1,0:T(8,128)S(1)} %get-tuple-element.49.begun, ...), custom_call_target="tpu_custom_call" | custom-call | tf_op jit(solution)/shard_map/pallas_call | solution.py:485
  14.5 0.0 collective-permute-done.3.pair_strip
  14.5 0.0 collective-permute-done.4.other_strip
  14.5 0.3 shard_map.51
  14.7 1.7 %collective-permute-start.7 = (f32[8,128]{1,0:T(8,128)S(1)}, f32[8,128]{1,0:T(8,128)S(1)}, u32[]{:S(2)}, u32[]{:S(2)}) collective-permute-start(f32[8,128]{1,0:T(8,128)S(1)} %get-tuple-element.69), channel_id=1, source_target_pairs={{0,3},{1,2},{2,1},{3,0},{4,7},{5,6},{6,5},{7,4},{8,11},{9,10},{10,... | collective-permute-start | bytes 12296 | tf_op jit(solution)/shard_map/ppermute | solution.py:66
  16.4 0.5 %collective-permute-start.6 = (f32[8,128]{1,0:T(8,128)S(1)}, f32[8,128]{1,0:T(8,128)S(1)}, u32[]{:S(2)}, u32[]{:S(2)}) collective-permute-start(f32[8,128]{1,0:T(8,128)S(1)} %get-tuple-element.69), channel_id=1, source_target_pairs={{0,2},{2,0},{1,3},{3,1},{4,6},{6,4},{5,7},{7,5},{8,10},{10,8},{9,1... | collective-permute-start | bytes 12296 | tf_op jit(solution)/shard_map/ppermute | solution.py:66
  16.9 0.0 collective-permute-start.5
  17.0 0.9 %collective-permute-done.7 = f32[8,128]{1,0:T(8,128)S(1)} collective-permute-done((f32[8,128]{1,0:T(8,128)S(1)}, f32[8,128]{1,0:T(8,128)S(1)}, u32[]{:S(2)}, u32[]{:S(2)}) %collective-permute-start.7) | collective-permute-done | bytes 4128 | tf_op jit(solution)/shard_map/ppermute | solution.py:66
  17.8 2.2 %collective-permute-done.6 = f32[8,128]{1,0:T(8,128)S(1)} collective-permute-done((f32[8,128]{1,0:T(8,128)S(1)}, f32[8,128]{1,0:T(8,128)S(1)}, u32[]{:S(2)}, u32[]{:S(2)}) %collective-permute-start.6) | collective-permute-done | bytes 4128 | tf_op jit(solution)/shard_map/ppermute | solution.py:66
  20.0 0.0 collective-permute-done.5
  20.0 0.0 copy-done.1
  20.0 1.0 %shard_map.52 = (f32[2,20,24,256]{3,2,1,0:T(8,128)S(1)}, f32[20,24,256]{2,1,0:T(8,128)S(1)}, f32[20,24,256]{2,1,0:T(8,128)S(1)}) custom-call(f32[2,20,24,256]{3,2,1,0:T(8,128)S(1)} %copy-done.1, f32[20]{0:T(128)S(1)} %copy-done.2, f32[20]{0:T(128)S(1)} %collective-permute-done.profile.profile_other, f32[2,24,256]{2,1,0:T(8,128)S(1)} %add_multiply_fusion.factors, ...), custom_call_target="tpu_custom_call" | custom-call | tf_op jit(solution)/shard_map/pallas_call | solution.py:485
  21.1 0.1 collective-permute-start.8
  21.2 2.0 %collective-permute-start.9 = (f32[8,128]{1,0:T(8,128)S(1)}, f32[8,128]{1,0:T(8,128)S(1)}, u32[]{:S(2)}, u32[]{:S(2)}) collective-permute-start(f32[8,128]{1,0:T(8,128)S(1)} %add_add_fusion._), channel_id=1, source_target_pairs={{0,4},{4,0},{8,12},{12,8},{1,5},{5,1},{9,13},{13,9},{2,6},{6,2},{1... | collective-permute-start | bytes 12296 | tf_op jit(solution)/shard_map/ppermute | solution.py:66
  23.2 1.7 %collective-permute-done.9 = f32[8,128]{1,0:T(8,128)S(1)} collective-permute-done((f32[8,128]{1,0:T(8,128)S(1)}, f32[8,128]{1,0:T(8,128)S(1)}, u32[]{:S(2)}, u32[]{:S(2)}) %collective-permute-start.9) | collective-permute-done | bytes 4128 | tf_op jit(solution)/shard_map/ppermute | solution.py:66
  24.8 3.2 %collective-permute-start.10 = (f32[8,128]{1,0:T(8,128)S(1)}, f32[8,128]{1,0:T(8,128)S(1)}, u32[]{:S(2)}, u32[]{:S(2)}) collective-permute-start(f32[8,128]{1,0:T(8,128)S(1)} %add.31), channel_id=1, source_target_pairs={{0,8},{4,12},{8,0},{12,4},{1,9},{5,13},{9,1},{13,5},{2,10},{6,14},... | collective-permute-start | bytes 12296 | tf_op jit(solution)/shard_map/ppermute | solution.py:66
  28.1 1.6 %collective-permute-done.10 = f32[8,128]{1,0:T(8,128)S(1)} collective-permute-done((f32[8,128]{1,0:T(8,128)S(1)}, f32[8,128]{1,0:T(8,128)S(1)}, u32[]{:S(2)}, u32[]{:S(2)}) %collective-permute-start.10) | collective-permute-done | bytes 4128 | tf_op jit(solution)/shard_map/ppermute | solution.py:66
  29.7 0.0 collective-permute-done.8.received
  29.7 1.8 %final.1 = f32[2,20,24,256]{3,2,1,0:T(8,128)} custom-call(f32[2,20,24,256]{3,2,1,0:T(8,128)S(1)} %get-tuple-element.70.base, f32[20,24,256]{2,1,0:T(8,128)S(1)} %get-tuple-element.71.kept, f32[20,24,256]{2,1,0:T(8,128)S(1)} %collective-permute-done.8.received, f32[8,128]{1,0:T(8,128)S(1)} %add.32.sums), custom_call_target="tpu_custom_call" | custom-call | tf_op jit(solution)/shard_map/final/pallas_call | solution.py:563
  (6 shorter events, 0.0 us)
Async XLA Ops:
  0.0 3.7 %collective-permute-start.1 = (f32[2,20,24,256]{3,2,1,0:T(8,128)}, f32[2,20,24,256]{3,2,1,0:T(8,128)S(1)}, u32[]{:S(2)}, u32[]{:S(2)}) collective-permute-start(f32[2,20,24,256]{3,2,1,0:T(8,128)} %source.3), channel_id=1, source_target_pairs={{0,1},{1,0},{2,3},{3,2},{4,5},{5,4},{6,7},{7,6},{8,9},{9,8},{10,11... | collective-permute-start | bytes 2949128 | tf_op jit(solution)/shard_map/ppermute | solution.py:503
  0.5 3.2 %collective-permute-start = (f32[20]{0:T(128)}, f32[20]{0:T(128)S(1)}, u32[]{:S(2)}, u32[]{:S(2)}) collective-permute-start(f32[20]{0:T(128)} %profile_own.1), channel_id=1, source_target_pairs={{0,1},{1,0},{2,3},{3,2},{4,5},{5,4},{6,7},{7,6},{8,9},{9,8},{10,11... | collective-permute-start | bytes 248 | tf_op jit(solution)/shard_map/ppermute | solution.py:504
  0.5 0.8 %copy-start.2 = (f32[20]{0:T(128)S(1)}, f32[20]{0:T(128)}, u32[]{:S(2)}) copy-start(f32[20]{0:T(128)} %profile_own.1) | copy-start | bytes 244
  1.4 1.2 %copy-start = (f32[2,20,24,256]{3,2,1,0:T(8,128)S(1)}, f32[2,20,24,256]{3,2,1,0:T(8,128)}, u32[]{:S(2)}) copy-start(f32[2,20,24,256]{3,2,1,0:T(8,128)} %source.3) | copy-start | bytes 2949124
  4.8 4.8 %collective-permute-start.2 = (f32[48,128]{1,0:T(8,128)S(1)}, f32[48,128]{1,0:T(8,128)S(1)}, u32[]{:S(2)}, u32[]{:S(2)}) collective-permute-start(f32[48,128]{1,0:T(8,128)S(1)} %broadcast_select_fusion), channel_id=1, source_target_pairs={{0,2},{1,3},{2,0},{3,1},{4,6},{5,7},{6,4},{7,5},{8,10},{9,11},{10,... | collective-permute-start | bytes 73736 | tf_op jit(solution)/shard_map/ppermute | solution.py:42
  9.7 4.8 %collective-permute-start.3 = (f32[168,128]{1,0:T(8,128)S(1)}, f32[168,128]{1,0:T(8,128)S(1)}, u32[]{:S(2)}, u32[]{:S(2)}) collective-permute-start(f32[168,128]{1,0:T(8,128)S(1)} %get-tuple-element.55), channel_id=1, source_target_pairs={{0,4},{1,5},{4,0},{5,1},{8,12},{9,13},{12,8},{13,9},{2,6},{3,7},{6... | collective-permute-start | bytes 258056 | tf_op jit(solution)/shard_map/ppermute | solution.py:42
  11.9 2.6 %collective-permute-start.4 = (f32[168,128]{1,0:T(8,128)S(1)}, f32[168,128]{1,0:T(8,128)S(1)}, u32[]{:S(2)}, u32[]{:S(2)}) collective-permute-start(f32[168,128]{1,0:T(8,128)S(1)} %get-tuple-element.56), channel_id=1, source_target_pairs={{0,1},{1,0},{4,8},{5,9},{8,4},{9,5},{12,13},{13,12},{2,3},{3,2},{6... | collective-permute-start | bytes 258056 | tf_op jit(solution)/shard_map/ppermute | solution.py:42
  12.7 7.3 %copy-start.1 = (f32[2,20,24,256]{3,2,1,0:T(8,128)S(1)}, f32[2,20,24,256]{3,2,1,0:T(8,128)}, u32[]{:S(2)}) copy-start(f32[2,20,24,256]{3,2,1,0:T(8,128)} %source.3) | copy-start | bytes 2949124
  14.7 3.1 %collective-permute-start.7 = (f32[8,128]{1,0:T(8,128)S(1)}, f32[8,128]{1,0:T(8,128)S(1)}, u32[]{:S(2)}, u32[]{:S(2)}) collective-permute-start(f32[8,128]{1,0:T(8,128)S(1)} %get-tuple-element.69), channel_id=1, source_target_pairs={{0,3},{1,2},{2,1},{3,0},{4,7},{5,6},{6,5},{7,4},{8,11},{9,10},{10,... | collective-permute-start | bytes 12296 | tf_op jit(solution)/shard_map/ppermute | solution.py:66
  16.4 3.6 %collective-permute-start.6 = (f32[8,128]{1,0:T(8,128)S(1)}, f32[8,128]{1,0:T(8,128)S(1)}, u32[]{:S(2)}, u32[]{:S(2)}) collective-permute-start(f32[8,128]{1,0:T(8,128)S(1)} %get-tuple-element.69), channel_id=1, source_target_pairs={{0,2},{2,0},{1,3},{3,1},{4,6},{6,4},{5,7},{7,5},{8,10},{10,8},{9,1... | collective-permute-start | bytes 12296 | tf_op jit(solution)/shard_map/ppermute | solution.py:66
  16.9 3.1 %collective-permute-start.5 = (f32[8,128]{1,0:T(8,128)S(1)}, f32[8,128]{1,0:T(8,128)S(1)}, u32[]{:S(2)}, u32[]{:S(2)}) collective-permute-start(f32[8,128]{1,0:T(8,128)S(1)} %get-tuple-element.69), channel_id=1, source_target_pairs={{0,1},{1,0},{2,3},{3,2},{4,5},{5,4},{6,7},{7,6},{8,9},{9,8},{10,11... | collective-permute-start | bytes 12296 | tf_op jit(solution)/shard_map/ppermute | solution.py:66
  21.1 8.6 %collective-permute-start.8 = (f32[20,24,256]{2,1,0:T(8,128)S(1)}, f32[20,24,256]{2,1,0:T(8,128)S(1)}, u32[]{:S(2)}, u32[]{:S(2)}) collective-permute-start(f32[20,24,256]{2,1,0:T(8,128)S(1)} %get-tuple-element.72), channel_id=1, source_target_pairs={{0,1},{1,0},{2,3},{3,2},{4,5},{5,4},{6,7},{7,6},{8,9},{9,8},{10,11... | collective-permute-start | bytes 1474568 | tf_op jit(solution)/shard_map/ppermute | solution.py:560
  21.2 3.7 %collective-permute-start.9 = (f32[8,128]{1,0:T(8,128)S(1)}, f32[8,128]{1,0:T(8,128)S(1)}, u32[]{:S(2)}, u32[]{:S(2)}) collective-permute-start(f32[8,128]{1,0:T(8,128)S(1)} %add_add_fusion._), channel_id=1, source_target_pairs={{0,4},{4,0},{8,12},{12,8},{1,5},{5,1},{9,13},{13,9},{2,6},{6,2},{1... | collective-permute-start | bytes 12296 | tf_op jit(solution)/shard_map/ppermute | solution.py:66
  24.8 4.8 %collective-permute-start.10 = (f32[8,128]{1,0:T(8,128)S(1)}, f32[8,128]{1,0:T(8,128)S(1)}, u32[]{:S(2)}, u32[]{:S(2)}) collective-permute-start(f32[8,128]{1,0:T(8,128)S(1)} %add.31), channel_id=1, source_target_pairs={{0,8},{4,12},{8,0},{12,4},{1,9},{5,13},{9,1},{13,5},{2,10},{6,14},... | collective-permute-start | bytes 12296 | tf_op jit(solution)/shard_map/ppermute | solution.py:66

commit v6 on v5

--- a/solution.py
+++ b/solution.py
@@ -17,6 +17,9 @@
 
 LANES = 128
 GRANT = 8 << 20
+OWN_GRANT = 53_750_000
+CHUNKS = 4
+PIECES = 4
 
 
 def line_pairs(count, first):
@@ -145,84 +148,98 @@
             high[pl.ds(i * count + k, 1), :] = tile[rows - 1 : rows]
 
 
-def weigh(base, read, profile, columns, carry, refs):
+def weigh(k, forcing, level, columns, refs):
     weighted, gain, strip_low, strip_high, prof = refs
-    rows, width = columns.shape
-    count, tiles = weighted.shape[0], width // LANES
-    lane = iota((rows, LANES), 1)
+    count, tiles = weighted.shape[0], len(forcing)
+    parts = []
+    for i, (y, column) in enumerate(zip(forcing, columns)):
+        g, _ = gains(level * column)
+        u = g * y
+        weighted[k, :, i * LANES : (i + 1) * LANES] = u
+        gain[k, :, i * LANES : (i + 1) * LANES] = g
+        strip_low[pl.ds((tiles + i) * count + k, 1), :] = u[1:2]
+        parts.append(u)
+    keep_rows(k, parts, strip_low, strip_high, count)
+    prof[pl.ds(k, 1), :] = level
+    return parts, dot(parts, forcing)
+
+
+def level_rows(profile, rows):
+    line = profile[...][None]
+    square = (rows.shape[0], line.shape[1])
+    column = jnp.sum(jnp.where(iota(square, 0) == iota(square, 1), line, 0.0), axis=1, keepdims=True)
+    rows[...] = jnp.broadcast_to(column, rows.shape)
+
+
+def weigh_planes(start, stop, unroll, base, read, levels_at, columns, carry, refs):
+    lane = iota(columns[0].shape, 1)
 
     def step(at, carry):
         first, second, last, acc = carry
         k = base + at
-        g, _ = gains(profile[at] * columns)
-        forcing = source_scale * read(at)
-        u = g * forcing
-        weighted[k] = u
-        gain[k] = g
-        parts = tiles_of(u)
-        keep_rows(k, parts, strip_low, strip_high, count)
-        for i, part in enumerate(parts):
-            strip_low[pl.ds((tiles + i) * count + k, 1), :] = part[1:2]
-        prof[pl.ds(k, 1), :] = jnp.full((1, LANES), profile[at])
+        forcing = [source_scale * tile for tile in tiles_of(read(at))]
+        parts, share = weigh(k, forcing, levels_at[pl.ds(at, 1), :], columns, refs)
         first = jnp.where(lane == k, pltpu.roll(parts[0], k, 1), first)
-        second = jnp.where(lane == k, pltpu.roll(parts[0], lax.rem(k + LANES - 1, LANES), 1), second)
+        at_second = k + LANES // 2
+        second = jnp.where(lane == at_second, pltpu.roll(parts[0], at_second - 1, 1), second)
         last = jnp.where(lane == k, pltpu.roll(parts[-1], k + 1, 1), last)
-        return first, second, last, acc + dot(parts, tiles_of(forcing))
-
-    return lax.fori_loop(0, weighted.shape[0] // 2, step, carry, unroll=5)
+        return first, second, last, acc + share
+
+    return lax.fori_loop(start, stop, step, carry, unroll=unroll)
 
 
 def own_kernel(
-    source, profile, factors, weighted, gain, strip_low, strip_high, cols_low, cols_high, prof, sums
+    held, profile, factors, weighted, gain, strip_low, strip_high, cols_low, cols_high, prof, sums, plane, levels_at, arrived
 ):
     layer = lax.axis_index("layer")
-    half, rows, width = source.shape[1:]
+    half, rows, width = plane.shape
     count, tiles = 2 * half, width // LANES
-    columns = factors[layer]
+    size = half // CHUNKS
+    parts = [slice(i * size, (i + 1) * size) for i in range(CHUNKS)]
+    copies = [pltpu.make_async_copy(held.at[layer, part], plane.at[part], arrived.at[i]) for i, part in enumerate(parts)]
+    for copy in copies:
+        copy.start()
+    columns = tiles_of(factors[layer])
+    level_rows(profile, levels_at)
     lane = iota((rows, LANES), 1)
+    for i, tile in enumerate(columns):
+        strip_low[2 * tiles * count + 2 + i : 2 * tiles * count + 3 + i, :] = tile[0:1]
     zeros = jnp.zeros((rows, LANES), jnp.float32)
-    edge = tiles_of(columns)
-    carry = (jnp.where(lane == LANES - 1, turned(edge[0], -1, 1), 0.0), zeros, zeros, jnp.zeros((8, LANES), jnp.float32))
-    for i, tile in enumerate(edge):
-        strip_low[2 * tiles * count + 2 + i : 2 * tiles * count + 3 + i, :] = tile[0:1]
-    first, second, last, acc = weigh(
-        layer * half,
-        lambda at: source[layer, at],
-        profile,
-        columns,
-        carry,
-        (weighted, gain, strip_low, strip_high, prof),
-    )
-    cols_low[0:rows] = first
-    cols_low[rows:] = second
-    cols_high[0:rows] = last
-    cols_high[rows:] = jnp.zeros_like(last)
-    sums[...] = acc
+    edge = jnp.where(lane == LANES - 1, turned(columns[0], -1, 1), 0.0)
+    carry = (edge, zeros, zeros, jnp.zeros((8, LANES), jnp.float32))
+    refs = (weighted, gain, strip_low, strip_high, prof)
+    for part, copy in zip(parts, copies):
+        copy.wait()
+        carry = weigh_planes(
+            part.start, part.stop, size, layer * half, lambda at: plane[at], levels_at, columns, carry, refs
+        )
+    first, second, cols_high[...], sums[...] = carry
+    cols_low[...] = first + second
 
 
 def other_kernel(source, profile, factors, *refs):
-    low, high, acc = refs[4], refs[5], refs[7]
-    weighted, gain, strip_low, strip_high, cols_low, cols_high, prof, sums = refs[8:]
+    weighted, gain, strip_low, strip_high, cols_low, cols_high, prof, sums, levels_at = refs[8:]
     layer = lax.axis_index("layer")
-    half, rows = source.shape[1:3]
-    carry = (low[0:rows], low[rows:], high[0:rows], acc[...])
-    first, second, last, acc = weigh(
+    half = source.shape[1]
+    columns = tiles_of(factors[layer])
+    level_rows(profile, levels_at)
+    zeros = jnp.zeros(columns[0].shape, jnp.float32)
+    first, second, cols_high[...], sums[...] = weigh_planes(
+        0,
+        half,
+        5,
         (1 - layer) * half,
         lambda at: source[layer, at],
-        profile,
-        factors[layer],
-        carry,
+        levels_at,
+        columns,
+        (refs[4][...], zeros, refs[5][...], refs[7][...]),
         (weighted, gain, strip_low, strip_high, prof),
     )
-    cols_low[0:rows] = first
-    cols_low[rows:] = second
-    cols_high[0:rows] = last
-    cols_high[rows:] = jnp.zeros_like(last)
-    sums[...] = acc
+    cols_low[...] = first + second
 
 
 def join_kernel(nr, strip_low, strip_high, pair_cols, other_cols, for_pairs, for_others):
-    rows = pair_cols.shape[0] // 2
+    rows = pair_cols.shape[0]
     low_cols, high_cols = halves(pair_cols[...], other_cols[...], "col")
     at = iota(strip_low.shape, 0)
     low, high = strip_low[...], strip_high[...]
@@ -285,7 +302,7 @@
 def inner_kernel(begun, weighted, gain, pair_cols, other_cols, image, q_low, q_high, k_low, k_high, pack, sums, again):
     count, rows, width = weighted.shape
     lane = iota((rows, LANES), 1)
-    low, high = halves(pair_cols[0:rows], other_cols[0:rows], "col")
+    low, high = halves(pair_cols[...], other_cols[...], "col")
     add_low = near(jnp.where(lane < count, low, 0.0), 1)
     add_high = near(jnp.where(lane < count, high, 0.0), 1)
     one = jnp.zeros((8, LANES), jnp.float32)
@@ -334,7 +351,7 @@
     k_low,
     k_high,
     pack,
-    cols_high,
+    last,
     pair_cols,
     other_cols,
     prof,
@@ -396,12 +413,12 @@
 
     lane, row = iota((rows, LANES), 1), iota((rows, LANES), 0)
     held = lane < count
-    u_next = jnp.where(held, high_cols[0:rows], 0.0)
+    u_next = jnp.where(held, high_cols, 0.0)
     up = jnp.where(row == 0, jnp.where(held, low[2 * nr + 1 : 2 * nr + 2], 0.0), turned(u_next, 1, 0))
     down = jnp.where(row == rows - 1, jnp.where(held, high[2 * nr + 1 : 2 * nr + 2], 0.0), turned(u_next, -1, 0))
-    side = cols_high[0:rows] + high_cols[rows:] + up + down
+    side = last[...] + jnp.where(held, turned(high_cols, LANES // 2, 1), 0.0) + up + down
     q_next = side + shifts(weight_vert * u_next + weight_cross * side, 1)
-    g, _ = gains(to_line(level) * high_cols[0:rows, LANES - 1 :])
+    g, _ = gains(to_line(level) * high_cols[:, LANES - 1 :])
     ub = pack[...]
     ub = ub + jnp.where(row == 0, to_line(e_low[-1][:, LANES - 1 :]), 0.0)
     ub = ub + jnp.where(row == rows - 1, to_line(e_high[-1][:, LANES - 1 :]), 0.0)
@@ -413,9 +430,9 @@
         out[pl.ds(2 * i + layer, 1), :] = jnp.sum(values, axis=0, keepdims=True)
 
 
-def ready_kernel(source, profile_own, profile_other, factors, image, add_low, add_high, _, base, kept, sent):
+def ready_kernel(source, prof, factors, image, add_low, add_high, _, base, kept, sent):
     layer = lax.axis_index("layer")
-    half, rows, _ = source.shape[1:]
+    half, rows, width = source.shape[1:]
     count = 2 * half
     mine, theirs = factors[layer], factors[1 - layer]
     row = iota((rows, LANES), 0)
@@ -427,54 +444,53 @@
             q = q + jnp.where(row == rows - 1, add_high[pl.ds(i * count + k, 1), :], 0.0)
             ref[where, :, i * LANES : (i + 1) * LANES] = scale[i] * q
 
+    def level(k):
+        return jnp.broadcast_to(prof[pl.ds(k, 1), 0:1], (rows, width))
+
     def step(at, _):
-        _, scale = gains(profile_other[at] * mine)
-        store(sent, at, scale, (1 - layer) * half + at)
-        _, scale = gains(profile_own[at] * mine)
-        store(kept, at, scale, layer * half + at)
+        here, there = layer * half + at, (1 - layer) * half + at
+        _, scale = gains(level(there) * mine)
+        store(sent, at, scale, there)
+        _, scale = gains(level(here) * mine)
+        store(kept, at, scale, here)
         base[layer, at] = scale * (source_scale * source[layer, at])
-        _, scale = gains(profile_own[at] * theirs)
+        _, scale = gains(level(here) * theirs)
         base[1 - layer, at] = scale * (source_scale * source[1 - layer, at])
         return 0
 
     lax.fori_loop(0, half, step, 0, unroll=4)
 
 
-def final_kernel(base, kept, received, sums, out, factors):
+def final_kernel(base, kept, received, sums, out, filled, left):
     layer = lax.axis_index("layer")
-    which, at = pl.program_id(0), pl.program_id(1)
-    size, rows, width = out.shape[1:]
-
-    @pl.when((which == 0) & (at == 0))
-    def _():
-        values = jnp.sum(sums[...], axis=1, keepdims=True)
-        zz, zb, bb, bbb = (values[2 * i : 2 * i + 2] for i in range(4))
-        delta = zz - zb
-        alpha = zz / delta
-        rest = -zb / delta
-        beta = (zz * bb - zb * zb) / (delta * delta)
-        gamma = zz * beta
-        delta_next = gamma - (rest * rest * zb + 2.0 * alpha * rest * bb + alpha * alpha * bbb)
-        alpha_next = gamma / (delta_next - beta * gamma / alpha)
-        factors[0] = jnp.broadcast_to(alpha + alpha_next * (rest + beta), (2, LANES))
-        factors[1] = jnp.broadcast_to(alpha_next * alpha, (2, LANES))
-
-    first = factors[0, pl.ds(which, 1), :][:, 0:1]
-    second = factors[1, pl.ds(which, 1), :][:, 0:1]
-    first, second = jnp.broadcast_to(first, (rows, width)), jnp.broadcast_to(second, (rows, width))
-
-    def fill(image):
-        for i in range(size):
-            k = at * size + i
-            out[0, i] = first * base[which, k] + second * image[k]
-
-    @pl.when(which == layer)
-    def _():
-        fill(kept)
-
-    @pl.when(which != layer)
-    def _():
-        fill(received)
+    half = base.shape[1]
+    size = half // PIECES
+    values = jnp.sum(sums[...], axis=1, keepdims=True)
+    zz, zb, bb, bbb = (values[2 * i : 2 * i + 2] for i in range(4))
+    delta = zz - zb
+    alpha = zz / delta
+    rest = -zb / delta
+    beta = (zz * bb - zb * zb) / (delta * delta)
+    gamma = zz * beta
+    delta_next = gamma - (rest * rest * zb + 2.0 * alpha * rest * bb + alpha * alpha * bbb)
+    alpha_next = gamma / (delta_next - beta * gamma / alpha)
+    first, second = alpha + alpha_next * (rest + beta), alpha_next * alpha
+    mine = iota((2, 1), 0) == layer
+    copies = []
+    for which, chosen, image in ((layer, mine, kept), (1 - layer, jnp.logical_not(mine), received)):
+        a, b = (
+            jnp.broadcast_to(jnp.sum(jnp.where(chosen, factor, 0.0), axis=0, keepdims=True), base.shape[2:])
+            for factor in (first, second)
+        )
+        for piece in range(PIECES):
+            for k in range(piece * size, (piece + 1) * size):
+                filled[which, k] = a * base[which, k] + b * image[k]
+            part = pl.ds(piece * size, size)
+            copy = pltpu.make_async_copy(filled.at[which, part], out.at[which, part], left.at[len(copies)])
+            copy.start()
+            copies.append(copy)
+    for copy in copies:
+        copy.wait()
 
 
 VMEM = pl.BlockSpec(memory_space=pltpu.VMEM)
@@ -497,19 +513,37 @@
 def solve(source, profile, column, terrain_height_error):
     copies, half, rows, width = source.shape
     count, tiles = 2 * half, width // LANES
-    assert lax.axis_size("layer") == copies == 2 and count < LANES and width % LANES == 0
-    assert count % 8 == 0 and rows % 8 == 0 and rows > 2
+    assert lax.axis_size("layer") == copies == 2 and count < LANES // 2 and width % LANES == 0
+    assert count % 8 == 0 and rows % 8 == 0 and rows > 2 and half % CHUNKS == half % PIECES == 0
     swap = [(0, 1), (1, 0)]
     other = lax.ppermute(source, "layer", swap)
     profile_other = lax.ppermute(profile, "layer", swap)
     nr = tiles * count
     block, row, pack = (count, rows, width), (nr, LANES), (rows, LANES)
     strip = (-(-(2 * nr + 2 + tiles) // 8) * 8, LANES)
-    shapes = [block, block, strip, strip, (2 * rows, LANES), (2 * rows, LANES), (count, LANES), (8, LANES)]
+    shapes = [block, block, strip, strip, pack, pack, (count, LANES), (8, LANES)]
+    lines = (-(-half // 8) * 8, LANES)
     factors = column * (1.0 + 0.002 * terrain_height_error.astype(jnp.float32))
-    begun = call(own_kernel, shapes, (source, profile, factors), (1,))
+    own = pl.pallas_call(
+        own_kernel,
+        out_shape=[jax.ShapeDtypeStruct(shape, jnp.float32) for shape in shapes],
+        in_specs=[pl.BlockSpec(memory_space=pltpu.HBM), VMEM, VMEM],
+        out_specs=[VMEM] * len(shapes),
+        scratch_shapes=[
+            pltpu.VMEM((half, rows, width), jnp.float32),
+            pltpu.VMEM(lines, jnp.float32),
+            pltpu.SemaphoreType.DMA((CHUNKS,)),
+        ],
+        compiler_params=pltpu.CompilerParams(vmem_limit_bytes=OWN_GRANT),
+        name="own",
+    )
+    begun = own(source, profile, factors)
     weighted, gain, strip_low, strip_high, cols_low, cols_high, prof, sum_zz = call(
-        other_kernel, shapes, (other, profile_other, factors, *begun), (1,), aliases={3 + i: i for i in range(8)}
+        other_kernel,
+        shapes,
+        (other, profile_other, factors, *begun),
+        scratch=(lines,),
+        aliases={3 + i: i for i in range(8)},
     )
     even = lax.axis_index("col") % 2 == 0
     pair_cols, other_cols = exchanged(
@@ -552,21 +586,16 @@
     part = (half, rows, width)
     sums, later = total(sums)
     base, kept, sent = call(
-        ready_kernel,
-        [source.shape, part, part],
-        (source, profile, profile_other, factors, image, add_low, add_high, sums),
-        (1, 2),
+        ready_kernel, [source.shape, part, part], (source, prof, factors, image, add_low, add_high, sums)
     )
     received = lax.ppermute(sent, "layer", swap)
     sums = later(sums)
-    size = half // 2 if half % 2 == 0 else half
     return pl.pallas_call(
         final_kernel,
         out_shape=jax.ShapeDtypeStruct(source.shape, jnp.float32),
-        grid=(2, half // size),
         in_specs=[VMEM] * 4,
-        out_specs=pl.BlockSpec((1, size, rows, width), lambda i, j: (i, j, 0, 0)),
-        scratch_shapes=[pltpu.VMEM((2, 2, LANES), jnp.float32)],
+        out_specs=pl.BlockSpec(memory_space=pltpu.HBM),
+        scratch_shapes=[pltpu.VMEM(source.shape, jnp.float32), pltpu.SemaphoreType.DMA((2 * PIECES,))],
         compiler_params=pltpu.CompilerParams(vmem_limit_bytes=GRANT),
         name="final",
     )(base, kept, received, sums)

time: 31.7 us -> 29.1 us (0.918)
  Pallas kernels: 7.92 us -> 6.71 us
  local copies, waits for them, and re-layouts: 1.21 us -> 0.01 us
    pallas_call x7 -> x6, Pallas kernels: 6.09 us -> 4.03 us  [call(): pl.pallas_call(kernel, out_shape=[jax.ShapeDtypeStruct(shape, jnp.float32...]
    pallas_call x0 -> x1, Pallas kernels: none -> 1.47 us  [solve(): begun = own(source, profile, factors)]
    unnamed x6 -> x4, local copies, waits for them, and re-layouts: 1.21 us -> 0.01 us
    pallas_call x1, Pallas kernels: 1.82 us -> 1.21 us  [solve(): pl.pallas_call(final_kernel, out_shape=jax.ShapeDtypeStruct(source.shape,...]
  transfers between devices with their start and end apart: 11 -> 11, of which waited for: 5 -> 6; matrix products, arithmetic and copies ran while one was open for 3% -> 3% of each run, Pallas kernels for 12% -> 14%
where the time goes in v6:
time: 29.1 us; the launch traced here: 29 us
  starting transfers between devices  13.2 us (45%)
  waiting for transfers between devices  8.08 us (28%)
  Pallas kernels  6.71 us (23%)
  other arithmetic  0.84 us (3%)
    ppermute x5, starting transfers between devices, flipped(): return lax.ppermute(values, axes, pairs)  7.43 us
    ppermute x5, waiting for transfers between devices, flipped(): return lax.ppermute(values, axes, pairs)  6.34 us
    ppermute x3, starting transfers between devices, exchanged(): received.append(lax.ppermute(values, (axis, 'layer'), pairs))  5.17 us
    pallas_call x6, Pallas kernels, call(): pl.pallas_call(kernel, out_shape=[jax.ShapeDtypeStruct(shape, jnp.float32...  4.03 us
    ppermute x3, waiting for transfers between devices, exchanged(): received.append(lax.ppermute(values, (axis, 'layer'), pairs))  1.68 us
    pallas_call x1, Pallas kernels, solve(): begun = own(source, profile, factors)  1.47 us
    pallas_call x1, Pallas kernels, solve(): pl.pallas_call(final_kernel, out_shape=jax.ShapeDtypeStruct(source.shape,...  1.21 us
    mul x1, other arithmetic, solve(): factors = column * (1.0 + 0.002 * terrain_height_error.astype(jnp.float32))  0.82 us
  transfers between devices with their start and end apart: 11, of which 6 were waited for; matrix products, arithmetic and copies ran while one was open for 3% of the time, Pallas kernels for 14%

profile of v6, /device:TPU:0, one launch (start us, length us, event | category | flops | bytes accessed | tf_op | source)
XLA Modules:
  0.0 29.0 jit_solution(64208999676668345)
XLA Ops:
  0.0 0.5 %collective-permute-start = (f32[2,20,24,256]{3,2,1,0:T(8,128)}, f32[2,20,24,256]{3,2,1,0:T(8,128)S(1)}, u32[]{:S(2)}, u32[]{:S(2)}) collective-permute-start(f32[2,20,24,256]{3,2,1,0:T(8,128)} %source.1), channel_id=1, source_target_pairs={{0,1},{1,0},{2,3},{3,2},{4,5},{5,4},{6,7},{7,6},{8,9},{9,8},{10,11... | collective-permute-start | bytes 2949128 | tf_op jit(solution)/shard_map/ppermute | solution.py:519
  0.5 0.0 collective-permute-start.1
  0.5 0.0 copy-start.1
  0.5 0.8 %add_multiply_fusion.factors = f32[2,24,256]{2,1,0:T(8,128)S(1)} fusion(s32[2,24,256]{2,1,0:T(8,128)} %param.7, f32[24,256]{1,0:T(8,128)} %param.6), kind=kLoop, calls=%fused_computation | loop fusion | flops 49152 | bytes 122880 | tf_op jit(solution)/shard_map/mul | solution.py:526
  1.3 0.0 copy-done.1
  1.4 1.5 %own.1 = (f32[40,24,256]{2,1,0:T(8,128)S(1)}, f32[40,24,256]{2,1,0:T(8,128)S(1)}, f32[168,128]{1,0:T(8,128)S(1)}, f32[168,128]{1,0:T(8,128)S(1)}, f32[24,128]{1,...) custom-call(f32[2,20,24,256]{3,2,1,0:T(8,128)} %source.1, f32[20]{0:T(128)S(1)} %copy-done.1, ...), custom_call_target="tpu_custom_call" | custom-call | tf_op jit(solution)/shard_map/own/pallas_call | solution.py:540
  2.8 0.1 collective-permute-done.1.profile
  2.9 0.0 collective-permute-done.source
  2.9 0.6 %shard_map.46 = (f32[40,24,256]{2,1,0:T(8,128)S(1)}, f32[40,24,256]{2,1,0:T(8,128)S(1)}, f32[168,128]{1,0:T(8,128)S(1)}, f32[168,128]{1,0:T(8,128)S(1)}, f32[24,...) custom-call(f32[2,20,24,256]{3,2,1,0:T(8,128)S(1)} %collective-permu, ...), custom_call_target="tpu_custom_call", output_to_operand_aliasing={{0}: (3, {}), {1}: (4, {}), {2}: (5, {}), {3}: (6, {}), {4}... | custom-call | tf_op jit(solution)/shard_map/pallas_call | solution.py:501
  3.5 3.0 %collective-permute-start.2 = (f32[24,128]{1,0:T(8,128)S(1)}, f32[24,128]{1,0:T(8,128)S(1)}, u32[]{:S(2)}, u32[]{:S(2)}) collective-permute-start(f32[24,128]{1,0:T(8,128)S(1)} %broadcast_select_fusion), channel_id=1, source_target_pairs={{0,2},{1,3},{2,0},{3,1},{4,6},{5,7},{6,4},{7,5},{8,10},{9,11},{10,... | collective-permute-start | bytes 36872 | tf_op jit(solution)/shard_map/ppermute | solution.py:45
  6.5 1.7 %collective-permute-done.2.pair_cols = f32[24,128]{1,0:T(8,128)S(1)} collective-permute-done((f32[24,128]{1,0:T(8,128)S(1)}, f32[24,128]{1,0:T(8,128)S(1)}, u32[]{:S(2)}, u32[]{:S(2)}) %collective-permute-start.2) | collective-permute-done | bytes 12320 | tf_op jit(solution)/shard_map/ppermute | solution.py:45
  8.2 2.2 %collective-permute-start.3 = (f32[168,128]{1,0:T(8,128)S(1)}, f32[168,128]{1,0:T(8,128)S(1)}, u32[]{:S(2)}, u32[]{:S(2)}) collective-permute-start(f32[168,128]{1,0:T(8,128)S(1)} %get-tuple-element.56), channel_id=1, source_target_pairs={{0,4},{1,5},{4,0},{5,1},{8,12},{9,13},{12,8},{13,9},{2,6},{3,7},{6... | collective-permute-start | bytes 258056 | tf_op jit(solution)/shard_map/ppermute | solution.py:45
  10.4 0.0 collective-permute-start.4
  10.4 0.8 %shard_map.47 = (f32[40,24,256]{2,1,0:T(8,128)S(1)}, f32[80,128]{1,0:T(8,128)S(1)}, f32[80,128]{1,0:T(8,128)S(1)}) custom-call(f32[40,24,256]{2,1,0:T(8,128)S(1)} %get-tuple-element.48.weighted, f32[40,24,256]{2,1,0:T(8,128)S(1)} %get-tuple-element.49.gain), custom_call_target="tpu_custom_call" | custom-call | tf_op jit(solution)/shard_map/pallas_call | solution.py:501
  11.2 0.0 copy-start
  11.2 1.8 %shard_map.48 = (f32[40,24,256]{2,1,0:T(8,128)S(1)}, f32[80,128]{1,0:T(8,128)S(1)}, f32[80,128]{1,0:T(8,128)S(1)}, f32[80,128]{1,0:T(8,128)S(1)}, f32[80,128]{1,...) custom-call(f32[40,24,256]{2,1,0:T(8,128)S(1)} %get-tuple-element.50.begun, ...), custom_call_target="tpu_custom_call" | custom-call | tf_op jit(solution)/shard_map/pallas_call | solution.py:501
  13.0 0.0 collective-permute-done.3.pair_strip
  13.0 0.0 collective-permute-done.4.other_strip
  13.0 0.3 shard_map.50
  13.3 1.7 %collective-permute-start.7 = (f32[8,128]{1,0:T(8,128)S(1)}, f32[8,128]{1,0:T(8,128)S(1)}, u32[]{:S(2)}, u32[]{:S(2)}) collective-permute-start(f32[8,128]{1,0:T(8,128)S(1)} %get-tuple-element.69), channel_id=1, source_target_pairs={{0,3},{1,2},{2,1},{3,0},{4,7},{5,6},{6,5},{7,4},{8,11},{9,10},{10,... | collective-permute-start | bytes 12296 | tf_op jit(solution)/shard_map/ppermute | solution.py:69
  15.0 0.5 %collective-permute-start.6 = (f32[8,128]{1,0:T(8,128)S(1)}, f32[8,128]{1,0:T(8,128)S(1)}, u32[]{:S(2)}, u32[]{:S(2)}) collective-permute-start(f32[8,128]{1,0:T(8,128)S(1)} %get-tuple-element.69), channel_id=1, source_target_pairs={{0,2},{2,0},{1,3},{3,1},{4,6},{6,4},{5,7},{7,5},{8,10},{10,8},{9,1... | collective-permute-start | bytes 12296 | tf_op jit(solution)/shard_map/ppermute | solution.py:69
  15.5 0.0 collective-permute-start.5
  15.5 0.9 %collective-permute-done.7 = f32[8,128]{1,0:T(8,128)S(1)} collective-permute-done((f32[8,128]{1,0:T(8,128)S(1)}, f32[8,128]{1,0:T(8,128)S(1)}, u32[]{:S(2)}, u32[]{:S(2)}) %collective-permute-start.7) | collective-permute-done | bytes 4128 | tf_op jit(solution)/shard_map/ppermute | solution.py:69
  16.4 2.2 %collective-permute-done.6 = f32[8,128]{1,0:T(8,128)S(1)} collective-permute-done((f32[8,128]{1,0:T(8,128)S(1)}, f32[8,128]{1,0:T(8,128)S(1)}, u32[]{:S(2)}, u32[]{:S(2)}) %collective-permute-start.6) | collective-permute-done | bytes 4128 | tf_op jit(solution)/shard_map/ppermute | solution.py:69
  18.6 0.0 collective-permute-done.5
  18.6 0.0 copy-done
  18.6 0.6 %shard_map.51 = (f32[2,20,24,256]{3,2,1,0:T(8,128)S(1)}, f32[20,24,256]{2,1,0:T(8,128)S(1)}, f32[20,24,256]{2,1,0:T(8,128)S(1)}) custom-call(f32[2,20,24,256]{3,2,1,0:T(8,128)S(1)} %copy-done, f32[40,128]{1,0:T(8,128)S(1)} %get-tuple-element.47.prof, f32[2,24,256]{2,1,0:T(8,128)S(1)} %add_multiply_fusion.factors, ...), custom_call_target="tpu_custom_call" | custom-call | tf_op jit(solution)/shard_map/pallas_call | solution.py:501
  19.2 0.1 collective-permute-start.8
  19.2 2.0 %collective-permute-start.9 = (f32[8,128]{1,0:T(8,128)S(1)}, f32[8,128]{1,0:T(8,128)S(1)}, u32[]{:S(2)}, u32[]{:S(2)}) collective-permute-start(f32[8,128]{1,0:T(8,128)S(1)} %add_add_fusion._), channel_id=1, source_target_pairs={{0,4},{4,0},{8,12},{12,8},{1,5},{5,1},{9,13},{13,9},{2,6},{6,2},{1... | collective-permute-start | bytes 12296 | tf_op jit(solution)/shard_map/ppermute | solution.py:69
  21.2 1.7 %collective-permute-done.9 = f32[8,128]{1,0:T(8,128)S(1)} collective-permute-done((f32[8,128]{1,0:T(8,128)S(1)}, f32[8,128]{1,0:T(8,128)S(1)}, u32[]{:S(2)}, u32[]{:S(2)}) %collective-permute-start.9) | collective-permute-done | bytes 4128 | tf_op jit(solution)/shard_map/ppermute | solution.py:69
  22.9 3.2 %collective-permute-start.10 = (f32[8,128]{1,0:T(8,128)S(1)}, f32[8,128]{1,0:T(8,128)S(1)}, u32[]{:S(2)}, u32[]{:S(2)}) collective-permute-start(f32[8,128]{1,0:T(8,128)S(1)} %add.31), channel_id=1, source_target_pairs={{0,8},{4,12},{8,0},{12,4},{1,9},{5,13},{9,1},{13,5},{2,10},{6,14},... | collective-permute-start | bytes 12296 | tf_op jit(solution)/shard_map/ppermute | solution.py:69
  26.2 1.6 %collective-permute-done.10 = f32[8,128]{1,0:T(8,128)S(1)} collective-permute-done((f32[8,128]{1,0:T(8,128)S(1)}, f32[8,128]{1,0:T(8,128)S(1)}, u32[]{:S(2)}, u32[]{:S(2)}) %collective-permute-start.10) | collective-permute-done | bytes 4128 | tf_op jit(solution)/shard_map/ppermute | solution.py:69
  27.7 0.0 collective-permute-done.8.received
  27.7 1.2 %final.1 = f32[2,20,24,256]{3,2,1,0:T(8,128)} custom-call(f32[2,20,24,256]{3,2,1,0:T(8,128)S(1)} %get-tuple-element.70.base, f32[20,24,256]{2,1,0:T(8,128)S(1)} %get-tuple-element.71.kept, f32[20,24,256]{2,1,0:T(8,128)S(1)} %collective-permute-done.8.received, f32[8,128]{1,0:T(8,128)S(1)} %add.32.sums), custom_call_target="tpu_custom_call" | custom-call | tf_op jit(solution)/shard_map/final/pallas_call | solution.py:593
  (6 shorter events, 0.0 us)
Async XLA Ops:
  0.0 2.9 %collective-permute-start = (f32[2,20,24,256]{3,2,1,0:T(8,128)}, f32[2,20,24,256]{3,2,1,0:T(8,128)S(1)}, u32[]{:S(2)}, u32[]{:S(2)}) collective-permute-start(f32[2,20,24,256]{3,2,1,0:T(8,128)} %source.1), channel_id=1, source_target_pairs={{0,1},{1,0},{2,3},{3,2},{4,5},{5,4},{6,7},{7,6},{8,9},{9,8},{10,11... | collective-permute-start | bytes 2949128 | tf_op jit(solution)/shard_map/ppermute | solution.py:519
  0.5 2.4 %collective-permute-start.1 = (f32[20]{0:T(128)}, f32[20]{0:T(128)S(1)}, u32[]{:S(2)}, u32[]{:S(2)}) collective-permute-start(f32[20]{0:T(128)} %profile.1), channel_id=1, source_target_pairs={{0,1},{1,0},{2,3},{3,2},{4,5},{5,4},{6,7},{7,6},{8,9},{9,8},{10,11... | collective-permute-start | bytes 248 | tf_op jit(solution)/shard_map/ppermute | solution.py:520
  0.5 0.8 %copy-start.1 = (f32[20]{0:T(128)S(1)}, f32[20]{0:T(128)}, u32[]{:S(2)}) copy-start(f32[20]{0:T(128)} %profile.1) | copy-start | bytes 244
  3.5 4.7 %collective-permute-start.2 = (f32[24,128]{1,0:T(8,128)S(1)}, f32[24,128]{1,0:T(8,128)S(1)}, u32[]{:S(2)}, u32[]{:S(2)}) collective-permute-start(f32[24,128]{1,0:T(8,128)S(1)} %broadcast_select_fusion), channel_id=1, source_target_pairs={{0,2},{1,3},{2,0},{3,1},{4,6},{5,7},{6,4},{7,5},{8,10},{9,11},{10,... | collective-permute-start | bytes 36872 | tf_op jit(solution)/shard_map/ppermute | solution.py:45
  8.2 4.8 %collective-permute-start.3 = (f32[168,128]{1,0:T(8,128)S(1)}, f32[168,128]{1,0:T(8,128)S(1)}, u32[]{:S(2)}, u32[]{:S(2)}) collective-permute-start(f32[168,128]{1,0:T(8,128)S(1)} %get-tuple-element.56), channel_id=1, source_target_pairs={{0,4},{1,5},{4,0},{5,1},{8,12},{9,13},{12,8},{13,9},{2,6},{3,7},{6... | collective-permute-start | bytes 258056 | tf_op jit(solution)/shard_map/ppermute | solution.py:45
  10.4 2.6 %collective-permute-start.4 = (f32[168,128]{1,0:T(8,128)S(1)}, f32[168,128]{1,0:T(8,128)S(1)}, u32[]{:S(2)}, u32[]{:S(2)}) collective-permute-start(f32[168,128]{1,0:T(8,128)S(1)} %get-tuple-element.57), channel_id=1, source_target_pairs={{0,1},{1,0},{4,8},{5,9},{8,4},{9,5},{12,13},{13,12},{2,3},{3,2},{6... | collective-permute-start | bytes 258056 | tf_op jit(solution)/shard_map/ppermute | solution.py:45
  11.2 7.4 %copy-start = (f32[2,20,24,256]{3,2,1,0:T(8,128)S(1)}, f32[2,20,24,256]{3,2,1,0:T(8,128)}, u32[]{:S(2)}) copy-start(f32[2,20,24,256]{3,2,1,0:T(8,128)} %source.1) | copy-start | bytes 2949124
  13.3 3.1 %collective-permute-start.7 = (f32[8,128]{1,0:T(8,128)S(1)}, f32[8,128]{1,0:T(8,128)S(1)}, u32[]{:S(2)}, u32[]{:S(2)}) collective-permute-start(f32[8,128]{1,0:T(8,128)S(1)} %get-tuple-element.69), channel_id=1, source_target_pairs={{0,3},{1,2},{2,1},{3,0},{4,7},{5,6},{6,5},{7,4},{8,11},{9,10},{10,... | collective-permute-start | bytes 12296 | tf_op jit(solution)/shard_map/ppermute | solution.py:69
  15.0 3.6 %collective-permute-start.6 = (f32[8,128]{1,0:T(8,128)S(1)}, f32[8,128]{1,0:T(8,128)S(1)}, u32[]{:S(2)}, u32[]{:S(2)}) collective-permute-start(f32[8,128]{1,0:T(8,128)S(1)} %get-tuple-element.69), channel_id=1, source_target_pairs={{0,2},{2,0},{1,3},{3,1},{4,6},{6,4},{5,7},{7,5},{8,10},{10,8},{9,1... | collective-permute-start | bytes 12296 | tf_op jit(solution)/shard_map/ppermute | solution.py:69
  15.5 3.1 %collective-permute-start.5 = (f32[8,128]{1,0:T(8,128)S(1)}, f32[8,128]{1,0:T(8,128)S(1)}, u32[]{:S(2)}, u32[]{:S(2)}) collective-permute-start(f32[8,128]{1,0:T(8,128)S(1)} %get-tuple-element.69), channel_id=1, source_target_pairs={{0,1},{1,0},{2,3},{3,2},{4,5},{5,4},{6,7},{7,6},{8,9},{9,8},{10,11... | collective-permute-start | bytes 12296 | tf_op jit(solution)/shard_map/ppermute | solution.py:69
  19.2 8.6 %collective-permute-start.8 = (f32[20,24,256]{2,1,0:T(8,128)S(1)}, f32[20,24,256]{2,1,0:T(8,128)S(1)}, u32[]{:S(2)}, u32[]{:S(2)}) collective-permute-start(f32[20,24,256]{2,1,0:T(8,128)S(1)} %get-tuple-element.72), channel_id=1, source_target_pairs={{0,1},{1,0},{2,3},{3,2},{4,5},{5,4},{6,7},{7,6},{8,9},{9,8},{10,11... | collective-permute-start | bytes 1474568 | tf_op jit(solution)/shard_map/ppermute | solution.py:591
  19.2 3.7 %collective-permute-start.9 = (f32[8,128]{1,0:T(8,128)S(1)}, f32[8,128]{1,0:T(8,128)S(1)}, u32[]{:S(2)}, u32[]{:S(2)}) collective-permute-start(f32[8,128]{1,0:T(8,128)S(1)} %add_add_fusion._), channel_id=1, source_target_pairs={{0,4},{4,0},{8,12},{12,8},{1,5},{5,1},{9,13},{13,9},{2,6},{6,2},{1... | collective-permute-start | bytes 12296 | tf_op jit(solution)/shard_map/ppermute | solution.py:69
  22.9 4.8 %collective-permute-start.10 = (f32[8,128]{1,0:T(8,128)S(1)}, f32[8,128]{1,0:T(8,128)S(1)}, u32[]{:S(2)}, u32[]{:S(2)}) collective-permute-start(f32[8,128]{1,0:T(8,128)S(1)} %add.31), channel_id=1, source_target_pairs={{0,8},{4,12},{8,0},{12,4},{1,9},{5,13},{9,1},{13,5},{2,10},{6,14},... | collective-permute-start | bytes 12296 | tf_op jit(solution)/shard_map/ppermute | solution.py:69

commit v7 on v6

--- a/solution.py
+++ b/solution.py
@@ -72,26 +72,21 @@
 def total(values):
     sizes = {axis: lax.axis_size(axis) for axis in ("layer", "col", "tile")}
     assert all(size & (size - 1) == 0 for size in sizes.values())
-    first = 1
-    if sizes["col"] > 1 and sizes["layer"] == 2:
-        values = (
-            values
-            + flipped(values, sizes, ("layer",), (1,))
-            + flipped(values, sizes, ("col",), (1,))
-            + flipped(values, sizes, ("col", "layer"), (1, 1))
-        )
-        first = 2
-    else:
-        values = values + flipped(values, sizes, ("layer",), (1,))
+    both = sizes["tile"] > 1
+    first = flipped(values, sizes, ("layer",), (1,))
+    if both:
+        first = first + flipped(values, sizes, ("tile",), (1,))
+        first = first + flipped(values, sizes, ("tile", "layer"), (1, 1))
 
     def later(values):
-        for axis, bit in (("col", first), ("tile", 1)):
+        values = values + first
+        for axis, bit in (("tile", 2 if both else 1), ("col", 2)):
             while bit < sizes[axis]:
                 values = values + flipped(values, sizes, (axis,), (bit,))
                 bit *= 2
         return values
 
-    return values, later
+    return later
 
 
 def tiles_of(plane):
@@ -203,7 +198,7 @@
     level_rows(profile, levels_at)
     lane = iota((rows, LANES), 1)
     for i, tile in enumerate(columns):
-        strip_low[2 * tiles * count + 2 + i : 2 * tiles * count + 3 + i, :] = tile[0:1]
+        strip_low[2 * tiles * count + i : 2 * tiles * count + i + 1, :] = tile[0:1]
     zeros = jnp.zeros((rows, LANES), jnp.float32)
     edge = jnp.where(lane == LANES - 1, turned(columns[0], -1, 1), 0.0)
     carry = (edge, zeros, zeros, jnp.zeros((8, LANES), jnp.float32))
@@ -236,18 +231,6 @@
         (weighted, gain, strip_low, strip_high, prof),
     )
     cols_low[...] = first + second
-
-
-def join_kernel(nr, strip_low, strip_high, pair_cols, other_cols, for_pairs, for_others):
-    rows = pair_cols.shape[0]
-    low_cols, high_cols = halves(pair_cols[...], other_cols[...], "col")
-    at = iota(strip_low.shape, 0)
-    low, high = strip_low[...], strip_high[...]
-    low = jnp.where(at == 2 * nr, low_cols[0:1], jnp.where(at == 2 * nr + 1, high_cols[0:1], low))
-    high = jnp.where(at == 2 * nr + 1, high_cols[rows - 1 : rows], high)
-    even = lax.axis_index("tile") % 2 == 0
-    for_pairs[...] = jnp.where(even, high, low)
-    for_others[...] = jnp.where(even, low, high)
 
 
 def shifts(values, axis):
@@ -374,9 +357,6 @@
     shape = (count, LANES)
     diagonal = iota(shape, 0) == iota(shape, 1)
 
-    def to_column(line):
-        return jnp.sum(jnp.where(diagonal, line, 0.0), axis=1, keepdims=True)
-
     def to_line(column):
         return jnp.sum(jnp.where(diagonal, column, 0.0), axis=0, keepdims=True)
 
@@ -400,22 +380,24 @@
         bb = bb + total(e, [2.0 * a + b for a, b in zip(q, h)])
         bbb = bbb + total(e, [2.0 * a + b for a, b in zip(ka, ke)])
         outer.append((u, e, [a * b + c for a, b, c in zip(g, q, e)]))
-    (_, e_low, _), (u_last, e_high, ub_last) = outer
+    (_, e_low, ub_first), (u_last, e_high, ub_last) = outer
+    corners = [to_line(high[(tiles - 1) * count : tiles * count][:, LANES - 1 :])]
+    corners += [to_line(values[0:count][:, 0:1]) for values in (high, low)]
 
     u_next, u_after = blocks(high), blocks(high, nr)
-    side = along(u_next, to_column(high[2 * nr : 2 * nr + 1]), to_column(high[2 * nr + 1 : 2 * nr + 2]))
+    side = along(u_next, 0.0, 0.0)
     side = [s + a + b for s, a, b in zip(side, u_last, u_after)]
     q_next = [s + shifts(weight_vert * a + weight_cross * s, 0) for a, s in zip(u_next, side)]
     level = prof[...]
+    g_next = [gains(level * high[2 * nr + i : 2 * nr + i + 1])[0] for i in range(tiles)]
     for i in range(tiles):
-        g, _ = gains(level * high[2 * nr + 2 + i : 2 * nr + 3 + i])
-        bbb = bbb + 2.0 * folded(ub_last[i] * near(g * q_next[i], 0))
+        bbb = bbb + 2.0 * folded(ub_last[i] * near(g_next[i] * q_next[i], 0))
 
     lane, row = iota((rows, LANES), 1), iota((rows, LANES), 0)
     held = lane < count
     u_next = jnp.where(held, high_cols, 0.0)
-    up = jnp.where(row == 0, jnp.where(held, low[2 * nr + 1 : 2 * nr + 2], 0.0), turned(u_next, 1, 0))
-    down = jnp.where(row == rows - 1, jnp.where(held, high[2 * nr + 1 : 2 * nr + 2], 0.0), turned(u_next, -1, 0))
+    up = jnp.where(row == 0, 0.0, turned(u_next, 1, 0))
+    down = jnp.where(row == rows - 1, 0.0, turned(u_next, -1, 0))
     side = last[...] + jnp.where(held, turned(high_cols, LANES // 2, 1), 0.0) + up + down
     q_next = side + shifts(weight_vert * u_next + weight_cross * side, 1)
     g, _ = gains(to_line(level) * high_cols[:, LANES - 1 :])
@@ -424,10 +406,38 @@
     ub = ub + jnp.where(row == rows - 1, to_line(e_high[-1][:, LANES - 1 :]), 0.0)
     bbb = bbb + 2.0 * folded(ub * near(g * q_next, 1))
 
+    def twice(value, gain):
+        value, gain = jnp.broadcast_to(value, (8, LANES)), jnp.broadcast_to(gain, (8, LANES))
+        return near(gain * near(value, 1), 1)[0:1]
+
+    last_line, first_line = (to_line(ub[-1][:, LANES - 1 :]) for ub in (ub_last, ub_first))
+    left = [
+        twice(last_line, to_line(g_next[-1][:, LANES - 1 :]) + g[rows - 1 : rows]),
+        twice(first_line, g[0:1]),
+        corners[0],
+    ]
+    right = [corners[1], corners[2], twice(to_line(ub_last[0][:, 0:1]), to_line(g_next[0][:, 0:1]))]
+
     layer = lax.axis_index("layer")
     out[...] = jnp.zeros_like(out)
+    for i, line in enumerate(left + right):
+        out[8 + i : 9 + i, :] = line
     for i, values in enumerate((sum_zz[...], zb, bb, bbb)):
         out[pl.ds(2 * i + layer, 1), :] = jnp.sum(values, axis=0, keepdims=True)
+
+
+def corner_kernel(others, mine, theirs, out):
+    place, count, layer = lax.axis_index("col"), lax.axis_size("col"), lax.axis_index("layer")
+    is_left = place % 2 == (1 if others else 0)
+    here, there = mine[...], theirs[...]
+    left, right = jnp.where(is_left, here, there), jnp.where(is_left, there, here)
+    line = 2.0 * (left[8:9] * right[11:12] + left[9:10] * right[12:13] + left[10:11] * right[13:14])
+    added = jnp.where(iota((8, LANES), 0) == 6 + layer, line, 0.0)
+    if others:
+        out[...] = here
+        out[0:8] = here[0:8] + jnp.where(is_left & (place < count - 1), added, 0.0)
+    else:
+        out[...] = here[0:8] + there[0:8] + added
 
 
 def ready_kernel(source, prof, factors, image, add_low, add_high, _, base, kept, sent):
@@ -520,7 +530,7 @@
     profile_other = lax.ppermute(profile, "layer", swap)
     nr = tiles * count
     block, row, pack = (count, rows, width), (nr, LANES), (rows, LANES)
-    strip = (-(-(2 * nr + 2 + tiles) // 8) * 8, LANES)
+    strip = (-(-(2 * nr + tiles) // 8) * 8, LANES)
     shapes = [block, block, strip, strip, pack, pack, (count, LANES), (8, LANES)]
     lines = (-(-half // 8) * 8, LANES)
     factors = column * (1.0 + 0.002 * terrain_height_error.astype(jnp.float32))
@@ -550,10 +560,10 @@
         jnp.where(even, cols_high, cols_low), jnp.where(even, cols_low, cols_high), "col"
     )
     image, g_low, g_high = call(image_kernel, [block, row, row], (weighted, gain))
-    for_pairs, for_others = call(
-        functools.partial(join_kernel, nr), [strip, strip], (strip_low, strip_high, pair_cols, other_cols)
-    )
-    pair_strip, other_strip = exchanged(for_pairs, for_others, "tile")
+    even = lax.axis_index("tile") % 2 == 0
+    pair_strip, other_strip = exchanged(
+        jnp.where(even, strip_high, strip_low), jnp.where(even, strip_low, strip_high), "tile"
+    )
     image, q_low, q_high, k_low, k_high, packed, sum_rest = call(
         inner_kernel,
         [block, row, row, row, row, pack, (3, 8, LANES)],
@@ -562,7 +572,7 @@
     )
     sums, add_low, add_high = call(
         finish_kernel,
-        [(8, LANES), row, row],
+        [(16, LANES), row, row],
         (
             pair_strip,
             other_strip,
@@ -584,7 +594,17 @@
         ),
     )
     part = (half, rows, width)
-    sums, later = total(sums)
+    cols = lax.axis_size("col")
+    if cols > 2:
+        _, theirs = exchanged(sums, sums, "col")
+        (sums,) = call(functools.partial(corner_kernel, True), [(16, LANES)], (sums, theirs))
+    if cols > 1:
+        sizes = {"col": cols}
+        theirs = flipped(sums, sizes, ("col",), (1,))
+        (sums,) = call(functools.partial(corner_kernel, False), [(8, LANES)], (sums, theirs))
+    else:
+        sums = sums[0:8]
+    later = total(sums)
     base, kept, sent = call(
         ready_kernel, [source.shape, part, part], (source, prof, factors, image, add_low, add_high, sums)
     )

time: 29.1 us -> 30 us (1.031)
  waiting for transfers between devices: 8.08 us -> 11.4 us
  starting transfers between devices: 13.2 us -> 10.4 us
    ppermute x5, waiting for transfers between devices: 6.34 us -> 9.95 us  [flipped(): return lax.ppermute(values, axes, pairs)]
    ppermute x5, starting transfers between devices: 7.43 us -> 5.21 us  [flipped(): return lax.ppermute(values, axes, pairs)]
    ppermute x3, starting transfers between devices: 5.17 us -> 4.61 us  [exchanged(): received.append(lax.ppermute(values, (axis, 'layer'), pairs))]
  transfers between devices with their start and end apart: 11 -> 11, of which waited for: 6 -> 5; matrix products, arithmetic and copies ran while one was open for 3% -> 3% of each run, Pallas kernels for 14% -> 13%
where the time goes in v7:
time: 30 us; the launch traced here: 29.7 us
  waiting for transfers between devices  11.4 us (38%)
  starting transfers between devices  10.4 us (35%)
  Pallas kernels  6.76 us (23%)
  other arithmetic  0.86 us (3%)
    ppermute x5, waiting for transfers between devices, flipped(): return lax.ppermute(values, axes, pairs)  9.95 us
    ppermute x5, starting transfers between devices, flipped(): return lax.ppermute(values, axes, pairs)  5.21 us
    ppermute x3, starting transfers between devices, exchanged(): received.append(lax.ppermute(values, (axis, 'layer'), pairs))  4.61 us
    pallas_call x6, Pallas kernels, call(): pl.pallas_call(kernel, out_shape=[jax.ShapeDtypeStruct(shape, jnp.float32...  4.08 us
    pallas_call x1, Pallas kernels, solve(): begun = own(source, profile, factors)  1.47 us
    ppermute x3, waiting for transfers between devices, exchanged(): received.append(lax.ppermute(values, (axis, 'layer'), pairs))  1.4 us
    pallas_call x1, Pallas kernels, solve(): pl.pallas_call(final_kernel, out_shape=jax.ShapeDtypeStruct(source.shape,...  1.21 us
    mul x1, other arithmetic, solve(): factors = column * (1.0 + 0.002 * terrain_height_error.astype(jnp.float32))  0.82 us
  transfers between devices with their start and end apart: 11, of which 5 were waited for; matrix products, arithmetic and copies ran while one was open for 3% of the time, Pallas kernels for 13%

profile of v7, /device:TPU:0, one launch (start us, length us, event | category | flops | bytes accessed | tf_op | source)
XLA Modules:
  0.0 29.7 jit_solution(14761456948350342270)
XLA Ops:
  0.0 0.0 copy-start.2
  0.0 0.5 %collective-permute-start = (f32[2,20,24,256]{3,2,1,0:T(8,128)}, f32[2,20,24,256]{3,2,1,0:T(8,128)S(1)}, u32[]{:S(2)}, u32[]{:S(2)}) collective-permute-start(f32[2,20,24,256]{3,2,1,0:T(8,128)} %source.1), channel_id=1, source_target_pairs={{0,1},{1,0},{2,3},{3,2},{4,5},{5,4},{6,7},{7,6},{8,9},{9,8},{10,11... | collective-permute-start | bytes 2949128 | tf_op jit(solution)/shard_map/ppermute | solution.py:529
  0.5 0.1 collective-permute-start.1
  0.6 0.2 copy-done.2
  0.7 0.0 copy-start.1
  0.7 0.8 %add_multiply_fusion.factors = f32[2,24,256]{2,1,0:T(8,128)S(1)} fusion(s32[2,24,256]{2,1,0:T(8,128)} %param.7, f32[24,256]{1,0:T(8,128)S(1)} %copy-done.2), kind=kLoop, calls=%fused_computation | loop fusion | flops 49152 | bytes 122880 | tf_op jit(solution)/shard_map/mul | solution.py:536
  1.6 0.0 copy-done.1
  1.6 1.5 %own.1 = (f32[40,24,256]{2,1,0:T(8,128)S(1)}, f32[40,24,256]{2,1,0:T(8,128)S(1)}, f32[168,128]{1,0:T(8,128)S(1)}, f32[168,128]{1,0:T(8,128)S(1)}, f32[24,128]{1,...) custom-call(f32[2,20,24,256]{3,2,1,0:T(8,128)} %source.1, f32[20]{0:T(128)S(1)} %copy-done.1, ...), custom_call_target="tpu_custom_call" | custom-call | tf_op jit(solution)/shard_map/own/pallas_call | solution.py:550
  3.1 0.0 collective-permute-done.1.profile
  3.1 0.0 collective-permute-done.source
  3.1 0.6 %shard_map.46 = (f32[40,24,256]{2,1,0:T(8,128)S(1)}, f32[40,24,256]{2,1,0:T(8,128)S(1)}, f32[168,128]{1,0:T(8,128)S(1)}, f32[168,128]{1,0:T(8,128)S(1)}, f32[24,...) custom-call(f32[2,20,24,256]{3,2,1,0:T(8,128)S(1)} %collective-permu, ...), custom_call_target="tpu_custom_call", output_to_operand_aliasing={{0}: (3, {}), {1}: (4, {}), {2}: (5, {}), {3}: (6, {}), {4}... | custom-call | tf_op jit(solution)/shard_map/pallas_call | solution.py:511
  3.7 3.1 %collective-permute-start.3 = (f32[168,128]{1,0:T(8,128)S(1)}, f32[168,128]{1,0:T(8,128)S(1)}, u32[]{:S(2)}, u32[]{:S(2)}) collective-permute-start(f32[168,128]{1,0:T(8,128)S(1)} %get-tuple-element.70), channel_id=1, source_target_pairs={{0,4},{1,5},{4,0},{5,1},{8,12},{9,13},{12,8},{13,9},{2,6},{3,7},{6... | collective-permute-start | bytes 258056 | tf_op jit(solution)/shard_map/ppermute | solution.py:45
  6.9 0.0 collective-permute-start.4
  6.9 1.5 %collective-permute-start.2 = (f32[24,128]{1,0:T(8,128)S(1)}, f32[24,128]{1,0:T(8,128)S(1)}, u32[]{:S(2)}, u32[]{:S(2)}) collective-permute-start(f32[24,128]{1,0:T(8,128)S(1)} %broadcast_select_fusion.2), channel_id=1, source_target_pairs={{0,2},{1,3},{2,0},{3,1},{4,6},{5,7},{6,4},{7,5},{8,10},{9,11},{10,... | collective-permute-start | bytes 36872 | tf_op jit(solution)/shard_map/ppermute | solution.py:45
  8.4 0.8 %shard_map.47 = (f32[40,24,256]{2,1,0:T(8,128)S(1)}, f32[80,128]{1,0:T(8,128)S(1)}, f32[80,128]{1,0:T(8,128)S(1)}) custom-call(f32[40,24,256]{2,1,0:T(8,128)S(1)} %get-tuple-element.46.weighted, f32[40,24,256]{2,1,0:T(8,128)S(1)} %get-tuple-element.47.gain), custom_call_target="tpu_custom_call" | custom-call | tf_op jit(solution)/shard_map/pallas_call | solution.py:511
  9.2 1.4 %collective-permute-done.2.pair_cols = f32[24,128]{1,0:T(8,128)S(1)} collective-permute-done((f32[24,128]{1,0:T(8,128)S(1)}, f32[24,128]{1,0:T(8,128)S(1)}, u32[]{:S(2)}, u32[]{:S(2)}) %collective-permute-start.2) | collective-permute-done | bytes 12320 | tf_op jit(solution)/shard_map/ppermute | solution.py:45
  10.6 0.0 copy-start
  10.6 1.7 %shard_map.48 = (f32[40,24,256]{2,1,0:T(8,128)S(1)}, f32[80,128]{1,0:T(8,128)S(1)}, f32[80,128]{1,0:T(8,128)S(1)}, f32[80,128]{1,0:T(8,128)S(1)}, f32[80,128]{1,...) custom-call(f32[40,24,256]{2,1,0:T(8,128)S(1)} %get-tuple-element.48.begun, ...), custom_call_target="tpu_custom_call" | custom-call | tf_op jit(solution)/shard_map/pallas_call | solution.py:511
  12.3 0.0 collective-permute-done.3.pair_strip
  12.3 0.0 collective-permute-done.4.other_strip
  12.3 0.4 %shard_map.49 = (f32[16,128]{1,0:T(8,128)S(1)}, f32[80,128]{1,0:T(8,128)S(1)}, f32[80,128]{1,0:T(8,128)S(1)}) custom-call(f32[168,128]{1,0:T(8,128)S(1)} %collective-permute-done.3.pair_strip, f32[168,128]{1,0:T(8,128)S(1)} %collective-permute-done.4.other_strip, f32[168,128]{1,0:T(8,128)S(1)} %get-tuple-element.53.strip_low, ...), custom_call_target="tpu_custom_call" | custom-call | tf_op jit(solution)/shard_map/pallas_call | solution.py:511
  12.7 1.6 %collective-permute-start.5 = (f32[16,128]{1,0:T(8,128)S(1)}, f32[16,128]{1,0:T(8,128)S(1)}, u32[]{:S(2)}, u32[]{:S(2)}) collective-permute-start(f32[16,128]{1,0:T(8,128)S(1)} %get-tuple-element.65.mine), channel_id=1, source_target_pairs={{0,2},{2,0},{1,3},{3,1},{4,6},{6,4},{5,7},{7,5},{8,10},{10,8},{9,1... | collective-permute-start | bytes 24584 | tf_op jit(solution)/shard_map/ppermute | solution.py:69
  14.2 2.2 %collective-permute-done.5.theirs = f32[16,128]{1,0:T(8,128)S(1)} collective-permute-done((f32[16,128]{1,0:T(8,128)S(1)}, f32[16,128]{1,0:T(8,128)S(1)}, u32[]{:S(2)}, u32[]{:S(2)}) %collective-permute-start.5) | collective-permute-done | bytes 8224 | tf_op jit(solution)/shard_map/ppermute | solution.py:69
  16.4 0.0 copy-done
  16.4 0.6 %shard_map.51 = (f32[2,20,24,256]{3,2,1,0:T(8,128)S(1)}, f32[20,24,256]{2,1,0:T(8,128)S(1)}, f32[20,24,256]{2,1,0:T(8,128)S(1)}) custom-call(f32[2,20,24,256]{3,2,1,0:T(8,128)S(1)} %copy-done, f32[40,128]{1,0:T(8,128)S(1)} %get-tuple-element.45.prof, f32[2,24,256]{2,1,0:T(8,128)S(1)} %add_multiply_fusion.factors, ...), custom_call_target="tpu_custom_call" | custom-call | tf_op jit(solution)/shard_map/pallas_call | solution.py:511
  17.0 0.1 collective-permute-start.6
  17.1 3.3 %collective-permute-start.9 = (f32[8,128]{1,0:T(8,128)S(1)}, f32[8,128]{1,0:T(8,128)S(1)}, u32[]{:S(2)}, u32[]{:S(2)}) collective-permute-start(f32[8,128]{1,0:T(8,128)S(1)} %shard_map.50._), channel_id=1, source_target_pairs={{0,5},{1,4},{4,1},{5,0},{8,13},{9,12},{12,9},{13,8},{2,7},{3,6},{6... | collective-permute-start | bytes 12296 | tf_op jit(solution)/shard_map/ppermute | solution.py:69
  20.3 0.1 collective-permute-start.7
  20.4 0.3 %collective-permute-start.8 = (f32[8,128]{1,0:T(8,128)S(1)}, f32[8,128]{1,0:T(8,128)S(1)}, u32[]{:S(2)}, u32[]{:S(2)}) collective-permute-start(f32[8,128]{1,0:T(8,128)S(1)} %shard_map.50._), channel_id=1, source_target_pairs={{0,4},{4,0},{8,12},{12,8},{1,5},{5,1},{9,13},{13,9},{2,6},{6,2},{1... | collective-permute-start | bytes 12296 | tf_op jit(solution)/shard_map/ppermute | solution.py:69
  20.7 0.9 %collective-permute-done.9 = f32[8,128]{1,0:T(8,128)S(1)} collective-permute-done((f32[8,128]{1,0:T(8,128)S(1)}, f32[8,128]{1,0:T(8,128)S(1)}, u32[]{:S(2)}, u32[]{:S(2)}) %collective-permute-start.9) | collective-permute-done | bytes 4128 | tf_op jit(solution)/shard_map/ppermute | solution.py:69
  21.7 0.0 collective-permute-done.7
  21.7 2.4 %collective-permute-done.8 = f32[8,128]{1,0:T(8,128)S(1)} collective-permute-done((f32[8,128]{1,0:T(8,128)S(1)}, f32[8,128]{1,0:T(8,128)S(1)}, u32[]{:S(2)}, u32[]{:S(2)}) %collective-permute-start.8) | collective-permute-done | bytes 4128 | tf_op jit(solution)/shard_map/ppermute | solution.py:69
  24.0 0.0 collective-permute-start.10
  24.0 4.5 %collective-permute-done.10 = f32[8,128]{1,0:T(8,128)S(1)} collective-permute-done((f32[8,128]{1,0:T(8,128)S(1)}, f32[8,128]{1,0:T(8,128)S(1)}, u32[]{:S(2)}, u32[]{:S(2)}) %collective-permute-start.10) | collective-permute-done | bytes 4128 | tf_op jit(solution)/shard_map/ppermute | solution.py:69
  28.5 0.0 collective-permute-done.6.received
  28.5 1.2 %final.1 = f32[2,20,24,256]{3,2,1,0:T(8,128)} custom-call(f32[2,20,24,256]{3,2,1,0:T(8,128)S(1)} %get-tuple-element.66.base, f32[20,24,256]{2,1,0:T(8,128)S(1)} %get-tuple-element.67.kept, f32[20,24,256]{2,1,0:T(8,128)S(1)} %collective-permute-done.6.received, f32[8,128]{1,0:T(8,128)S(1)} %add.32.sums), custom_call_target="tpu_custom_call" | custom-call | tf_op jit(solution)/shard_map/final/pallas_call | solution.py:613
  (6 shorter events, 0.1 us)
Async XLA Ops:
  0.0 0.7 %copy-start.2 = (f32[24,256]{1,0:T(8,128)S(1)}, f32[24,256]{1,0:T(8,128)}, u32[]{:S(2)}) copy-start(f32[24,256]{1,0:T(8,128)} %param.6) | copy-start | bytes 73732
  0.0 3.1 %collective-permute-start = (f32[2,20,24,256]{3,2,1,0:T(8,128)}, f32[2,20,24,256]{3,2,1,0:T(8,128)S(1)}, u32[]{:S(2)}, u32[]{:S(2)}) collective-permute-start(f32[2,20,24,256]{3,2,1,0:T(8,128)} %source.1), channel_id=1, source_target_pairs={{0,1},{1,0},{2,3},{3,2},{4,5},{5,4},{6,7},{7,6},{8,9},{9,8},{10,11... | collective-permute-start | bytes 2949128 | tf_op jit(solution)/shard_map/ppermute | solution.py:529
  0.5 2.6 %collective-permute-start.1 = (f32[20]{0:T(128)}, f32[20]{0:T(128)S(1)}, u32[]{:S(2)}, u32[]{:S(2)}) collective-permute-start(f32[20]{0:T(128)} %profile.1), channel_id=1, source_target_pairs={{0,1},{1,0},{2,3},{3,2},{4,5},{5,4},{6,7},{7,6},{8,9},{9,8},{10,11... | collective-permute-start | bytes 248 | tf_op jit(solution)/shard_map/ppermute | solution.py:530
  0.7 0.8 %copy-start.1 = (f32[20]{0:T(128)S(1)}, f32[20]{0:T(128)}, u32[]{:S(2)}) copy-start(f32[20]{0:T(128)} %profile.1) | copy-start | bytes 244
  3.7 8.6 %collective-permute-start.3 = (f32[168,128]{1,0:T(8,128)S(1)}, f32[168,128]{1,0:T(8,128)S(1)}, u32[]{:S(2)}, u32[]{:S(2)}) collective-permute-start(f32[168,128]{1,0:T(8,128)S(1)} %get-tuple-element.70), channel_id=1, source_target_pairs={{0,4},{1,5},{4,0},{5,1},{8,12},{9,13},{12,8},{13,9},{2,6},{3,7},{6... | collective-permute-start | bytes 258056 | tf_op jit(solution)/shard_map/ppermute | solution.py:45
  6.9 5.5 %collective-permute-start.4 = (f32[168,128]{1,0:T(8,128)S(1)}, f32[168,128]{1,0:T(8,128)S(1)}, u32[]{:S(2)}, u32[]{:S(2)}) collective-permute-start(f32[168,128]{1,0:T(8,128)S(1)} %get-tuple-element.69), channel_id=1, source_target_pairs={{0,1},{1,0},{4,8},{5,9},{8,4},{9,5},{12,13},{13,12},{2,3},{3,2},{6... | collective-permute-start | bytes 258056 | tf_op jit(solution)/shard_map/ppermute | solution.py:45
  6.9 3.7 %collective-permute-start.2 = (f32[24,128]{1,0:T(8,128)S(1)}, f32[24,128]{1,0:T(8,128)S(1)}, u32[]{:S(2)}, u32[]{:S(2)}) collective-permute-start(f32[24,128]{1,0:T(8,128)S(1)} %broadcast_select_fusion.2), channel_id=1, source_target_pairs={{0,2},{1,3},{2,0},{3,1},{4,6},{5,7},{6,4},{7,5},{8,10},{9,11},{10,... | collective-permute-start | bytes 36872 | tf_op jit(solution)/shard_map/ppermute | solution.py:45
  10.6 5.9 %copy-start = (f32[2,20,24,256]{3,2,1,0:T(8,128)S(1)}, f32[2,20,24,256]{3,2,1,0:T(8,128)}, u32[]{:S(2)}) copy-start(f32[2,20,24,256]{3,2,1,0:T(8,128)} %source.1) | copy-start | bytes 2949124
  12.7 3.7 %collective-permute-start.5 = (f32[16,128]{1,0:T(8,128)S(1)}, f32[16,128]{1,0:T(8,128)S(1)}, u32[]{:S(2)}, u32[]{:S(2)}) collective-permute-start(f32[16,128]{1,0:T(8,128)S(1)} %get-tuple-element.65.mine), channel_id=1, source_target_pairs={{0,2},{2,0},{1,3},{3,1},{4,6},{6,4},{5,7},{7,5},{8,10},{10,8},{9,1... | collective-permute-start | bytes 24584 | tf_op jit(solution)/shard_map/ppermute | solution.py:69
  17.0 11.5 %collective-permute-start.6 = (f32[20,24,256]{2,1,0:T(8,128)S(1)}, f32[20,24,256]{2,1,0:T(8,128)S(1)}, u32[]{:S(2)}, u32[]{:S(2)}) collective-permute-start(f32[20,24,256]{2,1,0:T(8,128)S(1)} %get-tuple-element.68), channel_id=1, source_target_pairs={{0,1},{1,0},{2,3},{3,2},{4,5},{5,4},{6,7},{7,6},{8,9},{9,8},{10,11... | collective-permute-start | bytes 1474568 | tf_op jit(solution)/shard_map/ppermute | solution.py:611
  17.1 4.6 %collective-permute-start.9 = (f32[8,128]{1,0:T(8,128)S(1)}, f32[8,128]{1,0:T(8,128)S(1)}, u32[]{:S(2)}, u32[]{:S(2)}) collective-permute-start(f32[8,128]{1,0:T(8,128)S(1)} %shard_map.50._), channel_id=1, source_target_pairs={{0,5},{1,4},{4,1},{5,0},{8,13},{9,12},{12,9},{13,8},{2,7},{3,6},{6... | collective-permute-start | bytes 12296 | tf_op jit(solution)/shard_map/ppermute | solution.py:69
  20.3 1.3 %collective-permute-start.7 = (f32[8,128]{1,0:T(8,128)S(1)}, f32[8,128]{1,0:T(8,128)S(1)}, u32[]{:S(2)}, u32[]{:S(2)}) collective-permute-start(f32[8,128]{1,0:T(8,128)S(1)} %shard_map.50._), channel_id=1, source_target_pairs={{0,1},{1,0},{2,3},{3,2},{4,5},{5,4},{6,7},{7,6},{8,9},{9,8},{10,11... | collective-permute-start | bytes 12296 | tf_op jit(solution)/shard_map/ppermute | solution.py:69
  20.4 3.6 %collective-permute-start.8 = (f32[8,128]{1,0:T(8,128)S(1)}, f32[8,128]{1,0:T(8,128)S(1)}, u32[]{:S(2)}, u32[]{:S(2)}) collective-permute-start(f32[8,128]{1,0:T(8,128)S(1)} %shard_map.50._), channel_id=1, source_target_pairs={{0,4},{4,0},{8,12},{12,8},{1,5},{5,1},{9,13},{13,9},{2,6},{6,2},{1... | collective-permute-start | bytes 12296 | tf_op jit(solution)/shard_map/ppermute | solution.py:69
  24.0 4.5 %collective-permute-start.10 = (f32[8,128]{1,0:T(8,128)S(1)}, f32[8,128]{1,0:T(8,128)S(1)}, u32[]{:S(2)}, u32[]{:S(2)}) collective-permute-start(f32[8,128]{1,0:T(8,128)S(1)} %add_add_fusion), channel_id=1, source_target_pairs={{0,8},{4,12},{8,0},{12,4},{1,9},{5,13},{9,1},{13,5},{2,10},{6,14},... | collective-permute-start | bytes 12296 | tf_op jit(solution)/shard_map/ppermute | solution.py:69

commit v8 on v7

--- a/solution.py
+++ b/solution.py
@@ -18,7 +18,7 @@
 LANES = 128
 GRANT = 8 << 20
 OWN_GRANT = 53_750_000
-CHUNKS = 4
+CHUNKS = 2
 PIECES = 4
 
 
@@ -222,7 +222,7 @@
     first, second, cols_high[...], sums[...] = weigh_planes(
         0,
         half,
-        5,
+        20,
         (1 - layer) * half,
         lambda at: source[layer, at],
         levels_at,
@@ -476,14 +476,14 @@
     half = base.shape[1]
     size = half // PIECES
     values = jnp.sum(sums[...], axis=1, keepdims=True)
-    zz, zb, bb, bbb = (values[2 * i : 2 * i + 2] for i in range(4))
-    delta = zz - zb
-    alpha = zz / delta
-    rest = -zb / delta
-    beta = (zz * bb - zb * zb) / (delta * delta)
-    gamma = zz * beta
-    delta_next = gamma - (rest * rest * zb + 2.0 * alpha * rest * bb + alpha * alpha * bbb)
-    alpha_next = gamma / (delta_next - beta * gamma / alpha)
+    zz = values[0:2]
+    zb, bb, bbb = (values[2 * i : 2 * i + 2] / zz for i in range(1, 4))
+    delta = 1.0 - zb
+    alpha = 1.0 / delta
+    rest = -zb * alpha
+    beta = (bb - zb * zb) * (alpha * alpha)
+    delta_next = beta - (rest * rest * zb + 2.0 * alpha * rest * bb + alpha * alpha * bbb)
+    alpha_next = beta / (delta_next - beta * beta * delta)
     first, second = alpha + alpha_next * (rest + beta), alpha_next * alpha
     mine = iota((2, 1), 0) == layer
     copies = []

time: 30 us -> 29.6 us (0.987)
  Pallas kernels: 6.76 us -> 6.39 us
where the time goes in v8:
time: 29.6 us; the launch traced here: 29.4 us
  waiting for transfers between devices  11.4 us (39%)
  starting transfers between devices  10.4 us (35%)
  Pallas kernels  6.39 us (22%)
  other arithmetic  0.86 us (3%)
    ppermute x5, waiting for transfers between devices, flipped(): return lax.ppermute(values, axes, pairs)  9.95 us
    ppermute x5, starting transfers between devices, flipped(): return lax.ppermute(values, axes, pairs)  5.21 us
    ppermute x3, starting transfers between devices, exchanged(): received.append(lax.ppermute(values, (axis, 'layer'), pairs))  4.61 us
    pallas_call x6, Pallas kernels, call(): pl.pallas_call(kernel, out_shape=[jax.ShapeDtypeStruct(shape, jnp.float32...  3.85 us
    ppermute x3, waiting for transfers between devices, exchanged(): received.append(lax.ppermute(values, (axis, 'layer'), pairs))  1.4 us
    pallas_call x1, Pallas kernels, solve(): begun = own(source, profile, factors)  1.33 us
    pallas_call x1, Pallas kernels, solve(): pl.pallas_call(final_kernel, out_shape=jax.ShapeDtypeStruct(source.shape,...  1.22 us
    mul x1, other arithmetic, solve(): factors = column * (1.0 + 0.002 * terrain_height_error.astype(jnp.float32))  0.82 us
  transfers between devices with their start and end apart: 11, of which 5 were waited for; matrix products, arithmetic and copies ran while one was open for 3% of the time, Pallas kernels for 13%

profile of v8, /device:TPU:0, one launch (start us, length us, event | category | flops | bytes accessed | tf_op | source)
XLA Modules:
  0.0 29.4 jit_solution(7489451148925166469)
XLA Ops:
  0.0 0.0 copy-start.2
  0.0 0.5 %collective-permute-start = (f32[2,20,24,256]{3,2,1,0:T(8,128)}, f32[2,20,24,256]{3,2,1,0:T(8,128)S(1)}, u32[]{:S(2)}, u32[]{:S(2)}) collective-permute-start(f32[2,20,24,256]{3,2,1,0:T(8,128)} %source.1), channel_id=1, source_target_pairs={{0,1},{1,0},{2,3},{3,2},{4,5},{5,4},{6,7},{7,6},{8,9},{9,8},{10,11... | collective-permute-start | bytes 2949128 | tf_op jit(solution)/shard_map/ppermute | solution.py:529
  0.5 0.1 collective-permute-start.1
  0.6 0.2 copy-done.2
  0.7 0.0 copy-start.1
  0.7 0.8 %add_multiply_fusion.factors = f32[2,24,256]{2,1,0:T(8,128)S(1)} fusion(s32[2,24,256]{2,1,0:T(8,128)} %param.7, f32[24,256]{1,0:T(8,128)S(1)} %copy-done.2), kind=kLoop, calls=%fused_computation | loop fusion | flops 49152 | bytes 122880 | tf_op jit(solution)/shard_map/mul | solution.py:536
  1.6 0.0 copy-done.1
  1.6 1.3 %own.1 = (f32[40,24,256]{2,1,0:T(8,128)S(1)}, f32[40,24,256]{2,1,0:T(8,128)S(1)}, f32[168,128]{1,0:T(8,128)S(1)}, f32[168,128]{1,0:T(8,128)S(1)}, f32[24,128]{1,...) custom-call(f32[2,20,24,256]{3,2,1,0:T(8,128)} %source.1, f32[20]{0:T(128)S(1)} %copy-done.1, ...), custom_call_target="tpu_custom_call" | custom-call | tf_op jit(solution)/shard_map/own/pallas_call | solution.py:550
  2.9 0.0 collective-permute-done.1.profile
  2.9 0.0 collective-permute-done.source
  2.9 0.4 %shard_map.46 = (f32[40,24,256]{2,1,0:T(8,128)S(1)}, f32[40,24,256]{2,1,0:T(8,128)S(1)}, f32[168,128]{1,0:T(8,128)S(1)}, f32[168,128]{1,0:T(8,128)S(1)}, f32[24,...) custom-call(f32[2,20,24,256]{3,2,1,0:T(8,128)S(1)} %collective-permu, ...), custom_call_target="tpu_custom_call", output_to_operand_aliasing={{0}: (3, {}), {1}: (4, {}), {2}: (5, {}), {3}: (6, {}), {4}... | custom-call | tf_op jit(solution)/shard_map/pallas_call | solution.py:511
  3.4 3.1 %collective-permute-start.3 = (f32[168,128]{1,0:T(8,128)S(1)}, f32[168,128]{1,0:T(8,128)S(1)}, u32[]{:S(2)}, u32[]{:S(2)}) collective-permute-start(f32[168,128]{1,0:T(8,128)S(1)} %get-tuple-element.70), channel_id=1, source_target_pairs={{0,4},{1,5},{4,0},{5,1},{8,12},{9,13},{12,8},{13,9},{2,6},{3,7},{6... | collective-permute-start | bytes 258056 | tf_op jit(solution)/shard_map/ppermute | solution.py:45
  6.5 0.0 collective-permute-start.4
  6.5 1.5 %collective-permute-start.2 = (f32[24,128]{1,0:T(8,128)S(1)}, f32[24,128]{1,0:T(8,128)S(1)}, u32[]{:S(2)}, u32[]{:S(2)}) collective-permute-start(f32[24,128]{1,0:T(8,128)S(1)} %broadcast_select_fusion.2), channel_id=1, source_target_pairs={{0,2},{1,3},{2,0},{3,1},{4,6},{5,7},{6,4},{7,5},{8,10},{9,11},{10,... | collective-permute-start | bytes 36872 | tf_op jit(solution)/shard_map/ppermute | solution.py:45
  8.0 0.8 %shard_map.47 = (f32[40,24,256]{2,1,0:T(8,128)S(1)}, f32[80,128]{1,0:T(8,128)S(1)}, f32[80,128]{1,0:T(8,128)S(1)}) custom-call(f32[40,24,256]{2,1,0:T(8,128)S(1)} %get-tuple-element.46.weighted, f32[40,24,256]{2,1,0:T(8,128)S(1)} %get-tuple-element.47.gain), custom_call_target="tpu_custom_call" | custom-call | tf_op jit(solution)/shard_map/pallas_call | solution.py:511
  8.8 1.4 %collective-permute-done.2.pair_cols = f32[24,128]{1,0:T(8,128)S(1)} collective-permute-done((f32[24,128]{1,0:T(8,128)S(1)}, f32[24,128]{1,0:T(8,128)S(1)}, u32[]{:S(2)}, u32[]{:S(2)}) %collective-permute-start.2) | collective-permute-done | bytes 12320 | tf_op jit(solution)/shard_map/ppermute | solution.py:45
  10.2 0.0 copy-start
  10.2 1.7 %shard_map.48 = (f32[40,24,256]{2,1,0:T(8,128)S(1)}, f32[80,128]{1,0:T(8,128)S(1)}, f32[80,128]{1,0:T(8,128)S(1)}, f32[80,128]{1,0:T(8,128)S(1)}, f32[80,128]{1,...) custom-call(f32[40,24,256]{2,1,0:T(8,128)S(1)} %get-tuple-element.48.begun, ...), custom_call_target="tpu_custom_call" | custom-call | tf_op jit(solution)/shard_map/pallas_call | solution.py:511
  11.9 0.0 collective-permute-done.3.pair_strip
  11.9 0.0 collective-permute-done.4.other_strip
  11.9 0.4 %shard_map.49 = (f32[16,128]{1,0:T(8,128)S(1)}, f32[80,128]{1,0:T(8,128)S(1)}, f32[80,128]{1,0:T(8,128)S(1)}) custom-call(f32[168,128]{1,0:T(8,128)S(1)} %collective-permute-done.3.pair_strip, f32[168,128]{1,0:T(8,128)S(1)} %collective-permute-done.4.other_strip, f32[168,128]{1,0:T(8,128)S(1)} %get-tuple-element.53.strip_low, ...), custom_call_target="tpu_custom_call" | custom-call | tf_op jit(solution)/shard_map/pallas_call | solution.py:511
  12.3 1.6 %collective-permute-start.5 = (f32[16,128]{1,0:T(8,128)S(1)}, f32[16,128]{1,0:T(8,128)S(1)}, u32[]{:S(2)}, u32[]{:S(2)}) collective-permute-start(f32[16,128]{1,0:T(8,128)S(1)} %get-tuple-element.65.mine), channel_id=1, source_target_pairs={{0,2},{2,0},{1,3},{3,1},{4,6},{6,4},{5,7},{7,5},{8,10},{10,8},{9,1... | collective-permute-start | bytes 24584 | tf_op jit(solution)/shard_map/ppermute | solution.py:69
  13.9 2.2 %collective-permute-done.5.theirs = f32[16,128]{1,0:T(8,128)S(1)} collective-permute-done((f32[16,128]{1,0:T(8,128)S(1)}, f32[16,128]{1,0:T(8,128)S(1)}, u32[]{:S(2)}, u32[]{:S(2)}) %collective-permute-start.5) | collective-permute-done | bytes 8224 | tf_op jit(solution)/shard_map/ppermute | solution.py:69
  16.0 0.0 copy-done
  16.0 0.6 %shard_map.51 = (f32[2,20,24,256]{3,2,1,0:T(8,128)S(1)}, f32[20,24,256]{2,1,0:T(8,128)S(1)}, f32[20,24,256]{2,1,0:T(8,128)S(1)}) custom-call(f32[2,20,24,256]{3,2,1,0:T(8,128)S(1)} %copy-done, f32[40,128]{1,0:T(8,128)S(1)} %get-tuple-element.45.prof, f32[2,24,256]{2,1,0:T(8,128)S(1)} %add_multiply_fusion.factors, ...), custom_call_target="tpu_custom_call" | custom-call | tf_op jit(solution)/shard_map/pallas_call | solution.py:511
  16.6 0.1 collective-permute-start.6
  16.7 3.3 %collective-permute-start.9 = (f32[8,128]{1,0:T(8,128)S(1)}, f32[8,128]{1,0:T(8,128)S(1)}, u32[]{:S(2)}, u32[]{:S(2)}) collective-permute-start(f32[8,128]{1,0:T(8,128)S(1)} %shard_map.50._), channel_id=1, source_target_pairs={{0,5},{1,4},{4,1},{5,0},{8,13},{9,12},{12,9},{13,8},{2,7},{3,6},{6... | collective-permute-start | bytes 12296 | tf_op jit(solution)/shard_map/ppermute | solution.py:69
  19.9 0.1 collective-permute-start.7
  20.0 0.3 %collective-permute-start.8 = (f32[8,128]{1,0:T(8,128)S(1)}, f32[8,128]{1,0:T(8,128)S(1)}, u32[]{:S(2)}, u32[]{:S(2)}) collective-permute-start(f32[8,128]{1,0:T(8,128)S(1)} %shard_map.50._), channel_id=1, source_target_pairs={{0,4},{4,0},{8,12},{12,8},{1,5},{5,1},{9,13},{13,9},{2,6},{6,2},{1... | collective-permute-start | bytes 12296 | tf_op jit(solution)/shard_map/ppermute | solution.py:69
  20.3 0.9 %collective-permute-done.9 = f32[8,128]{1,0:T(8,128)S(1)} collective-permute-done((f32[8,128]{1,0:T(8,128)S(1)}, f32[8,128]{1,0:T(8,128)S(1)}, u32[]{:S(2)}, u32[]{:S(2)}) %collective-permute-start.9) | collective-permute-done | bytes 4128 | tf_op jit(solution)/shard_map/ppermute | solution.py:69
  21.3 0.0 collective-permute-done.7
  21.3 2.4 %collective-permute-done.8 = f32[8,128]{1,0:T(8,128)S(1)} collective-permute-done((f32[8,128]{1,0:T(8,128)S(1)}, f32[8,128]{1,0:T(8,128)S(1)}, u32[]{:S(2)}, u32[]{:S(2)}) %collective-permute-start.8) | collective-permute-done | bytes 4128 | tf_op jit(solution)/shard_map/ppermute | solution.py:69
  23.6 0.0 collective-permute-start.10
  23.6 4.5 %collective-permute-done.10 = f32[8,128]{1,0:T(8,128)S(1)} collective-permute-done((f32[8,128]{1,0:T(8,128)S(1)}, f32[8,128]{1,0:T(8,128)S(1)}, u32[]{:S(2)}, u32[]{:S(2)}) %collective-permute-start.10) | collective-permute-done | bytes 4128 | tf_op jit(solution)/shard_map/ppermute | solution.py:69
  28.2 0.0 collective-permute-done.6.received
  28.2 1.2 %final.1 = f32[2,20,24,256]{3,2,1,0:T(8,128)} custom-call(f32[2,20,24,256]{3,2,1,0:T(8,128)S(1)} %get-tuple-element.66.base, f32[20,24,256]{2,1,0:T(8,128)S(1)} %get-tuple-element.67.kept, f32[20,24,256]{2,1,0:T(8,128)S(1)} %collective-permute-done.6.received, f32[8,128]{1,0:T(8,128)S(1)} %add.32.sums), custom_call_target="tpu_custom_call" | custom-call | tf_op jit(solution)/shard_map/final/pallas_call | solution.py:613
  (6 shorter events, 0.1 us)
Async XLA Ops:
  0.0 0.7 %copy-start.2 = (f32[24,256]{1,0:T(8,128)S(1)}, f32[24,256]{1,0:T(8,128)}, u32[]{:S(2)}) copy-start(f32[24,256]{1,0:T(8,128)} %param.6) | copy-start | bytes 73732
  0.0 2.9 %collective-permute-start = (f32[2,20,24,256]{3,2,1,0:T(8,128)}, f32[2,20,24,256]{3,2,1,0:T(8,128)S(1)}, u32[]{:S(2)}, u32[]{:S(2)}) collective-permute-start(f32[2,20,24,256]{3,2,1,0:T(8,128)} %source.1), channel_id=1, source_target_pairs={{0,1},{1,0},{2,3},{3,2},{4,5},{5,4},{6,7},{7,6},{8,9},{9,8},{10,11... | collective-permute-start | bytes 2949128 | tf_op jit(solution)/shard_map/ppermute | solution.py:529
  0.5 2.4 %collective-permute-start.1 = (f32[20]{0:T(128)}, f32[20]{0:T(128)S(1)}, u32[]{:S(2)}, u32[]{:S(2)}) collective-permute-start(f32[20]{0:T(128)} %profile.1), channel_id=1, source_target_pairs={{0,1},{1,0},{2,3},{3,2},{4,5},{5,4},{6,7},{7,6},{8,9},{9,8},{10,11... | collective-permute-start | bytes 248 | tf_op jit(solution)/shard_map/ppermute | solution.py:530
  0.7 0.8 %copy-start.1 = (f32[20]{0:T(128)S(1)}, f32[20]{0:T(128)}, u32[]{:S(2)}) copy-start(f32[20]{0:T(128)} %profile.1) | copy-start | bytes 244
  3.4 8.6 %collective-permute-start.3 = (f32[168,128]{1,0:T(8,128)S(1)}, f32[168,128]{1,0:T(8,128)S(1)}, u32[]{:S(2)}, u32[]{:S(2)}) collective-permute-start(f32[168,128]{1,0:T(8,128)S(1)} %get-tuple-element.70), channel_id=1, source_target_pairs={{0,4},{1,5},{4,0},{5,1},{8,12},{9,13},{12,8},{13,9},{2,6},{3,7},{6... | collective-permute-start | bytes 258056 | tf_op jit(solution)/shard_map/ppermute | solution.py:45
  6.5 5.5 %collective-permute-start.4 = (f32[168,128]{1,0:T(8,128)S(1)}, f32[168,128]{1,0:T(8,128)S(1)}, u32[]{:S(2)}, u32[]{:S(2)}) collective-permute-start(f32[168,128]{1,0:T(8,128)S(1)} %get-tuple-element.69), channel_id=1, source_target_pairs={{0,1},{1,0},{4,8},{5,9},{8,4},{9,5},{12,13},{13,12},{2,3},{3,2},{6... | collective-permute-start | bytes 258056 | tf_op jit(solution)/shard_map/ppermute | solution.py:45
  6.5 3.7 %collective-permute-start.2 = (f32[24,128]{1,0:T(8,128)S(1)}, f32[24,128]{1,0:T(8,128)S(1)}, u32[]{:S(2)}, u32[]{:S(2)}) collective-permute-start(f32[24,128]{1,0:T(8,128)S(1)} %broadcast_select_fusion.2), channel_id=1, source_target_pairs={{0,2},{1,3},{2,0},{3,1},{4,6},{5,7},{6,4},{7,5},{8,10},{9,11},{10,... | collective-permute-start | bytes 36872 | tf_op jit(solution)/shard_map/ppermute | solution.py:45
  10.2 5.9 %copy-start = (f32[2,20,24,256]{3,2,1,0:T(8,128)S(1)}, f32[2,20,24,256]{3,2,1,0:T(8,128)}, u32[]{:S(2)}) copy-start(f32[2,20,24,256]{3,2,1,0:T(8,128)} %source.1) | copy-start | bytes 2949124
  12.3 3.7 %collective-permute-start.5 = (f32[16,128]{1,0:T(8,128)S(1)}, f32[16,128]{1,0:T(8,128)S(1)}, u32[]{:S(2)}, u32[]{:S(2)}) collective-permute-start(f32[16,128]{1,0:T(8,128)S(1)} %get-tuple-element.65.mine), channel_id=1, source_target_pairs={{0,2},{2,0},{1,3},{3,1},{4,6},{6,4},{5,7},{7,5},{8,10},{10,8},{9,1... | collective-permute-start | bytes 24584 | tf_op jit(solution)/shard_map/ppermute | solution.py:69
  16.6 11.5 %collective-permute-start.6 = (f32[20,24,256]{2,1,0:T(8,128)S(1)}, f32[20,24,256]{2,1,0:T(8,128)S(1)}, u32[]{:S(2)}, u32[]{:S(2)}) collective-permute-start(f32[20,24,256]{2,1,0:T(8,128)S(1)} %get-tuple-element.68), channel_id=1, source_target_pairs={{0,1},{1,0},{2,3},{3,2},{4,5},{5,4},{6,7},{7,6},{8,9},{9,8},{10,11... | collective-permute-start | bytes 1474568 | tf_op jit(solution)/shard_map/ppermute | solution.py:611
  16.7 4.6 %collective-permute-start.9 = (f32[8,128]{1,0:T(8,128)S(1)}, f32[8,128]{1,0:T(8,128)S(1)}, u32[]{:S(2)}, u32[]{:S(2)}) collective-permute-start(f32[8,128]{1,0:T(8,128)S(1)} %shard_map.50._), channel_id=1, source_target_pairs={{0,5},{1,4},{4,1},{5,0},{8,13},{9,12},{12,9},{13,8},{2,7},{3,6},{6... | collective-permute-start | bytes 12296 | tf_op jit(solution)/shard_map/ppermute | solution.py:69
  19.9 1.3 %collective-permute-start.7 = (f32[8,128]{1,0:T(8,128)S(1)}, f32[8,128]{1,0:T(8,128)S(1)}, u32[]{:S(2)}, u32[]{:S(2)}) collective-permute-start(f32[8,128]{1,0:T(8,128)S(1)} %shard_map.50._), channel_id=1, source_target_pairs={{0,1},{1,0},{2,3},{3,2},{4,5},{5,4},{6,7},{7,6},{8,9},{9,8},{10,11... | collective-permute-start | bytes 12296 | tf_op jit(solution)/shard_map/ppermute | solution.py:69
  20.0 3.6 %collective-permute-start.8 = (f32[8,128]{1,0:T(8,128)S(1)}, f32[8,128]{1,0:T(8,128)S(1)}, u32[]{:S(2)}, u32[]{:S(2)}) collective-permute-start(f32[8,128]{1,0:T(8,128)S(1)} %shard_map.50._), channel_id=1, source_target_pairs={{0,4},{4,0},{8,12},{12,8},{1,5},{5,1},{9,13},{13,9},{2,6},{6,2},{1... | collective-permute-start | bytes 12296 | tf_op jit(solution)/shard_map/ppermute | solution.py:69
  23.6 4.5 %collective-permute-start.10 = (f32[8,128]{1,0:T(8,128)S(1)}, f32[8,128]{1,0:T(8,128)S(1)}, u32[]{:S(2)}, u32[]{:S(2)}) collective-permute-start(f32[8,128]{1,0:T(8,128)S(1)} %add_add_fusion), channel_id=1, source_target_pairs={{0,8},{4,12},{8,0},{12,4},{1,9},{5,13},{9,1},{13,5},{2,10},{6,14},... | collective-permute-start | bytes 12296 | tf_op jit(solution)/shard_map/ppermute | solution.py:69
